TPU v7x, 512 devices: a whole 4x8x8 slice. The times are simulated.
512 devices in a mesh: gx: 8 (over z), gy: 4 (over y_hi), gz: 16 (over y_lo, x, core).
Axes of the slice: x: 4, y: 8 (y_hi: 4, y_lo: 2; y = y_hi * 2 + y_lo), z: 8, core: 2. Of those that a mesh axis runs over, the one named last changes fastest.
Arguments:
- phi_start: float32 [64, 64, 2048], P('gx', 'gy', 'gz'), may hold values from -6 to 6
- section_first: float32 [64, 64, 2048], P('gx', 'gy', 'gz'), may hold values from -6 to 6
- section_middle: float32 [64, 64, 2048], P('gx', 'gy', 'gz'), may hold values from -6 to 6
- section_second: float32 [64, 64, 2048], P('gx', 'gy', 'gz'), may hold values from -6 to 6
- cot_final: float32 [64, 64, 2048], P('gx', 'gy', 'gz'), may hold values from -6 to 6
Outputs:
- cot_start: float32 [64, 64, 2048], P('gx', 'gy', 'gz')
All inputs are finite; a program needn't handle non-finite values.
Results may differ from a plain program's by a relative error of at most 0.0003.
Values sent between devices are 32-bit elements; how exact they have to be, the bound alone decides.
No kernel may reach another device: no remote copies, remote signals or barrier semaphores. Data moves between devices by JAX's collectives and lax.ppermute only.
A program may use at most 64 MiB of HBM per device.

v0:
```python
import jax
import jax.numpy as jnp
from jax import lax
from jax.sharding import PartitionSpec as P

tau_step = 0.3
weno_epsilon = 1e-06
smooth_epsilon = 0.01


def padded(cells, sides, width):
    for axis, dim in sides:
        count = lax.axis_size(axis)
        head = lax.slice_in_dim(cells, 0, width, axis=dim)
        tail = lax.slice_in_dim(cells, cells.shape[dim] - width, cells.shape[dim], axis=dim)
        cells = jnp.concatenate(
            [
                lax.ppermute(tail, axis, [(i, (i + 1) % count) for i in range(count)]),
                cells,
                lax.ppermute(head, axis, [((i + 1) % count, i) for i in range(count)]),
            ],
            axis=dim,
        )
    return cells


def weno_five(value_one, value_two, value_three, value_four, value_five):
    candidate_one = value_one / 3.0 - 7.0 * value_two / 6.0 + 11.0 * value_three / 6.0
    candidate_two = -value_two / 6.0 + 5.0 * value_three / 6.0 + value_four / 3.0
    candidate_three = value_three / 3.0 + 5.0 * value_four / 6.0 - value_five / 6.0
    beta_one = (
        13.0 / 12.0 * (value_one - 2.0 * value_two + value_three) ** 2
        + 0.25 * (value_one - 4.0 * value_two + 3.0 * value_three) ** 2
    )
    beta_two = (
        13.0 / 12.0 * (value_two - 2.0 * value_three + value_four) ** 2
        + 0.25 * (value_two - value_four) ** 2
    )
    beta_three = (
        13.0 / 12.0 * (value_three - 2.0 * value_four + value_five) ** 2
        + 0.25 * (3.0 * value_three - 4.0 * value_four + value_five) ** 2
    )
    weight_one = 0.1 / (weno_epsilon + beta_one) ** 2
    weight_two = 0.6 / (weno_epsilon + beta_two) ** 2
    weight_three = 0.3 / (weno_epsilon + beta_three) ** 2
    weighted = (
        weight_one * candidate_one + weight_two * candidate_two + weight_three * candidate_three
    )
    return weighted / (weight_one + weight_two + weight_three)


def one_sided(grid_field, along_axis):
    full_length = grid_field.shape[along_axis]
    cell_count = full_length - 6
    differences = lax.slice_in_dim(grid_field, 1, full_length, axis=along_axis) - lax.slice_in_dim(
        grid_field, 0, full_length - 1, axis=along_axis
    )
    shifted = [
        lax.slice_in_dim(differences, offset, offset + cell_count, axis=along_axis)
        for offset in range(6)
    ]
    minus_side = weno_five(shifted[0], shifted[1], shifted[2], shifted[3], shifted[4])
    plus_side = weno_five(shifted[5], shifted[4], shifted[3], shifted[2], shifted[1])
    return (minus_side, plus_side)


def smooth_max(first_term, second_term):
    return 0.5 * (
        first_term + second_term + jnp.sqrt((first_term - second_term) ** 2 + smooth_epsilon)
    )


def hamiltonian(padded_field, positive):
    squared_sum = None
    for along_axis in range(3):
        window = [slice(3, -3)] * 3
        window[along_axis] = slice(None)
        minus_side, plus_side = one_sided(padded_field[tuple(window)], along_axis)
        upwind = jnp.where(positive, jax.nn.relu(minus_side), jax.nn.relu(-minus_side))
        downwind = jnp.where(positive, jax.nn.relu(-plus_side), jax.nn.relu(plus_side))
        axis_term = smooth_max(upwind * upwind, downwind * downwind)
        squared_sum = axis_term if squared_sum is None else squared_sum + axis_term
    return jnp.sqrt(squared_sum)


def ghost_pair(gradient, along_axis):
    length_full = gradient.shape[along_axis]
    window_low = [slice(3, -3)] * 3
    window_low[along_axis] = slice(0, 3)
    window_high = [slice(3, -3)] * 3
    window_high[along_axis] = slice(length_full - 3, length_full)
    return jnp.concatenate(
        [gradient[tuple(window_low)], gradient[tuple(window_high)]], axis=along_axis
    )


def add_edges(inner_part, received, along_axis):
    inner_length = inner_part.shape[along_axis]
    from_lower = lax.slice_in_dim(received, 0, 3, axis=along_axis)
    from_upper = lax.slice_in_dim(received, 9, 12, axis=along_axis)
    widths_lower = [(0, 0)] * 3
    widths_lower[along_axis] = (0, inner_length - 3)
    widths_upper = [(0, 0)] * 3
    widths_upper[along_axis] = (inner_length - 3, 0)
    return inner_part + jnp.pad(from_lower, widths_lower) + jnp.pad(from_upper, widths_upper)


def fold_back(gradient):
    inner_part = gradient[3:-3, 3:-3, 3:-3]
    faces_first = padded(ghost_pair(gradient, 0), (("gx", 0),), 3)
    faces_second = padded(ghost_pair(gradient, 1), (("gy", 1),), 3)
    faces_third = padded(ghost_pair(gradient, 2), (("gz", 2),), 3)
    inner_part = add_edges(inner_part, faces_first, 0)
    inner_part = add_edges(inner_part, faces_second, 1)
    return add_edges(inner_part, faces_third, 2)


def section_adjoint(extended, positive_mask, weight):
    values, pullback = jax.vjp(lambda field_in: hamiltonian(field_in, positive_mask), extended)
    (gradient,) = pullback(weight)
    return (fold_back(gradient), values)


def extend_one(grid_field, rim_depth):
    return padded(grid_field, (("gx", 0), ("gy", 1), ("gz", 2)), rim_depth)


def shards(phi_start, section_first, section_middle, section_second, cot_final):
    rim_depth = 3

    def fetch_rim(grid_field):
        return extend_one(grid_field, rim_depth)

    extended_start = fetch_rim(phi_start)
    positive_mask = phi_start > 0
    squared_one = phi_start * phi_start + 1.0
    sign_value = phi_start / jnp.sqrt(squared_one)
    sign_slope = 1.0 / (squared_one * jnp.sqrt(squared_one))

    def section_terms(extended, incoming):
        gradient, values = section_adjoint(
            extended, positive_mask, -tau_step * sign_value * incoming
        )
        return (gradient, -tau_step * sign_slope * (values - 1.0) * incoming)

    half_final = 0.5 * cot_final
    back_second, part_second = section_terms(fetch_rim(section_second), half_final)
    cot_second = half_final + back_second
    back_middle, part_middle = section_terms(fetch_rim(section_middle), cot_second)
    cot_middle = half_final + cot_second + back_middle
    half_middle = 0.5 * cot_middle
    back_first, part_first = section_terms(fetch_rim(section_first), half_middle)
    cot_first = half_middle + back_first
    back_start, part_start = section_terms(extended_start, cot_first)
    return (
        half_middle + cot_first + back_start + part_second + part_middle + part_first + part_start
    )


def solution(mesh):
    return jax.shard_map(
        shards,
        mesh=mesh,
        in_specs=(
            P("gx", "gy", "gz"),
            P("gx", "gy", "gz"),
            P("gx", "gy", "gz"),
            P("gx", "gy", "gz"),
            P("gx", "gy", "gz"),
        ),
        out_specs=P("gx", "gy", "gz"),
        check_vma=False,
    )
```

profile of v0, /device:TPU:7, one launch (start us, length us, event | category | flops | bytes accessed | tf_op | source)
XLA Modules:
  0.0 216.9 jit_solution(11771873498620895198)
XLA Ops:
  0.8 4.1 %collective-permute-start = (f32[3,16,128]{2,1,0:T(8,128)S(1)}, f32[3,16,128]{2,1,0:T(8,128)S(1)}, u32[]{:S(2)}, u32[]{:S(2)}) collective-permute-start(f32[3,16,128]{2,1,0:T(8,128)S(1)} %get-tuple-element.552), channel_id=1, source_target_pairs={{0,64},{64,128},{128,192},{192,256},{256,320},{320,384},{384,448},... | collective-permute-start | bytes 73736 | tf_op jit(solution)/shard_map/ppermute | solution.py:18
  4.9 8.6 %collective-permute-start.1 = (f32[3,16,128]{2,1,0:T(8,128)S(1)}, f32[3,16,128]{2,1,0:T(8,128)S(1)}, u32[]{:S(2)}, u32[]{:S(2)}) collective-permute-start(f32[3,16,128]{2,1,0:T(8,128)S(1)} %get-tuple-element.551), channel_id=1, source_target_pairs={{64,0},{128,64},{192,128},{256,192},{320,256},{384,320},{448,384},... | collective-permute-start | bytes 73736 | tf_op jit(solution)/shard_map/ppermute | solution.py:20
  15.6 4.6 %collective-permute-start.13 = (f32[3,16,128]{2,1,0:T(8,128)S(1)}, f32[3,16,128]{2,1,0:T(8,128)S(1)}, u32[]{:S(2)}, u32[]{:S(2)}) collective-permute-start(f32[3,16,128]{2,1,0:T(8,128)S(1)} %get-tuple-element.547), channel_id=1, source_target_pairs={{64,0},{128,64},{192,128},{256,192},{320,256},{384,320},{448,384},... | collective-permute-start | bytes 73736 | tf_op jit(solution)/shard_map/ppermute | solution.py:20
  22.3 4.6 %collective-permute-start.25 = (f32[3,16,128]{2,1,0:T(8,128)S(1)}, f32[3,16,128]{2,1,0:T(8,128)S(1)}, u32[]{:S(2)}, u32[]{:S(2)}) collective-permute-start(f32[3,16,128]{2,1,0:T(8,128)S(1)} %get-tuple-element.549), channel_id=1, source_target_pairs={{64,0},{128,64},{192,128},{256,192},{320,256},{384,320},{448,384},... | collective-permute-start | bytes 73736 | tf_op jit(solution)/shard_map/ppermute | solution.py:20
  28.9 4.6 %collective-permute-start.37 = (f32[3,16,128]{2,1,0:T(8,128)S(1)}, f32[3,16,128]{2,1,0:T(8,128)S(1)}, u32[]{:S(2)}, u32[]{:S(2)}) collective-permute-start(f32[3,16,128]{2,1,0:T(8,128)S(1)} %get-tuple-element.545), channel_id=1, source_target_pairs={{64,0},{128,64},{192,128},{256,192},{320,256},{384,320},{448,384},... | collective-permute-start | bytes 73736 | tf_op jit(solution)/shard_map/ppermute | solution.py:20
  33.7 4.2 %collective-permute-start.2 = (f32[14,3,128]{2,1,0:T(4,128)S(1)}, f32[14,3,128]{2,1,0:T(4,128)S(1)}, u32[]{:S(2)}, u32[]{:S(2)}) collective-permute-start(f32[14,3,128]{2,1,0:T(4,128)S(1)} %get-tuple-element.535), channel_id=1, source_target_pairs={{0,16},{16,32},{32,48},{48,0},{1,17},{17,33},{33,49},{49,1},{2,18}... | collective-permute-start | bytes 64520 | tf_op jit(solution)/shard_map/ppermute | solution.py:18
  41.6 3.8 %collective-permute-start.14 = (f32[14,3,128]{2,1,0:T(4,128)S(1)}, f32[14,3,128]{2,1,0:T(4,128)S(1)}, u32[]{:S(2)}, u32[]{:S(2)}) collective-permute-start(f32[14,3,128]{2,1,0:T(4,128)S(1)} %get-tuple-element.531), channel_id=1, source_target_pairs={{0,16},{16,32},{32,48},{48,0},{1,17},{17,33},{33,49},{49,1},{2,18}... | collective-permute-start | bytes 64520 | tf_op jit(solution)/shard_map/ppermute | solution.py:18
  56.5 3.8 %collective-permute-start.38 = (f32[14,3,128]{2,1,0:T(4,128)S(1)}, f32[14,3,128]{2,1,0:T(4,128)S(1)}, u32[]{:S(2)}, u32[]{:S(2)}) collective-permute-start(f32[14,3,128]{2,1,0:T(4,128)S(1)} %get-tuple-element.529), channel_id=1, source_target_pairs={{0,16},{16,32},{32,48},{48,0},{1,17},{17,33},{33,49},{49,1},{2,18}... | collective-permute-start | bytes 64520 | tf_op jit(solution)/shard_map/ppermute | solution.py:18
  64.4 7.5 %collective-permute-start.4 = (f32[14,22,3]{2,1,0:T(8,128)S(1)}, f32[14,22,3]{2,1,0:T(8,128)S(1)}, u32[]{:S(2)}, u32[]{:S(2)}) collective-permute-start(f32[14,22,3]{2,1,0:T(8,128)S(1)} %get-tuple-element.523), channel_id=1, source_target_pairs={{0,1},{1,2},{2,3},{3,4},{4,5},{5,6},{6,7},{7,8},{8,9},{9,10},{10,1... | collective-permute-start | bytes 11096 | tf_op jit(solution)/shard_map/ppermute | solution.py:18
  74.0 5.8 %collective-permute-start.16 = (f32[14,22,3]{2,1,0:T(8,128)S(1)}, f32[14,22,3]{2,1,0:T(8,128)S(1)}, u32[]{:S(2)}, u32[]{:S(2)}) collective-permute-start(f32[14,22,3]{2,1,0:T(8,128)S(1)} %get-tuple-element.519), channel_id=1, source_target_pairs={{0,1},{1,2},{2,3},{3,4},{4,5},{5,6},{6,7},{7,8},{8,9},{9,10},{10,1... | collective-permute-start | bytes 11096 | tf_op jit(solution)/shard_map/ppermute | solution.py:18
  81.7 5.8 %collective-permute-start.28 = (f32[14,22,3]{2,1,0:T(8,128)S(1)}, f32[14,22,3]{2,1,0:T(8,128)S(1)}, u32[]{:S(2)}, u32[]{:S(2)}) collective-permute-start(f32[14,22,3]{2,1,0:T(8,128)S(1)} %get-tuple-element.521), channel_id=1, source_target_pairs={{0,1},{1,2},{2,3},{3,4},{4,5},{5,6},{6,7},{7,8},{8,9},{9,10},{10,1... | collective-permute-start | bytes 11096 | tf_op jit(solution)/shard_map/ppermute | solution.py:18
  89.4 5.9 %collective-permute-start.40 = (f32[14,22,3]{2,1,0:T(8,128)S(1)}, f32[14,22,3]{2,1,0:T(8,128)S(1)}, u32[]{:S(2)}, u32[]{:S(2)}) collective-permute-start(f32[14,22,3]{2,1,0:T(8,128)S(1)} %get-tuple-element.517), channel_id=1, source_target_pairs={{0,1},{1,2},{2,3},{3,4},{4,5},{5,6},{6,7},{7,8},{8,9},{9,10},{10,1... | collective-permute-start | bytes 11096 | tf_op jit(solution)/shard_map/ppermute | solution.py:18
  104.7 4.6 %collective-permute-start.7 = (f32[3,16,128]{2,1,0:T(8,128)S(1)}, f32[3,16,128]{2,1,0:T(8,128)S(1)}, u32[]{:S(2)}, u32[]{:S(2)}) collective-permute-start(f32[3,16,128]{2,1,0:T(8,128)S(1)} %get-tuple-element.484), channel_id=1, source_target_pairs={{64,0},{128,64},{192,128},{256,192},{320,256},{384,320},{448,384},... | collective-permute-start | bytes 73736 | tf_op jit(solution)/shard_map/ppermute | solution.py:20
  109.3 6.3 %collective-permute-start.10 = (f32[8,16,3]{2,1,0:T(8,128)S(1)}, f32[8,16,3]{2,1,0:T(8,128)S(1)}, u32[]{:S(2)}, u32[]{:S(2)}) collective-permute-start(f32[8,16,3]{2,1,0:T(8,128)S(1)} %get-tuple-element.487), channel_id=1, source_target_pairs={{0,1},{1,2},{2,3},{3,4},{4,5},{5,6},{6,7},{7,8},{8,9},{9,10},{10,1... | collective-permute-start | bytes 4616 | tf_op jit(solution)/shard_map/ppermute | solution.py:18
  118.9 4.4 %collective-permute-start.9 = (f32[8,3,128]{2,1,0:T(4,128)S(1)}, f32[8,3,128]{2,1,0:T(4,128)S(1)}, u32[]{:S(2)}, u32[]{:S(2)}) collective-permute-start(f32[8,3,128]{2,1,0:T(4,128)S(1)} %get-tuple-element.486), channel_id=1, source_target_pairs={{16,0},{32,16},{48,32},{0,48},{17,1},{33,17},{49,33},{1,49},{18,2}... | collective-permute-start | bytes 36872 | tf_op jit(solution)/shard_map/ppermute | solution.py:20
  125.6 5.4 %collective-permute-done.11 = f32[8,16,3]{2,1,0:T(8,128)S(1)} collective-permute-done((f32[8,16,3]{2,1,0:T(8,128)S(1)}, f32[8,16,3]{2,1,0:T(8,128)S(1)}, u32[]{:S(2)}, u32[]{:S(2)}) %collective-permute-start.11) | collective-permute-done | bytes 1568 | tf_op jit(solution)/shard_map/ppermute | solution.py:20
  139.7 4.6 %collective-permute-start.19 = (f32[3,16,128]{2,1,0:T(8,128)S(1)}, f32[3,16,128]{2,1,0:T(8,128)S(1)}, u32[]{:S(2)}, u32[]{:S(2)}) collective-permute-start(f32[3,16,128]{2,1,0:T(8,128)S(1)} %get-tuple-element.474), channel_id=1, source_target_pairs={{64,0},{128,64},{192,128},{256,192},{320,256},{384,320},{448,384},... | collective-permute-start | bytes 73736 | tf_op jit(solution)/shard_map/ppermute | solution.py:20
  147.5 4.1 %collective-permute-start.21 = (f32[8,3,128]{2,1,0:T(4,128)S(1)}, f32[8,3,128]{2,1,0:T(4,128)S(1)}, u32[]{:S(2)}, u32[]{:S(2)}) collective-permute-start(f32[8,3,128]{2,1,0:T(4,128)S(1)} %get-tuple-element.476), channel_id=1, source_target_pairs={{16,0},{32,16},{48,32},{0,48},{17,1},{33,17},{49,33},{1,49},{18,2}... | collective-permute-start | bytes 36872 | tf_op jit(solution)/shard_map/ppermute | solution.py:20
  155.4 3.9 %collective-permute-done.23 = f32[8,16,3]{2,1,0:T(8,128)S(1)} collective-permute-done((f32[8,16,3]{2,1,0:T(8,128)S(1)}, f32[8,16,3]{2,1,0:T(8,128)S(1)}, u32[]{:S(2)}, u32[]{:S(2)}) %collective-permute-start.23) | collective-permute-done | bytes 1568 | tf_op jit(solution)/shard_map/ppermute | solution.py:20
  168.1 4.6 %collective-permute-start.31 = (f32[3,16,128]{2,1,0:T(8,128)S(1)}, f32[3,16,128]{2,1,0:T(8,128)S(1)}, u32[]{:S(2)}, u32[]{:S(2)}) collective-permute-start(f32[3,16,128]{2,1,0:T(8,128)S(1)} %get-tuple-element.464), channel_id=1, source_target_pairs={{64,0},{128,64},{192,128},{256,192},{320,256},{384,320},{448,384},... | collective-permute-start | bytes 73736 | tf_op jit(solution)/shard_map/ppermute | solution.py:20
  175.9 4.1 %collective-permute-start.33 = (f32[8,3,128]{2,1,0:T(4,128)S(1)}, f32[8,3,128]{2,1,0:T(4,128)S(1)}, u32[]{:S(2)}, u32[]{:S(2)}) collective-permute-start(f32[8,3,128]{2,1,0:T(4,128)S(1)} %get-tuple-element.466), channel_id=1, source_target_pairs={{16,0},{32,16},{48,32},{0,48},{17,1},{33,17},{49,33},{1,49},{18,2}... | collective-permute-start | bytes 36872 | tf_op jit(solution)/shard_map/ppermute | solution.py:20
  196.5 4.6 %collective-permute-start.43 = (f32[3,16,128]{2,1,0:T(8,128)S(1)}, f32[3,16,128]{2,1,0:T(8,128)S(1)}, u32[]{:S(2)}, u32[]{:S(2)}) collective-permute-start(f32[3,16,128]{2,1,0:T(8,128)S(1)} %get-tuple-element.454), channel_id=1, source_target_pairs={{64,0},{128,64},{192,128},{256,192},{320,256},{384,320},{448,384},... | collective-permute-start | bytes 73736 | tf_op jit(solution)/shard_map/ppermute | solution.py:20
  204.3 4.1 %collective-permute-start.45 = (f32[8,3,128]{2,1,0:T(4,128)S(1)}, f32[8,3,128]{2,1,0:T(4,128)S(1)}, u32[]{:S(2)}, u32[]{:S(2)}) collective-permute-start(f32[8,3,128]{2,1,0:T(4,128)S(1)} %get-tuple-element.456), channel_id=1, source_target_pairs={{16,0},{32,16},{48,32},{0,48},{17,1},{33,17},{49,33},{1,49},{18,2}... | collective-permute-start | bytes 36872 | tf_op jit(solution)/shard_map/ppermute | solution.py:20
  212.2 3.9 %collective-permute-done.47 = f32[8,16,3]{2,1,0:T(8,128)S(1)} collective-permute-done((f32[8,16,3]{2,1,0:T(8,128)S(1)}, f32[8,16,3]{2,1,0:T(8,128)S(1)}, u32[]{:S(2)}, u32[]{:S(2)}) %collective-permute-start.47) | collective-permute-done | bytes 1568 | tf_op jit(solution)/shard_map/ppermute | solution.py:20
  (230 shorter events, 97.9 us)
Async XLA Ops:
  0.8 21.5 %collective-permute-start = (f32[3,16,128]{2,1,0:T(8,128)S(1)}, f32[3,16,128]{2,1,0:T(8,128)S(1)}, u32[]{:S(2)}, u32[]{:S(2)}) collective-permute-start(f32[3,16,128]{2,1,0:T(8,128)S(1)} %get-tuple-element.552), channel_id=1, source_target_pairs={{0,64},{64,128},{128,192},{192,256},{256,320},{320,384},{384,448},... | collective-permute-start | bytes 73736 | tf_op jit(solution)/shard_map/ppermute | solution.py:18
  4.9 22.0 %collective-permute-start.1 = (f32[3,16,128]{2,1,0:T(8,128)S(1)}, f32[3,16,128]{2,1,0:T(8,128)S(1)}, u32[]{:S(2)}, u32[]{:S(2)}) collective-permute-start(f32[3,16,128]{2,1,0:T(8,128)S(1)} %get-tuple-element.551), channel_id=1, source_target_pairs={{64,0},{128,64},{192,128},{256,192},{320,256},{384,320},{448,384},... | collective-permute-start | bytes 73736 | tf_op jit(solution)/shard_map/ppermute | solution.py:20
  15.6 17.9 %collective-permute-start.13 = (f32[3,16,128]{2,1,0:T(8,128)S(1)}, f32[3,16,128]{2,1,0:T(8,128)S(1)}, u32[]{:S(2)}, u32[]{:S(2)}) collective-permute-start(f32[3,16,128]{2,1,0:T(8,128)S(1)} %get-tuple-element.547), channel_id=1, source_target_pairs={{64,0},{128,64},{192,128},{256,192},{320,256},{384,320},{448,384},... | collective-permute-start | bytes 73736 | tf_op jit(solution)/shard_map/ppermute | solution.py:20
  33.7 19.1 %collective-permute-start.2 = (f32[14,3,128]{2,1,0:T(4,128)S(1)}, f32[14,3,128]{2,1,0:T(4,128)S(1)}, u32[]{:S(2)}, u32[]{:S(2)}) collective-permute-start(f32[14,3,128]{2,1,0:T(4,128)S(1)} %get-tuple-element.535), channel_id=1, source_target_pairs={{0,16},{16,32},{32,48},{48,0},{1,17},{17,33},{33,49},{49,1},{2,18}... | collective-permute-start | bytes 64520 | tf_op jit(solution)/shard_map/ppermute | solution.py:18
  37.9 18.5 %collective-permute-start.3 = (f32[14,3,128]{2,1,0:T(4,128)S(1)}, f32[14,3,128]{2,1,0:T(4,128)S(1)}, u32[]{:S(2)}, u32[]{:S(2)}) collective-permute-start(f32[14,3,128]{2,1,0:T(4,128)S(1)} %get-tuple-element.536), channel_id=1, source_target_pairs={{16,0},{32,16},{48,32},{0,48},{17,1},{33,17},{49,33},{1,49},{18,2}... | collective-permute-start | bytes 64520 | tf_op jit(solution)/shard_map/ppermute | solution.py:20
  41.6 18.8 %collective-permute-start.14 = (f32[14,3,128]{2,1,0:T(4,128)S(1)}, f32[14,3,128]{2,1,0:T(4,128)S(1)}, u32[]{:S(2)}, u32[]{:S(2)}) collective-permute-start(f32[14,3,128]{2,1,0:T(4,128)S(1)} %get-tuple-element.531), channel_id=1, source_target_pairs={{0,16},{16,32},{32,48},{48,0},{1,17},{17,33},{33,49},{49,1},{2,18}... | collective-permute-start | bytes 64520 | tf_op jit(solution)/shard_map/ppermute | solution.py:18
  45.4 18.7 %collective-permute-start.15 = (f32[14,3,128]{2,1,0:T(4,128)S(1)}, f32[14,3,128]{2,1,0:T(4,128)S(1)}, u32[]{:S(2)}, u32[]{:S(2)}) collective-permute-start(f32[14,3,128]{2,1,0:T(4,128)S(1)} %get-tuple-element.532), channel_id=1, source_target_pairs={{16,0},{32,16},{48,32},{0,48},{17,1},{33,17},{49,33},{1,49},{18,2}... | collective-permute-start | bytes 64520 | tf_op jit(solution)/shard_map/ppermute | solution.py:20
  56.5 17.4 %collective-permute-start.38 = (f32[14,3,128]{2,1,0:T(4,128)S(1)}, f32[14,3,128]{2,1,0:T(4,128)S(1)}, u32[]{:S(2)}, u32[]{:S(2)}) collective-permute-start(f32[14,3,128]{2,1,0:T(4,128)S(1)} %get-tuple-element.529), channel_id=1, source_target_pairs={{0,16},{16,32},{32,48},{48,0},{1,17},{17,33},{33,49},{49,1},{2,18}... | collective-permute-start | bytes 64520 | tf_op jit(solution)/shard_map/ppermute | solution.py:18
  64.4 23.0 %collective-permute-start.4 = (f32[14,22,3]{2,1,0:T(8,128)S(1)}, f32[14,22,3]{2,1,0:T(8,128)S(1)}, u32[]{:S(2)}, u32[]{:S(2)}) collective-permute-start(f32[14,22,3]{2,1,0:T(8,128)S(1)} %get-tuple-element.523), channel_id=1, source_target_pairs={{0,1},{1,2},{2,3},{3,4},{4,5},{5,6},{6,7},{7,8},{8,9},{9,10},{10,1... | collective-permute-start | bytes 11096 | tf_op jit(solution)/shard_map/ppermute | solution.py:18
  71.9 17.5 %collective-permute-start.5 = (f32[14,22,3]{2,1,0:T(8,128)S(1)}, f32[14,22,3]{2,1,0:T(8,128)S(1)}, u32[]{:S(2)}, u32[]{:S(2)}) collective-permute-start(f32[14,22,3]{2,1,0:T(8,128)S(1)} %get-tuple-element.524), channel_id=1, source_target_pairs={{1,0},{2,1},{3,2},{4,3},{5,4},{6,5},{7,6},{8,7},{9,8},{10,9},{11,1... | collective-permute-start | bytes 11096 | tf_op jit(solution)/shard_map/ppermute | solution.py:20
  74.0 26.6 %collective-permute-start.16 = (f32[14,22,3]{2,1,0:T(8,128)S(1)}, f32[14,22,3]{2,1,0:T(8,128)S(1)}, u32[]{:S(2)}, u32[]{:S(2)}) collective-permute-start(f32[14,22,3]{2,1,0:T(8,128)S(1)} %get-tuple-element.519), channel_id=1, source_target_pairs={{0,1},{1,2},{2,3},{3,4},{4,5},{5,6},{6,7},{7,8},{8,9},{9,10},{10,1... | collective-permute-start | bytes 11096 | tf_op jit(solution)/shard_map/ppermute | solution.py:18
  79.8 22.7 %collective-permute-start.17 = (f32[14,22,3]{2,1,0:T(8,128)S(1)}, f32[14,22,3]{2,1,0:T(8,128)S(1)}, u32[]{:S(2)}, u32[]{:S(2)}) collective-permute-start(f32[14,22,3]{2,1,0:T(8,128)S(1)} %get-tuple-element.520), channel_id=1, source_target_pairs={{1,0},{2,1},{3,2},{4,3},{5,4},{6,5},{7,6},{8,7},{9,8},{10,9},{11,1... | collective-permute-start | bytes 11096 | tf_op jit(solution)/shard_map/ppermute | solution.py:20
  81.7 23.0 %collective-permute-start.28 = (f32[14,22,3]{2,1,0:T(8,128)S(1)}, f32[14,22,3]{2,1,0:T(8,128)S(1)}, u32[]{:S(2)}, u32[]{:S(2)}) collective-permute-start(f32[14,22,3]{2,1,0:T(8,128)S(1)} %get-tuple-element.521), channel_id=1, source_target_pairs={{0,1},{1,2},{2,3},{3,4},{4,5},{5,6},{6,7},{7,8},{8,9},{9,10},{10,1... | collective-permute-start | bytes 11096 | tf_op jit(solution)/shard_map/ppermute | solution.py:18
  87.5 21.8 %collective-permute-start.29 = (f32[14,22,3]{2,1,0:T(8,128)S(1)}, f32[14,22,3]{2,1,0:T(8,128)S(1)}, u32[]{:S(2)}, u32[]{:S(2)}) collective-permute-start(f32[14,22,3]{2,1,0:T(8,128)S(1)} %get-tuple-element.522), channel_id=1, source_target_pairs={{1,0},{2,1},{3,2},{4,3},{5,4},{6,5},{7,6},{8,7},{9,8},{10,9},{11,1... | collective-permute-start | bytes 11096 | tf_op jit(solution)/shard_map/ppermute | solution.py:20
  89.4 26.4 %collective-permute-start.40 = (f32[14,22,3]{2,1,0:T(8,128)S(1)}, f32[14,22,3]{2,1,0:T(8,128)S(1)}, u32[]{:S(2)}, u32[]{:S(2)}) collective-permute-start(f32[14,22,3]{2,1,0:T(8,128)S(1)} %get-tuple-element.517), channel_id=1, source_target_pairs={{0,1},{1,2},{2,3},{3,4},{4,5},{5,6},{6,7},{7,8},{8,9},{9,10},{10,1... | collective-permute-start | bytes 11096 | tf_op jit(solution)/shard_map/ppermute | solution.py:18
  100.6 18.3 %collective-permute-start.41 = (f32[14,22,3]{2,1,0:T(8,128)S(1)}, f32[14,22,3]{2,1,0:T(8,128)S(1)}, u32[]{:S(2)}, u32[]{:S(2)}) collective-permute-start(f32[14,22,3]{2,1,0:T(8,128)S(1)} %get-tuple-element.518), channel_id=1, source_target_pairs={{1,0},{2,1},{3,2},{4,3},{5,4},{6,5},{7,6},{8,7},{9,8},{10,9},{11,1... | collective-permute-start | bytes 11096 | tf_op jit(solution)/shard_map/ppermute | solution.py:20
  102.5 28.5 %collective-permute-start.6 = (f32[3,16,128]{2,1,0:T(8,128)S(1)}, f32[3,16,128]{2,1,0:T(8,128)S(1)}, u32[]{:S(2)}, u32[]{:S(2)}) collective-permute-start(f32[3,16,128]{2,1,0:T(8,128)S(1)} %get-tuple-element.483), channel_id=1, source_target_pairs={{0,64},{64,128},{128,192},{192,256},{256,320},{320,384},{384,448},... | collective-permute-start | bytes 73736 | tf_op jit(solution)/shard_map/ppermute | solution.py:18
  104.7 26.3 %collective-permute-start.7 = (f32[3,16,128]{2,1,0:T(8,128)S(1)}, f32[3,16,128]{2,1,0:T(8,128)S(1)}, u32[]{:S(2)}, u32[]{:S(2)}) collective-permute-start(f32[3,16,128]{2,1,0:T(8,128)S(1)} %get-tuple-element.484), channel_id=1, source_target_pairs={{64,0},{128,64},{192,128},{256,192},{320,256},{384,320},{448,384},... | collective-permute-start | bytes 73736 | tf_op jit(solution)/shard_map/ppermute | solution.py:20
  137.7 21.6 %collective-permute-start.18 = (f32[3,16,128]{2,1,0:T(8,128)S(1)}, f32[3,16,128]{2,1,0:T(8,128)S(1)}, u32[]{:S(2)}, u32[]{:S(2)}) collective-permute-start(f32[3,16,128]{2,1,0:T(8,128)S(1)} %get-tuple-element.473), channel_id=1, source_target_pairs={{0,64},{64,128},{128,192},{192,256},{256,320},{320,384},{384,448},... | collective-permute-start | bytes 73736 | tf_op jit(solution)/shard_map/ppermute | solution.py:18
  139.7 19.7 %collective-permute-start.19 = (f32[3,16,128]{2,1,0:T(8,128)S(1)}, f32[3,16,128]{2,1,0:T(8,128)S(1)}, u32[]{:S(2)}, u32[]{:S(2)}) collective-permute-start(f32[3,16,128]{2,1,0:T(8,128)S(1)} %get-tuple-element.474), channel_id=1, source_target_pairs={{64,0},{128,64},{192,128},{256,192},{320,256},{384,320},{448,384},... | collective-permute-start | bytes 73736 | tf_op jit(solution)/shard_map/ppermute | solution.py:20
  166.1 21.6 %collective-permute-start.30 = (f32[3,16,128]{2,1,0:T(8,128)S(1)}, f32[3,16,128]{2,1,0:T(8,128)S(1)}, u32[]{:S(2)}, u32[]{:S(2)}) collective-permute-start(f32[3,16,128]{2,1,0:T(8,128)S(1)} %get-tuple-element.463), channel_id=1, source_target_pairs={{0,64},{64,128},{128,192},{192,256},{256,320},{320,384},{384,448},... | collective-permute-start | bytes 73736 | tf_op jit(solution)/shard_map/ppermute | solution.py:18
  168.1 19.7 %collective-permute-start.31 = (f32[3,16,128]{2,1,0:T(8,128)S(1)}, f32[3,16,128]{2,1,0:T(8,128)S(1)}, u32[]{:S(2)}, u32[]{:S(2)}) collective-permute-start(f32[3,16,128]{2,1,0:T(8,128)S(1)} %get-tuple-element.464), channel_id=1, source_target_pairs={{64,0},{128,64},{192,128},{256,192},{320,256},{384,320},{448,384},... | collective-permute-start | bytes 73736 | tf_op jit(solution)/shard_map/ppermute | solution.py:20
  194.5 21.6 %collective-permute-start.42 = (f32[3,16,128]{2,1,0:T(8,128)S(1)}, f32[3,16,128]{2,1,0:T(8,128)S(1)}, u32[]{:S(2)}, u32[]{:S(2)}) collective-permute-start(f32[3,16,128]{2,1,0:T(8,128)S(1)} %get-tuple-element.453), channel_id=1, source_target_pairs={{0,64},{64,128},{128,192},{192,256},{256,320},{320,384},{384,448},... | collective-permute-start | bytes 73736 | tf_op jit(solution)/shard_map/ppermute | solution.py:18
  196.5 19.7 %collective-permute-start.43 = (f32[3,16,128]{2,1,0:T(8,128)S(1)}, f32[3,16,128]{2,1,0:T(8,128)S(1)}, u32[]{:S(2)}, u32[]{:S(2)}) collective-permute-start(f32[3,16,128]{2,1,0:T(8,128)S(1)} %get-tuple-element.454), channel_id=1, source_target_pairs={{64,0},{128,64},{192,128},{256,192},{320,256},{384,320},{448,384},... | collective-permute-start | bytes 73736 | tf_op jit(solution)/shard_map/ppermute | solution.py:20
  (29 other events, 362.3 us)
where the time goes:
time: 219 us; the launch traced here: 217 us
  starting transfers between devices  175 us (80%)
  other arithmetic  21.7 us (10%)
  waiting for transfers between devices  17.1 us (8%)
    ppermute x24, starting transfers between devices, padded(): lax.ppermute(head, axis, [((i + 1) % count, i) for i in range(count)])  92.4 us
    ppermute x24, starting transfers between devices, padded(): lax.ppermute(tail, axis, [(i, (i + 1) % count) for i in range(count)])  83.1 us
    ppermute x24, waiting for transfers between devices, padded(): lax.ppermute(head, axis, [((i + 1) % count, i) for i in range(count)])  17 us
    add_any x4, other arithmetic, hamiltonian(): -plus_side  4.92 us
  transfers between devices with their start and end apart: 48, of which 4 were waited for; matrix products, arithmetic and copies ran while one was open for 3% of the time, Pallas kernels for 0%

commit v1 on v0

v1 whole, which is shorter than its diff:
```python
import jax
import jax.numpy as jnp
from jax import lax
from jax.experimental import pallas as pl
from jax.experimental.pallas import tpu as pltpu
from jax.sharding import PartitionSpec as P

TAU = 0.3
WENO_EPS = 1e-06
SMOOTH_EPS = 0.01
LANES = 128
BX, BY = 8, 16
F32 = jnp.float32


def lane_iota(shape):
    return lax.broadcasted_iota(jnp.int32, shape, len(shape) - 1)


def major_roll(v, k):
    n = v.shape[0]
    return jnp.concatenate([v[(g + k) % n][None] for g in range(n)], axis=0)


def shift_x(v, k):
    lane = lane_iota(v.shape)
    rolled = pltpu.roll(v, (-BY * k) % LANES, 2)
    carried = pltpu.roll(rolled, (-1 if k > 0 else 1) % v.shape[1], 1)
    crossing = lane >= LANES - BY * k if k > 0 else lane < -BY * k
    return jnp.where(crossing, carried, rolled)


def shift_y(v, k):
    inner = lane_iota(v.shape) % BY
    rolled = pltpu.roll(v, (-k) % LANES, 2)
    if k > 0:
        carried = major_roll(pltpu.roll(v, (BY - k) % LANES, 2), 1)
        return jnp.where(inner >= BY - k, carried, rolled)
    carried = major_roll(pltpu.roll(v, (-BY - k) % LANES, 2), -1)
    return jnp.where(inner < -k, carried, rolled)


def weno_center(b, dm, d0, d1, d2):
    e1, e2, e3 = d0 - dm, d1 - d0, d2 - d1
    p1, p2, p3 = 0.5 * e1 + d0, 0.5 * (d0 + d1), 0.5 * e3 - d1
    f1, f2, f3 = (13.0 / 12.0) * e1, (13.0 / 12.0) * e2, (13.0 / 12.0) * e3
    t1 = WENO_EPS + (f1 * e1 + p1 * p1)
    t2 = WENO_EPS + (f2 * e2 + p2 * p2)
    t3 = WENO_EPS + (f3 * e3 + p3 * p3)
    t12 = t1 * t2
    whole = 1.0 / (t12 * t3)
    i3 = whole * t12
    whole3 = whole * t3
    i1, i2 = whole3 * t2, whole3 * t1
    a1, a2, a3 = i1 * i1, i2 * i2, i3 * i3
    m1, m2, m3 = 0.1 * a1, 0.6 * a2, 0.3 * a3
    r1, r3 = 0.1 * a3, 0.3 * a1
    sum_m, sum_p = m1 + m2 + m3, r1 + m2 + r3
    both = 1.0 / (sum_m * sum_p)
    inv_m, inv_p = both * sum_p, both * sum_m
    w1, w2, w3 = m1 * inv_m, m2 * inv_m, m3 * inv_m
    v1, v2, v3 = r1 * inv_p, m2 * inv_p, r3 * inv_p
    y1, y3 = (e1 - e2) * (1.0 / 3.0), (e2 - e3) * (1.0 / 6.0)
    y1h, y3d = 0.5 * y1, 2.0 * y3
    corr_m = w1 * y1 + w3 * y3
    corr_p = v1 * y3d + v3 * y1h
    base = b + e2 * (1.0 / 3.0)
    minus = base + 0.5 * d0 + corr_m
    plus = base - 0.5 * d1 - corr_p
    j1, j2, j3 = -4.0 * i1, -4.0 * i2, -4.0 * i3
    g1, g3 = f1 + 0.5 * p1, f3 + 0.5 * p3
    half_p2 = 0.5 * p2

    def spread(s1, s2, s3, cy1, cy3, own0, own1):
        ce1 = cy1 + s1 * g1
        ce2 = (cy3 - cy1) + ((1.0 / 3.0) + s2 * f2)
        ce3 = s3 * g3 - cy3
        s2p = s2 * half_p2
        cd0 = s1 * p1 + s2p
        cd1 = s2p - s3 * p3
        if own0:
            cd0 = cd0 + 0.5
        if own1:
            cd1 = cd1 - 0.5
        return (-ce1, cd0 + (ce1 - ce2), cd1 + (ce2 - ce3), ce3)

    jac_m = spread(
        j1 * (w1 * (y1 - corr_m)), -j2 * (w2 * corr_m), j3 * (w3 * (y3 - corr_m)),
        w1 * (1.0 / 3.0), w3 * (1.0 / 6.0), True, False,
    )
    jac_p = spread(
        j1 * (v3 * (corr_p - y1h)), j2 * (v2 * corr_p), j3 * (v1 * (corr_p - y3d)),
        v3 * (-1.0 / 6.0), v1 * (-1.0 / 3.0), False, True,
    )
    return minus, plus, jac_m, jac_p


def upwind_term(minus, plus, side):
    u = jnp.maximum(side * minus, 0.0)
    v = jnp.maximum(-side * plus, 0.0)
    uu, vv = u * u, v * v
    gap = uu - vv
    square = gap * gap + SMOOTH_EPS
    root = lax.rsqrt(square)
    slope = gap * root
    term = 0.5 * (uu + vv + square * root)
    return term, 2.0 * ((1.0 + slope) * (u * side)), -2.0 * ((1.0 - slope) * (v * side))


PER_AXIS = 10


def coef_kernel(section, f_ref, lo_ref, hi_ref, phi_ref, co_ref, pc_ref):
    fref = f_ref

    def keep(axis, z, minus_plus, jac_m, jac_p):
        for n, part in enumerate(minus_plus + jac_m + jac_p):
            co_ref[PER_AXIS * axis + n, z] = part

    def plane(z, carry):
        f = fref[z]
        side = jnp.where(phi_ref[z] > 0, 1.0, -1.0).astype(F32)
        total = None
        for axis, shift in ((0, shift_x), (1, shift_y)):
            b = f - shift(f, -1)
            d = b - shift(b, -1)
            minus, plus, jac_m, jac_p = weno_center(b, shift(d, -1), d, shift(d, 1), shift(d, 2))
            term, by_minus, by_plus = upwind_term(minus, shift(plus, 1), side)
            keep(axis, z, (by_minus, by_plus), jac_m, jac_p)
            total = term if total is None else total + term
        pc_ref[z] = total
        return carry

    lax.fori_loop(0, 4, plane, 0)

    def column(g, carry):
        f = (
            [lo_ref[3 * section + i, g] for i in range(3)]
            + [fref[i, g] for i in range(4)]
            + [hi_ref[3 * section + i, g] for i in range(3)]
        )
        b = [None] + [f[i] - f[i - 1] for i in range(1, 10)]
        d = [None, None] + [b[i] - b[i - 1] for i in range(2, 10)]
        centers = [weno_center(b[m + 3], d[m + 2], d[m + 3], d[m + 4], d[m + 5]) for m in range(5)]
        for z in range(4):
            phi = phi_ref[z, g]
            side = jnp.where(phi > 0, 1.0, -1.0).astype(F32)
            term, by_minus, by_plus = upwind_term(centers[z][0], centers[z + 1][1], side)
            square = phi * phi + 1.0
            root = lax.rsqrt(square)
            ham2 = pc_ref[z, g] + term
            inv = lax.rsqrt(ham2)
            ham = ham2 * inv
            scale = (-0.25 * TAU) * ((phi * root) * inv)
            pc_ref[z, g] = (-TAU) * ((root * root * root) * (ham - 1.0))
            for axis in (0, 1):
                for n in (0, 1):
                    co_ref[PER_AXIS * axis + n, z, g] = co_ref[PER_AXIS * axis + n, z, g] * scale
            parts = (by_minus * scale, by_plus * scale) + centers[z][2] + centers[z + 1][3]
            for n, part in enumerate(parts):
                co_ref[PER_AXIS * 2 + n, z, g] = part
        return carry

    lax.fori_loop(0, 4, column, 0)


def apply_local(c_ref, co_ref, out_ref, up_ref, dn_ref):
    def plane(z, carry):
        c = c_ref[z]
        total = None
        for axis, shift in ((0, shift_x), (1, shift_y)):
            co = lambda n: co_ref[PER_AXIS * axis + n, z]
            a = c * co(0)
            g = shift(c * co(1), -1)
            t = [a * co(2 + k) + g * co(6 + k) for k in range(4)]
            dbar = t[1] + shift(t[0], 1) + shift(t[2], -1) + shift(t[3], -2)
            bbar = (a + g) + (dbar - shift(dbar, 1))
            part = bbar - shift(bbar, 1)
            total = part if total is None else total + part
        out_ref[z] = total
        return carry

    lax.fori_loop(0, 4, plane, 0)

    def column(g, carry):
        dbar = [None] * 8
        bbar = [None] * 9

        def add(into, at, value):
            into[at] = value if into[at] is None else into[at] + value

        for z in range(4):
            c = c_ref[z, g]
            co = lambda n: co_ref[PER_AXIS * 2 + n, z, g]
            a, p = c * co(0), c * co(1)
            for k in range(4):
                add(dbar, z + k, a * co(2 + k))
                add(dbar, z + k + 1, p * co(6 + k))
            add(bbar, z + 2, a)
            add(bbar, z + 3, p)
        for j in range(8):
            add(bbar, j + 1, dbar[j])
            add(bbar, j, -dbar[j])
        for z in range(4):
            out_ref[z, g] = out_ref[z, g] + (bbar[z + 2] - bbar[z + 3])
        for k in range(3):
            up_ref[k, g] = bbar[6 + k]
            dn_ref[k, g] = bbar[k]
        return carry

    lax.fori_loop(0, 4, column, 0)


def joined(own_ref, lo_ref, hi_ref):
    lo0, lo1, lo2 = lo_ref[0], lo_ref[1], lo_ref[2]
    hi0, hi1, hi2 = hi_ref[0], hi_ref[1], hi_ref[2]
    return (
        own_ref[0] + (lo0 - lo1),
        own_ref[1] + (lo1 - lo2 - hi0),
        own_ref[2] + (lo2 + hi0 - hi1),
        own_ref[3] + (hi1 - hi2),
    )


def stage_one(cot_ref, co_ref, pc_ref, own_ref, up_ref, dn_ref, c_ref, acc_ref):
    half = 0.5 * cot_ref[...]
    c_ref[...] = half
    acc_ref[...] = pc_ref[...] * half
    apply_local(c_ref, co_ref, own_ref, up_ref, dn_ref)


def stage_two(half_ref, own_in, lo_ref, hi_ref, acc_in, co_ref, pc_ref, own_ref, up_ref, dn_ref, c_ref, acc_ref):
    for z, back in enumerate(joined(own_in, lo_ref, hi_ref)):
        c = half_ref[z] + back
        c_ref[z] = c
        acc_ref[z] = acc_in[z] + pc_ref[z] * c
    apply_local(c_ref, co_ref, own_ref, up_ref, dn_ref)


def stage_three(half_ref, second_ref, own_in, lo_ref, hi_ref, acc_in, co_ref, pc_ref, own_ref, up_ref, dn_ref, c_ref, acc_ref):
    for z, back in enumerate(joined(own_in, lo_ref, hi_ref)):
        c = 0.5 * (half_ref[z] + second_ref[z] + back)
        c_ref[z] = c
        acc_ref[z] = acc_in[z] + pc_ref[z] * c
    apply_local(c_ref, co_ref, own_ref, up_ref, dn_ref)


def stage_four(middle_ref, own_in, lo_ref, hi_ref, acc_in, co_ref, pc_ref, own_ref, up_ref, dn_ref, c_ref, acc_ref):
    for z, back in enumerate(joined(own_in, lo_ref, hi_ref)):
        c = middle_ref[z] + back
        c_ref[z] = c
        acc_ref[z] = acc_in[z] + pc_ref[z] * c + (middle_ref[z] + c)
    apply_local(c_ref, co_ref, own_ref, up_ref, dn_ref)


def finish(own_in, lo_ref, hi_ref, acc_in, out_ref):
    for z, back in enumerate(joined(own_in, lo_ref, hi_ref)):
        whole = acc_in[z] + back
        for gy in range(whole.shape[0]):
            for gx in range(whole.shape[1]):
                out_ref[gy * whole.shape[1] + gx, z] = whole[gy, gx]


def slab_path(n_gx, n_gy):
    position = {}
    for gy in range(n_gy):
        for step in range(n_gx):
            gx = step if gy % 2 == 0 else n_gx - 1 - step
            position[gy, gx] = gy * n_gx + step
    return position


def to_slabs(count, depth, position, *refs):
    odd_ref, ins, out_ref, scratch = refs[0], refs[1:-2], refs[-2], refs[-1]
    odd = odd_ref[0] == 1
    for n, ref in enumerate(ins):
        block = ref[...].reshape(BX * BY, LANES)
        scratch[...] = block.T
        for j in range(count):
            at = position[j]
            even_rows = scratch[pl.ds(depth * at, depth), :]
            odd_rows = scratch[pl.ds(depth * (count - 1 - at), depth), :]
            out_ref[j, pl.ds(depth * n, depth), :] = jnp.where(odd, odd_rows, even_rows)


def from_slabs(count, depth, position, odd_ref, in_ref, out_ref, scratch):
    odd = odd_ref[0] == 1
    for j in range(count):
        at = position[j]
        rows = in_ref[j]

        @pl.when(odd)
        def _():
            scratch[pl.ds(depth * (count - 1 - at), depth), :] = rows

        @pl.when(jnp.logical_not(odd))
        def _():
            scratch[pl.ds(depth * at, depth), :] = rows

    out_ref[...] = scratch[...].T.reshape(BX, BY, LANES)


def unpack(n_gy, n_gx, in_ref, f0, f1, f2, f3, f4, up_ref, dn_ref):
    outs = (f0, f1, f2, f3, f4)
    for n, out in enumerate(outs):
        for z in range(4):
            for gy in range(n_gy):
                rows = in_ref[pl.ds(gy * n_gx, n_gx), 4 * n + z, :]
                out[z, gy] = rows
                if n < 4:
                    if z >= 1:
                        up_ref[3 * n + z - 1, gy] = rows
                    if z <= 2:
                        dn_ref[3 * n + z, gy] = rows


def make_shards(sizes, interpret=False):
    n_gx, n_gy, n_gz = sizes["gx"], sizes["gy"], sizes["gz"]
    count = n_gx * n_gy
    depth = LANES // count
    assert depth == 4
    position = slab_path(n_gx, n_gy)
    flat_position = [position[j // n_gx, j % n_gx] for j in range(count)]
    order = []
    for gz in range(n_gz):
        line = sorted(position, key=position.get, reverse=gz % 2 == 1)
        order += [(gx * n_gy + gy) * n_gz + gz for gy, gx in line]
    total = len(order)
    upward = [(order[i], order[(i + 1) % total]) for i in range(total)]
    downward = [(order[(i + 1) % total], order[i]) for i in range(total)]
    everywhere = ("gx", "gy", "gz")
    vmem = pl.BlockSpec(memory_space=pltpu.VMEM)
    smem = pl.BlockSpec(memory_space=pltpu.SMEM)
    slab = (4, n_gy, n_gx, LANES)
    rim = (3, n_gy, n_gx, LANES)

    def like(*shape):
        return jax.ShapeDtypeStruct(shape, F32)

    def call(kernel, out_shape, *args, first=vmem, scratch=(), name=None):
        many = isinstance(out_shape, list)
        return pl.pallas_call(
            kernel,
            out_shape=out_shape,
            in_specs=[first] + [vmem] * (len(args) - 1),
            out_specs=[vmem] * len(out_shape) if many else vmem,
            scratch_shapes=list(scratch),
            name=name,
            interpret=interpret,
        )(*args)

    def exchange(up, dn):
        return lax.ppermute(up, everywhere, upward), lax.ppermute(dn, everywhere, downward)

    def shards(phi_start, section_first, section_middle, section_second, cot_final):
        odd = (lax.axis_index("gz") % 2).astype(jnp.int32).reshape(1)
        turn = pltpu.VMEM((LANES, LANES), F32)

        packed = call(
            lambda *refs: to_slabs(count, depth, flat_position, *refs),
            like(count, 5 * depth, LANES),
            odd, section_second, section_middle, section_first, phi_start, cot_final,
            first=smem, scratch=[turn], name="to_slabs",
        )
        packed = lax.all_to_all(packed, ("gy", "gx"), 0, 0)
        *fields, rim_up, rim_dn = call(
            lambda *refs: unpack(n_gy, n_gx, *refs),
            [like(*slab)] * 5 + [like(12, *slab[1:])] * 2,
            packed, name="unpack",
        )
        phi, cot = fields[3], fields[4]
        rim_lo, rim_hi = exchange(rim_up, rim_dn)

        def coefs(n):
            return call(
                lambda *refs: coef_kernel(n, *refs),
                [like(3 * PER_AXIS, *slab), like(*slab)],
                fields[n], rim_lo, rim_hi, phi, name=f"coefs_{n}",
            )

        results = [like(*slab), like(*rim), like(*rim), like(*slab), like(*slab)]
        co, pc = coefs(0)
        own, up, dn, half, acc = call(stage_one, results, cot, co, pc, name="stage_one")
        lo, hi = exchange(up, dn)
        co, pc = coefs(1)
        own, up, dn, second, acc = call(stage_two, results, half, own, lo, hi, acc, co, pc, name="stage_two")
        lo, hi = exchange(up, dn)
        co, pc = coefs(2)
        own, up, dn, middle, acc = call(stage_three, results, half, second, own, lo, hi, acc, co, pc, name="stage_three")
        lo, hi = exchange(up, dn)
        co, pc = coefs(3)
        own, up, dn, _, acc = call(stage_four, results, middle, own, lo, hi, acc, co, pc, name="stage_four")
        lo, hi = exchange(up, dn)
        slabs = call(finish, like(count, depth, LANES), own, lo, hi, acc, name="finish")
        slabs = lax.all_to_all(slabs, ("gy", "gx"), 0, 0)
        return call(
            lambda *refs: from_slabs(count, depth, flat_position, *refs),
            like(BX, BY, LANES), odd, slabs, first=smem, scratch=[turn], name="from_slabs",
        )

    return shards


def solution(mesh):
    spec = P("gx", "gy", "gz")
    return jax.shard_map(
        make_shards(dict(mesh.shape)),
        mesh=mesh,
        in_specs=(spec,) * 5,
        out_specs=spec,
        check_vma=False,
    )
```

time: 219 us -> 145 us (0.66)
  the two profiles are of different devices: /device:TPU:7 before, /device:TPU:6 now
where the time goes in v1:
time: 145 us; the launch traced here: 144 us
  blocking collectives  60.7 us (42%)
  Pallas kernels  42.3 us (29%)
  starting transfers between devices  27.8 us (19%)
  waiting for transfers between devices  9.59 us (7%)
  local copies, waits for them, and re-layouts  3.17 us (2%)
    pallas_call x12, Pallas kernels, call(): pl.pallas_call(kernel, out_shape=out_shape, in_specs=[first] + [vmem] * (...  42.3 us
    all_to_all x1, blocking collectives, shards(): packed = lax.all_to_all(packed, ('gy', 'gx'), 0, 0)  32.7 us
    all_to_all x1, blocking collectives, shards(): slabs = lax.all_to_all(slabs, ('gy', 'gx'), 0, 0)  28 us
    ppermute x5, starting transfers between devices, exchange(): lax.ppermute(up, everywhere, upward)  14.4 us
    ppermute x5, starting transfers between devices, exchange(): lax.ppermute(dn, everywhere, downward)  13.4 us
    ppermute x5, waiting for transfers between devices, exchange(): lax.ppermute(dn, everywhere, downward)  6.88 us
    unnamed x20, local copies, waits for them, and re-layouts  3.17 us
  transfers between devices with their start and end apart: 10, of which 3 were waited for; matrix products, arithmetic and copies ran while one was open for 0% of the time, Pallas kernels for 10%

profile of v1, /device:TPU:6, one launch (start us, length us, event | category | flops | bytes accessed | tf_op | source)
XLA Modules:
  0.0 143.7 jit_solution(6537202869121885184)
XLA Ops:
  0.0 1.9 %to_slabs.1 = f32[32,20,128]{2,1,0:T(8,128)} custom-call(s32[1]{0:T(128)} %bitcast.refs_0_, f32[8,16,128]{2,1,0:T(8,128)} %refs_1_.1, f32[8,16,128]{2,1,0:T(8,128)} %refs_2_.1, f32[8,16,128]{2,1,0:T(8,128)} %refs_3_.1, f32[8,16,128]{2,1,0:T(8,128)} %refs_4_.1, f32[8,16,128]{2,1,0:T(8,128)} %refs_5_.1), custom_call_target="tpu_custom_call" | custom-call | tf_op jit(solution)/shard_map/to_slabs/pallas_call | solution.py:342
  1.9 32.7 %all_to_all.10.refs_0_ = f32[32,20,128]{2,1,0:T(8,128)} all-to-all(f32[32,20,128]{2,1,0:T(8,128)} %to_slabs.1), channel_id=1, replica_groups=mesh['gx'=8,'gy'=4,'gz'=16] {'gy','gx'}, dimensions={0} | all-to-all | bytes 655360 | tf_op jit(solution)/shard_map/all_to_all | solution.py:365
  34.6 2.0 %unpack.1 = (f32[4,4,8,128]{3,2,1,0:T(8,128)}, f32[4,4,8,128]{3,2,1,0:T(8,128)}, f32[4,4,8,128]{3,2,1,0:T(8,128)}, f32[4,4,8,128]{3,2,1,0:T(8,128)}, f32[4,4,8,1...) custom-call(f32[32,20,128]{2,1,0:T(8,128)} %all_to_all.10.refs_0_), custom_call_target="tpu_custom_call" | custom-call | tf_op jit(solution)/shard_map/unpack/pallas_call | solution.py:342
  36.6 3.7 %collective-permute-start = (f32[12,4,8,128]{3,2,1,0:T(8,128)}, f32[12,4,8,128]{3,2,1,0:T(8,128)S(1)}, u32[]{:S(2)}, u32[]{:S(2)}) collective-permute-start(f32[12,4,8,128]{3,2,1,0:T(8,128)} %get-tuple-element.41), channel_id=1, source_target_pairs={{0,64},{64,128},{128,192},{192,256},{256,320},{320,384},{384,448},... | collective-permute-start | bytes 589832 | tf_op jit(solution)/shard_map/ppermute | solution.py:353
  42.2 2.7 %collective-permute-done.refs_1_ = f32[12,4,8,128]{3,2,1,0:T(8,128)S(1)} collective-permute-done((f32[12,4,8,128]{3,2,1,0:T(8,128)}, f32[12,4,8,128]{3,2,1,0:T(8,128)S(1)}, u32[]{:S(2)}, u32[]{:S(2)}) %collective-permute-start) | collective-permute-done | bytes 196640 | tf_op jit(solution)/shard_map/ppermute | solution.py:353
  44.9 3.2 %collective-permute-done.1.refs_2_ = f32[12,4,8,128]{3,2,1,0:T(8,128)S(1)} collective-permute-done((f32[12,4,8,128]{3,2,1,0:T(8,128)}, f32[12,4,8,128]{3,2,1,0:T(8,128)S(1)}, u32[]{:S(2)}, u32[]{:S(2)}) %collective-permute-start.1) | collective-permute-done | bytes 196640 | tf_op jit(solution)/shard_map/ppermute | solution.py:353
  48.8 4.9 %coefs_0.1 = (f32[30,4,4,8,128]{4,3,2,1,0:T(8,128)}, f32[4,4,8,128]{3,2,1,0:T(8,128)}) custom-call(f32[4,4,8,128]{3,2,1,0:T(8,128)} %get-tuple-element.40.refs_0_, f32[12,4,8,128]{3,2,1,0:T(8,128)} %copy-done, f32[12,4,8,128]{3,2,1,0:T(8,128)} %copy-done.1, f32[4,4,8,128]{3,2,1,0:T(8,128)} %get-tuple-element.43.refs_3_.refs_0_), custom_call_target="tpu_custom_call" | custom-call | tf_op jit(solution)/shard_map/coefs_0/pallas_call | solution.py:342
  53.7 3.8 %stage_one.1 = (f32[4,4,8,128]{3,2,1,0:T(8,128)}, f32[3,4,8,128]{3,2,1,0:T(8,128)}, f32[3,4,8,128]{3,2,1,0:T(8,128)}, f32[4,4,8,128]{3,2,1,0:T(8,128)}, f32[4,4,8,128]{3,2,1,0:T(8,128)}) custom-call(f32[4,4,8,128]{3,2,1,0:T(8,128)} %get-tuple-element.39.cot_ref, f32[30,4,4,8,128]{4,3,2,1,0:T(8,128)} %get-tuple-element.44.co_ref, ...), custom_call_target="tpu_custom_call" | custom-call | tf_op jit(solution)/shard_map/stage_one/pallas_call | solution.py:342
  57.4 2.3 %collective-permute-start.2 = (f32[3,4,8,128]{3,2,1,0:T(8,128)}, f32[3,4,8,128]{3,2,1,0:T(8,128)S(1)}, u32[]{:S(2)}, u32[]{:S(2)}) collective-permute-start(f32[3,4,8,128]{3,2,1,0:T(8,128)} %get-tuple-element.48), channel_id=1, source_target_pairs={{0,64},{64,128},{128,192},{192,256},{256,320},{320,384},{384,448},... | collective-permute-start | bytes 147464 | tf_op jit(solution)/shard_map/ppermute | solution.py:353
  59.7 3.3 %collective-permute-start.3 = (f32[3,4,8,128]{3,2,1,0:T(8,128)}, f32[3,4,8,128]{3,2,1,0:T(8,128)S(1)}, u32[]{:S(2)}, u32[]{:S(2)}) collective-permute-start(f32[3,4,8,128]{3,2,1,0:T(8,128)} %get-tuple-element.49), channel_id=1, source_target_pairs={{64,0},{128,64},{192,128},{256,192},{320,256},{384,320},{448,384},... | collective-permute-start | bytes 147464 | tf_op jit(solution)/shard_map/ppermute | solution.py:353
  63.0 4.9 %coefs_1.1 = (f32[30,4,4,8,128]{4,3,2,1,0:T(8,128)}, f32[4,4,8,128]{3,2,1,0:T(8,128)}) custom-call(f32[4,4,8,128]{3,2,1,0:T(8,128)} %get-tuple-element.51.refs_0_, f32[12,4,8,128]{3,2,1,0:T(8,128)} %copy-done, f32[12,4,8,128]{3,2,1,0:T(8,128)} %copy-done.1, f32[4,4,8,128]{3,2,1,0:T(8,128)} %get-tuple-element.43.refs_3_.refs_0_), custom_call_target="tpu_custom_call" | custom-call | tf_op jit(solution)/shard_map/coefs_1/pallas_call | solution.py:342
  68.5 3.9 %stage_two.1 = (f32[4,4,8,128]{3,2,1,0:T(8,128)}, f32[3,4,8,128]{3,2,1,0:T(8,128)}, f32[3,4,8,128]{3,2,1,0:T(8,128)}, f32[4,4,8,128]{3,2,1,0:T(8,128)}, f32[4,4,8,128]{3,2,1,0:T(8,128)}) custom-call(f32[4,4,8,128]{3,2,1,0:T(8,128)} %get-tuple-element.46.half_ref, f32[4,4,8,128]{3,2,1,0:T(8,128)} %get-tuple-element.47.own_in, f32[3,4,8,128]{3,2,1,0:T(8,128)} %copy-done.6, ...), custom_call_target="tpu_custom_call" | custom-call | tf_op jit(solution)/shard_map/stage_two/pallas_call | solution.py:342
  72.4 2.5 %collective-permute-start.4 = (f32[3,4,8,128]{3,2,1,0:T(8,128)}, f32[3,4,8,128]{3,2,1,0:T(8,128)S(1)}, u32[]{:S(2)}, u32[]{:S(2)}) collective-permute-start(f32[3,4,8,128]{3,2,1,0:T(8,128)} %get-tuple-element.56), channel_id=1, source_target_pairs={{0,64},{64,128},{128,192},{192,256},{256,320},{320,384},{384,448},... | collective-permute-start | bytes 147464 | tf_op jit(solution)/shard_map/ppermute | solution.py:353
  75.0 3.0 %collective-permute-start.5 = (f32[3,4,8,128]{3,2,1,0:T(8,128)}, f32[3,4,8,128]{3,2,1,0:T(8,128)S(1)}, u32[]{:S(2)}, u32[]{:S(2)}) collective-permute-start(f32[3,4,8,128]{3,2,1,0:T(8,128)} %get-tuple-element.57), channel_id=1, source_target_pairs={{64,0},{128,64},{192,128},{256,192},{320,256},{384,320},{448,384},... | collective-permute-start | bytes 147464 | tf_op jit(solution)/shard_map/ppermute | solution.py:353
  78.0 4.9 %coefs_2.1 = (f32[30,4,4,8,128]{4,3,2,1,0:T(8,128)}, f32[4,4,8,128]{3,2,1,0:T(8,128)}) custom-call(f32[4,4,8,128]{3,2,1,0:T(8,128)} %get-tuple-element.59.refs_0_, f32[12,4,8,128]{3,2,1,0:T(8,128)} %copy-done, f32[12,4,8,128]{3,2,1,0:T(8,128)} %copy-done.1, f32[4,4,8,128]{3,2,1,0:T(8,128)} %get-tuple-element.43.refs_3_.refs_0_), custom_call_target="tpu_custom_call" | custom-call | tf_op jit(solution)/shard_map/coefs_2/pallas_call | solution.py:342
  83.5 4.0 %stage_three.1 = (f32[4,4,8,128]{3,2,1,0:T(8,128)}, f32[3,4,8,128]{3,2,1,0:T(8,128)}, f32[3,4,8,128]{3,2,1,0:T(8,128)}, f32[4,4,8,128]{3,2,1,0:T(8,128)}, f32[4,4,8,128]{3,2,1,0:T(8,128)}) custom-call(f32[4,4,8,128]{3,2,1,0:T(8,128)} %get-tuple-element.46.half_ref, f32[4,4,8,128]{3,2,1,0:T(8,128)} %get-tuple-element.54.second_ref, ...), custom_call_target="tpu_custom_call" | custom-call | tf_op jit(solution)/shard_map/stage_three/pallas_call | solution.py:342
  87.6 2.8 %collective-permute-start.6 = (f32[3,4,8,128]{3,2,1,0:T(8,128)}, f32[3,4,8,128]{3,2,1,0:T(8,128)S(1)}, u32[]{:S(2)}, u32[]{:S(2)}) collective-permute-start(f32[3,4,8,128]{3,2,1,0:T(8,128)} %get-tuple-element.64), channel_id=1, source_target_pairs={{0,64},{64,128},{128,192},{192,256},{256,320},{320,384},{384,448},... | collective-permute-start | bytes 147464 | tf_op jit(solution)/shard_map/ppermute | solution.py:353
  90.4 2.7 %collective-permute-start.7 = (f32[3,4,8,128]{3,2,1,0:T(8,128)}, f32[3,4,8,128]{3,2,1,0:T(8,128)S(1)}, u32[]{:S(2)}, u32[]{:S(2)}) collective-permute-start(f32[3,4,8,128]{3,2,1,0:T(8,128)} %get-tuple-element.65), channel_id=1, source_target_pairs={{64,0},{128,64},{192,128},{256,192},{320,256},{384,320},{448,384},... | collective-permute-start | bytes 147464 | tf_op jit(solution)/shard_map/ppermute | solution.py:353
  93.1 4.9 %coefs_3.1 = (f32[30,4,4,8,128]{4,3,2,1,0:T(8,128)}, f32[4,4,8,128]{3,2,1,0:T(8,128)}) custom-call(f32[4,4,8,128]{3,2,1,0:T(8,128)} %get-tuple-element.43.refs_3_.refs_0_, f32[12,4,8,128]{3,2,1,0:T(8,128)} %copy-done, f32[12,4,8,128]{3,2,1,0:T(8,128)} %copy-done.1, f32[4,4,8,128]{3,2,1,0:T(8,128)} %get-tuple-element.43.refs_3_.refs_0_), custom_call_target="tpu_custom_call" | custom-call | tf_op jit(solution)/shard_map/coefs_3/pallas_call | solution.py:342
  98.7 3.9 %stage_four.1 = (f32[4,4,8,128]{3,2,1,0:T(8,128)}, f32[3,4,8,128]{3,2,1,0:T(8,128)}, f32[3,4,8,128]{3,2,1,0:T(8,128)}, f32[4,4,8,128]{3,2,1,0:T(8,128)}, f32[4,4,8,128]{3,2,1,0:T(8,128)}) custom-call(f32[4,4,8,128]{3,2,1,0:T(8,128)} %get-tuple-element.62.middle_ref, f32[4,4,8,128]{3,2,1,0:T(8,128)} %get-tuple-element.63.own_in, f32[3,4,8,128]{3,2,1,0:T(8,128)} %copy-done.5, ...), custom_call_target="tpu_custom_call" | custom-call | tf_op jit(solution)/shard_map/stage_four/pallas_call | solution.py:342
  102.5 3.1 %collective-permute-start.8 = (f32[3,4,8,128]{3,2,1,0:T(8,128)}, f32[3,4,8,128]{3,2,1,0:T(8,128)S(1)}, u32[]{:S(2)}, u32[]{:S(2)}) collective-permute-start(f32[3,4,8,128]{3,2,1,0:T(8,128)} %get-tuple-element.70), channel_id=1, source_target_pairs={{0,64},{64,128},{128,192},{192,256},{256,320},{320,384},{384,448},... | collective-permute-start | bytes 147464 | tf_op jit(solution)/shard_map/ppermute | solution.py:353
  105.6 2.4 %collective-permute-start.9 = (f32[3,4,8,128]{3,2,1,0:T(8,128)}, f32[3,4,8,128]{3,2,1,0:T(8,128)S(1)}, u32[]{:S(2)}, u32[]{:S(2)}) collective-permute-start(f32[3,4,8,128]{3,2,1,0:T(8,128)} %get-tuple-element.71), channel_id=1, source_target_pairs={{64,0},{128,64},{192,128},{256,192},{320,256},{384,320},{448,384},... | collective-permute-start | bytes 147464 | tf_op jit(solution)/shard_map/ppermute | solution.py:353
  108.1 3.7 %collective-permute-done.9.hi_ref = f32[3,4,8,128]{3,2,1,0:T(8,128)S(1)} collective-permute-done((f32[3,4,8,128]{3,2,1,0:T(8,128)}, f32[3,4,8,128]{3,2,1,0:T(8,128)S(1)}, u32[]{:S(2)}, u32[]{:S(2)}) %collective-permute-start.9) | collective-permute-done | bytes 49184 | tf_op jit(solution)/shard_map/ppermute | solution.py:353
  114.0 28.0 %all_to_all.11.refs_1_ = f32[32,4,128]{2,1,0:T(4,128)} all-to-all(f32[32,4,128]{2,1,0:T(4,128)} %finish.1), channel_id=1, replica_groups=mesh['gx'=8,'gy'=4,'gz'=16] {'gy','gx'}, dimensions={0} | all-to-all | bytes 131072 | tf_op jit(solution)/shard_map/all_to_all | solution.py:395
  (30 shorter events, 8.4 us)
Async XLA Ops:
  36.6 8.3 %collective-permute-start = (f32[12,4,8,128]{3,2,1,0:T(8,128)}, f32[12,4,8,128]{3,2,1,0:T(8,128)S(1)}, u32[]{:S(2)}, u32[]{:S(2)}) collective-permute-start(f32[12,4,8,128]{3,2,1,0:T(8,128)} %get-tuple-element.41), channel_id=1, source_target_pairs={{0,64},{64,128},{128,192},{192,256},{256,320},{320,384},{384,448},... | collective-permute-start | bytes 589832 | tf_op jit(solution)/shard_map/ppermute | solution.py:353
  40.3 7.8 %collective-permute-start.1 = (f32[12,4,8,128]{3,2,1,0:T(8,128)}, f32[12,4,8,128]{3,2,1,0:T(8,128)S(1)}, u32[]{:S(2)}, u32[]{:S(2)}) collective-permute-start(f32[12,4,8,128]{3,2,1,0:T(8,128)} %get-tuple-element.42), channel_id=1, source_target_pairs={{64,0},{128,64},{192,128},{256,192},{320,256},{384,320},{448,384},... | collective-permute-start | bytes 589832 | tf_op jit(solution)/shard_map/ppermute | solution.py:353
  44.9 3.2 %copy-start = (f32[12,4,8,128]{3,2,1,0:T(8,128)}, f32[12,4,8,128]{3,2,1,0:T(8,128)S(1)}, u32[]{:S(2)}) copy-start(f32[12,4,8,128]{3,2,1,0:T(8,128)S(1)} %collective-permute-done.refs_1_) | copy-start | bytes 589828
  48.1 0.7 copy-start.1
  57.4 10.5 %collective-permute-start.2 = (f32[3,4,8,128]{3,2,1,0:T(8,128)}, f32[3,4,8,128]{3,2,1,0:T(8,128)S(1)}, u32[]{:S(2)}, u32[]{:S(2)}) collective-permute-start(f32[3,4,8,128]{3,2,1,0:T(8,128)} %get-tuple-element.48), channel_id=1, source_target_pairs={{0,64},{64,128},{128,192},{192,256},{256,320},{320,384},{384,448},... | collective-permute-start | bytes 147464 | tf_op jit(solution)/shard_map/ppermute | solution.py:353
  59.7 8.2 %collective-permute-start.3 = (f32[3,4,8,128]{3,2,1,0:T(8,128)}, f32[3,4,8,128]{3,2,1,0:T(8,128)S(1)}, u32[]{:S(2)}, u32[]{:S(2)}) collective-permute-start(f32[3,4,8,128]{3,2,1,0:T(8,128)} %get-tuple-element.49), channel_id=1, source_target_pairs={{64,0},{128,64},{192,128},{256,192},{320,256},{384,320},{448,384},... | collective-permute-start | bytes 147464 | tf_op jit(solution)/shard_map/ppermute | solution.py:353
  67.9 0.6 copy-start.6
  67.9 0.6 copy-start.9
  72.4 10.4 %collective-permute-start.4 = (f32[3,4,8,128]{3,2,1,0:T(8,128)}, f32[3,4,8,128]{3,2,1,0:T(8,128)S(1)}, u32[]{:S(2)}, u32[]{:S(2)}) collective-permute-start(f32[3,4,8,128]{3,2,1,0:T(8,128)} %get-tuple-element.56), channel_id=1, source_target_pairs={{0,64},{64,128},{128,192},{192,256},{256,320},{320,384},{384,448},... | collective-permute-start | bytes 147464 | tf_op jit(solution)/shard_map/ppermute | solution.py:353
  75.0 7.9 %collective-permute-start.5 = (f32[3,4,8,128]{3,2,1,0:T(8,128)}, f32[3,4,8,128]{3,2,1,0:T(8,128)S(1)}, u32[]{:S(2)}, u32[]{:S(2)}) collective-permute-start(f32[3,4,8,128]{3,2,1,0:T(8,128)} %get-tuple-element.57), channel_id=1, source_target_pairs={{64,0},{128,64},{192,128},{256,192},{320,256},{384,320},{448,384},... | collective-permute-start | bytes 147464 | tf_op jit(solution)/shard_map/ppermute | solution.py:353
  82.9 0.6 copy-start.4
  82.9 0.6 copy-start.7
  87.6 10.4 %collective-permute-start.6 = (f32[3,4,8,128]{3,2,1,0:T(8,128)}, f32[3,4,8,128]{3,2,1,0:T(8,128)S(1)}, u32[]{:S(2)}, u32[]{:S(2)}) collective-permute-start(f32[3,4,8,128]{3,2,1,0:T(8,128)} %get-tuple-element.64), channel_id=1, source_target_pairs={{0,64},{64,128},{128,192},{192,256},{256,320},{320,384},{384,448},... | collective-permute-start | bytes 147464 | tf_op jit(solution)/shard_map/ppermute | solution.py:353
  90.4 7.6 %collective-permute-start.7 = (f32[3,4,8,128]{3,2,1,0:T(8,128)}, f32[3,4,8,128]{3,2,1,0:T(8,128)S(1)}, u32[]{:S(2)}, u32[]{:S(2)}) collective-permute-start(f32[3,4,8,128]{3,2,1,0:T(8,128)} %get-tuple-element.65), channel_id=1, source_target_pairs={{64,0},{128,64},{192,128},{256,192},{320,256},{384,320},{448,384},... | collective-permute-start | bytes 147464 | tf_op jit(solution)/shard_map/ppermute | solution.py:353
  98.0 0.6 copy-start.5
  98.0 0.6 copy-start.8
  102.5 5.6 %collective-permute-start.8 = (f32[3,4,8,128]{3,2,1,0:T(8,128)}, f32[3,4,8,128]{3,2,1,0:T(8,128)S(1)}, u32[]{:S(2)}, u32[]{:S(2)}) collective-permute-start(f32[3,4,8,128]{3,2,1,0:T(8,128)} %get-tuple-element.70), channel_id=1, source_target_pairs={{0,64},{64,128},{128,192},{192,256},{256,320},{320,384},{384,448},... | collective-permute-start | bytes 147464 | tf_op jit(solution)/shard_map/ppermute | solution.py:353
  105.6 6.2 %collective-permute-start.9 = (f32[3,4,8,128]{3,2,1,0:T(8,128)}, f32[3,4,8,128]{3,2,1,0:T(8,128)S(1)}, u32[]{:S(2)}, u32[]{:S(2)}) collective-permute-start(f32[3,4,8,128]{3,2,1,0:T(8,128)} %get-tuple-element.71), channel_id=1, source_target_pairs={{64,0},{128,64},{192,128},{256,192},{320,256},{384,320},{448,384},... | collective-permute-start | bytes 147464 | tf_op jit(solution)/shard_map/ppermute | solution.py:353
  108.1 3.7 %copy-start.2 = (f32[3,4,8,128]{3,2,1,0:T(8,128)}, f32[3,4,8,128]{3,2,1,0:T(8,128)S(1)}, u32[]{:S(2)}) copy-start(f32[3,4,8,128]{3,2,1,0:T(8,128)S(1)} %collective-permute-done.8.lo_ref) | copy-start | bytes 147460
  111.8 0.6 copy-start.3

commit v2 on v1

--- a/solution.py
+++ b/solution.py
@@ -337,14 +337,22 @@
     def like(*shape):
         return jax.ShapeDtypeStruct(shape, F32)
 
-    def call(kernel, out_shape, *args, first=vmem, scratch=(), name=None):
+    def near(*shape):
+        return like(*shape) if interpret else pltpu.VMEM(shape, F32)
+
+    def call(kernel, out_shape, *args, first=vmem, scratch=(), name=None, far=False):
         many = isinstance(out_shape, list)
+        if not (far or interpret):
+            args = [
+                x if x.ndim == 1 else pltpu.with_memory_space_constraint(x, pltpu.VMEM) for x in args
+            ]
         return pl.pallas_call(
             kernel,
             out_shape=out_shape,
             in_specs=[first] + [vmem] * (len(args) - 1),
             out_specs=[vmem] * len(out_shape) if many else vmem,
             scratch_shapes=list(scratch),
+            compiler_params=pltpu.CompilerParams(vmem_limit_bytes=8 << 20),
             name=name,
             interpret=interpret,
         )(*args)
@@ -358,14 +366,14 @@
 
         packed = call(
             lambda *refs: to_slabs(count, depth, flat_position, *refs),
-            like(count, 5 * depth, LANES),
+            near(count, 5 * depth, LANES),
             odd, section_second, section_middle, section_first, phi_start, cot_final,
-            first=smem, scratch=[turn], name="to_slabs",
+            first=smem, far=True, scratch=[turn], name="to_slabs",
         )
         packed = lax.all_to_all(packed, ("gy", "gx"), 0, 0)
         *fields, rim_up, rim_dn = call(
             lambda *refs: unpack(n_gy, n_gx, *refs),
-            [like(*slab)] * 5 + [like(12, *slab[1:])] * 2,
+            [near(*slab)] * 5 + [near(12, *slab[1:])] * 2,
             packed, name="unpack",
         )
         phi, cot = fields[3], fields[4]
@@ -374,11 +382,11 @@
         def coefs(n):
             return call(
                 lambda *refs: coef_kernel(n, *refs),
-                [like(3 * PER_AXIS, *slab), like(*slab)],
+                [near(3 * PER_AXIS, *slab), near(*slab)],
                 fields[n], rim_lo, rim_hi, phi, name=f"coefs_{n}",
             )
 
-        results = [like(*slab), like(*rim), like(*rim), like(*slab), like(*slab)]
+        results = [near(*slab), near(*rim), near(*rim), near(*slab), near(*slab)]
         co, pc = coefs(0)
         own, up, dn, half, acc = call(stage_one, results, cot, co, pc, name="stage_one")
         lo, hi = exchange(up, dn)
@@ -391,7 +399,7 @@
         co, pc = coefs(3)
         own, up, dn, _, acc = call(stage_four, results, middle, own, lo, hi, acc, co, pc, name="stage_four")
         lo, hi = exchange(up, dn)
-        slabs = call(finish, like(count, depth, LANES), own, lo, hi, acc, name="finish")
+        slabs = call(finish, near(count, depth, LANES), own, lo, hi, acc, name="finish")
         slabs = lax.all_to_all(slabs, ("gy", "gx"), 0, 0)
         return call(
             lambda *refs: from_slabs(count, depth, flat_position, *refs),

time: 145 us -> 121 us (0.83)
  Pallas kernels: 42.3 us -> 18 us
  blocking collectives: 60.7 us -> 57.2 us
  waiting for transfers between devices: 9.59 us -> 11.8 us
    pallas_call x12, Pallas kernels: 42.3 us -> 18 us  [call(): pl.pallas_call(kernel, out_shape=out_shape, in_specs=[first] + [vmem] * (...]
    all_to_all x1, blocking collectives: 28 us -> 24.8 us  [shards(): slabs = lax.all_to_all(slabs, ('gy', 'gx'), 0, 0)]
    ppermute x5, waiting for transfers between devices: 6.88 us -> 9.4 us  [exchange(): lax.ppermute(dn, everywhere, downward)]
    ppermute x5, starting transfers between devices: 14.4 us -> 16 us  [exchange(): lax.ppermute(up, everywhere, upward)]
    unnamed x20 -> x10, local copies, waits for them, and re-layouts: 3.17 us -> 4.19 us
  transfers between devices with their start and end apart: 10 -> 10, of which waited for: 3 -> 6; matrix products, arithmetic and copies ran while one was open for 0% -> 0% of each run, Pallas kernels for 10% -> 6%
where the time goes in v2:
time: 121 us; the launch traced here: 120 us
  blocking collectives  57.2 us (47%)
  starting transfers between devices  28.1 us (23%)
  Pallas kernels  18 us (15%)
  waiting for transfers between devices  11.8 us (10%)
  local copies, waits for them, and re-layouts  4.19 us (3%)
    all_to_all x1, blocking collectives, shards(): packed = lax.all_to_all(packed, ('gy', 'gx'), 0, 0)  32.4 us
    all_to_all x1, blocking collectives, shards(): slabs = lax.all_to_all(slabs, ('gy', 'gx'), 0, 0)  24.8 us
    pallas_call x12, Pallas kernels, call(): pl.pallas_call(kernel, out_shape=out_shape, in_specs=[first] + [vmem] * (...  18 us
    ppermute x5, starting transfers between devices, exchange(): lax.ppermute(up, everywhere, upward)  16 us
    ppermute x5, starting transfers between devices, exchange(): lax.ppermute(dn, everywhere, downward)  12.1 us
    ppermute x5, waiting for transfers between devices, exchange(): lax.ppermute(dn, everywhere, downward)  9.4 us
    unnamed x10, local copies, waits for them, and re-layouts  4.19 us
  transfers between devices with their start and end apart: 10, of which 6 were waited for; matrix products, arithmetic and copies ran while one was open for 0% of the time, Pallas kernels for 6%

profile of v2, /device:TPU:6, one launch (start us, length us, event | category | flops | bytes accessed | tf_op | source)
XLA Modules:
  0.0 119.5 jit_solution(11856065730149644286)
XLA Ops:
  4.4 32.4 %all_to_all.10.refs_0_ = f32[32,20,128]{2,1,0:T(8,128)S(1)} all-to-all(f32[32,20,128]{2,1,0:T(8,128)S(1)} %to_slabs.1), channel_id=1, replica_groups=mesh['gx'=8,'gy'=4,'gz'=16] {'gy','gx'}, dimensions={0} | all-to-all | bytes 655360 | tf_op jit(solution)/shard_map/all_to_all | solution.py:373
  37.0 3.7 %collective-permute-start = (f32[12,4,8,128]{3,2,1,0:T(8,128)S(1)}, f32[12,4,8,128]{3,2,1,0:T(8,128)S(1)}, u32[]{:S(2)}, u32[]{:S(2)}) collective-permute-start(f32[12,4,8,128]{3,2,1,0:T(8,128)S(1)} %get-tuple-element.41), channel_id=1, source_target_pairs={{0,64},{64,128},{128,192},{192,256},{256,320},{320,384},{384,448},... | collective-permute-start | bytes 589832 | tf_op jit(solution)/shard_map/ppermute | solution.py:361
  40.7 1.9 %collective-permute-start.1 = (f32[12,4,8,128]{3,2,1,0:T(8,128)S(1)}, f32[12,4,8,128]{3,2,1,0:T(8,128)S(1)}, u32[]{:S(2)}, u32[]{:S(2)}) collective-permute-start(f32[12,4,8,128]{3,2,1,0:T(8,128)S(1)} %get-tuple-element.42), channel_id=1, source_target_pairs={{64,0},{128,64},{192,128},{256,192},{320,256},{384,320},{448,384},... | collective-permute-start | bytes 589832 | tf_op jit(solution)/shard_map/ppermute | solution.py:361
  42.6 2.4 %collective-permute-done.refs_1_ = f32[12,4,8,128]{3,2,1,0:T(8,128)S(1)} collective-permute-done((f32[12,4,8,128]{3,2,1,0:T(8,128)S(1)}, f32[12,4,8,128]{3,2,1,0:T(8,128)S(1)}, u32[]{:S(2)}, u32[]{:S(2)}) %collective-permute-start) | collective-permute-done | bytes 196640 | tf_op jit(solution)/shard_map/ppermute | solution.py:361
  45.0 3.3 %collective-permute-done.1.refs_2_ = f32[12,4,8,128]{3,2,1,0:T(8,128)S(1)} collective-permute-done((f32[12,4,8,128]{3,2,1,0:T(8,128)S(1)}, f32[12,4,8,128]{3,2,1,0:T(8,128)S(1)}, u32[]{:S(2)}, u32[]{:S(2)}) %collective-permute-start.1) | collective-permute-done | bytes 196640 | tf_op jit(solution)/shard_map/ppermute | solution.py:361
  48.2 2.5 %coefs_0.1 = (f32[30,4,4,8,128]{4,3,2,1,0:T(8,128)S(1)}, f32[4,4,8,128]{3,2,1,0:T(8,128)S(1)}) custom-call(f32[4,4,8,128]{3,2,1,0:T(8,128)S(1)} %get-tuple-element.40.refs_0_, f32[12,4,8,128]{3,2,1,0:T(8,128)S(1)} %collective-permute-done.refs_1_, f32[12,4,8,128]{3,2,1,0:T(8,128)S(1)} %collective-permute-done.1.refs_2_, ...), custom_call_target="tpu_custom_call" | custom-call | tf_op jit(solution)/shard_map/coefs_0/pallas_call | solution.py:349
  50.7 1.5 %stage_one.1 = (f32[4,4,8,128]{3,2,1,0:T(8,128)S(1)}, f32[3,4,8,128]{3,2,1,0:T(8,128)S(1)}, f32[3,4,8,128]{3,2,1,0:T(8,128)S(1)}, f32[4,4,8,128]{3,2,1,0:T(8,128)S(1)}, f32[4,4,8,128]{3,2,1,0:T(8,128)S(1)}) custom-call(f32[4,4,8,128]{3,2,1,0:T(8,128)S(1)} %get-tuple-element.39.cot_ref, f32[30,4,4,8,128]{4,3,2,1,0:T(8,128)S(1)} %get-tuple-element.44.co_ref, ...), custom_call_target="tpu_custom_call" | custom-call | tf_op jit(solution)/shard_map/stage_one/pallas_call | solution.py:349
  52.3 2.3 %collective-permute-start.2 = (f32[3,4,8,128]{3,2,1,0:T(8,128)S(1)}, f32[3,4,8,128]{3,2,1,0:T(8,128)S(1)}, u32[]{:S(2)}, u32[]{:S(2)}) collective-permute-start(f32[3,4,8,128]{3,2,1,0:T(8,128)S(1)} %get-tuple-element.48), channel_id=1, source_target_pairs={{0,64},{64,128},{128,192},{192,256},{256,320},{320,384},{384,448},... | collective-permute-start | bytes 147464 | tf_op jit(solution)/shard_map/ppermute | solution.py:361
  54.6 3.3 %collective-permute-start.3 = (f32[3,4,8,128]{3,2,1,0:T(8,128)S(1)}, f32[3,4,8,128]{3,2,1,0:T(8,128)S(1)}, u32[]{:S(2)}, u32[]{:S(2)}) collective-permute-start(f32[3,4,8,128]{3,2,1,0:T(8,128)S(1)} %get-tuple-element.49), channel_id=1, source_target_pairs={{64,0},{128,64},{192,128},{256,192},{320,256},{384,320},{448,384},... | collective-permute-start | bytes 147464 | tf_op jit(solution)/shard_map/ppermute | solution.py:361
  57.9 2.5 %coefs_1.1 = (f32[30,4,4,8,128]{4,3,2,1,0:T(8,128)S(1)}, f32[4,4,8,128]{3,2,1,0:T(8,128)S(1)}) custom-call(f32[4,4,8,128]{3,2,1,0:T(8,128)S(1)} %get-tuple-element.51.refs_0_, f32[12,4,8,128]{3,2,1,0:T(8,128)S(1)} %collective-permute-done.refs_1_, f32[12,4,8,128]{3,2,1,0:T(8,128)S(1)} %collective-permute-done.1.refs_2_, ...), custom_call_target="tpu_custom_call" | custom-call | tf_op jit(solution)/shard_map/coefs_1/pallas_call | solution.py:349
  60.5 1.5 %stage_two.1 = (f32[4,4,8,128]{3,2,1,0:T(8,128)S(1)}, f32[3,4,8,128]{3,2,1,0:T(8,128)S(1)}, f32[3,4,8,128]{3,2,1,0:T(8,128)S(1)}, f32[4,4,8,128]{3,2,1,0:T(8,128)S(1)}, f32[4,4,8,128]{3,2,1,0:T(8,128)S(1)}) custom-call(f32[4,4,8,128]{3,2,1,0:T(8,128)S(1)} %get-tuple-element.46.half_ref, f32[4,4,8,128]{3,2,1,0:T(8,128)S(1)} %get-tuple-element.47.own_in, ...), custom_call_target="tpu_custom_call" | custom-call | tf_op jit(solution)/shard_map/stage_two/pallas_call | solution.py:349
  62.1 3.0 %collective-permute-start.4 = (f32[3,4,8,128]{3,2,1,0:T(8,128)S(1)}, f32[3,4,8,128]{3,2,1,0:T(8,128)S(1)}, u32[]{:S(2)}, u32[]{:S(2)}) collective-permute-start(f32[3,4,8,128]{3,2,1,0:T(8,128)S(1)} %get-tuple-element.56), channel_id=1, source_target_pairs={{0,64},{64,128},{128,192},{192,256},{256,320},{320,384},{384,448},... | collective-permute-start | bytes 147464 | tf_op jit(solution)/shard_map/ppermute | solution.py:361
  65.1 2.6 %collective-permute-start.5 = (f32[3,4,8,128]{3,2,1,0:T(8,128)S(1)}, f32[3,4,8,128]{3,2,1,0:T(8,128)S(1)}, u32[]{:S(2)}, u32[]{:S(2)}) collective-permute-start(f32[3,4,8,128]{3,2,1,0:T(8,128)S(1)} %get-tuple-element.57), channel_id=1, source_target_pairs={{64,0},{128,64},{192,128},{256,192},{320,256},{384,320},{448,384},... | collective-permute-start | bytes 147464 | tf_op jit(solution)/shard_map/ppermute | solution.py:361
  67.7 2.5 %coefs_2.1 = (f32[30,4,4,8,128]{4,3,2,1,0:T(8,128)S(1)}, f32[4,4,8,128]{3,2,1,0:T(8,128)S(1)}) custom-call(f32[4,4,8,128]{3,2,1,0:T(8,128)S(1)} %get-tuple-element.59.refs_0_, f32[12,4,8,128]{3,2,1,0:T(8,128)S(1)} %collective-permute-done.refs_1_, f32[12,4,8,128]{3,2,1,0:T(8,128)S(1)} %collective-permute-done.1.refs_2_, ...), custom_call_target="tpu_custom_call" | custom-call | tf_op jit(solution)/shard_map/coefs_2/pallas_call | solution.py:349
  71.1 1.5 %stage_three.1 = (f32[4,4,8,128]{3,2,1,0:T(8,128)S(1)}, f32[3,4,8,128]{3,2,1,0:T(8,128)S(1)}, f32[3,4,8,128]{3,2,1,0:T(8,128)S(1)}, f32[4,4,8,128]{3,2,1,0:T(8,128)S(1)}, f32[4,4,8,128]{3,2,1,0:T(8,128)S(1)}) custom-call(f32[4,4,8,128]{3,2,1,0:T(8,128)S(1)} %get-tuple-element.46.half_ref, f32[4,4,8,128]{3,2,1,0:T(8,128)S(1)} %get-tuple-element.54.second_ref, ...), custom_call_target="tpu_custom_call" | custom-call | tf_op jit(solution)/shard_map/stage_three/pallas_call | solution.py:349
  72.6 3.9 %collective-permute-start.6 = (f32[3,4,8,128]{3,2,1,0:T(8,128)S(1)}, f32[3,4,8,128]{3,2,1,0:T(8,128)S(1)}, u32[]{:S(2)}, u32[]{:S(2)}) collective-permute-start(f32[3,4,8,128]{3,2,1,0:T(8,128)S(1)} %get-tuple-element.64), channel_id=1, source_target_pairs={{0,64},{64,128},{128,192},{192,256},{256,320},{320,384},{384,448},... | collective-permute-start | bytes 147464 | tf_op jit(solution)/shard_map/ppermute | solution.py:361
  76.5 1.9 %collective-permute-start.7 = (f32[3,4,8,128]{3,2,1,0:T(8,128)S(1)}, f32[3,4,8,128]{3,2,1,0:T(8,128)S(1)}, u32[]{:S(2)}, u32[]{:S(2)}) collective-permute-start(f32[3,4,8,128]{3,2,1,0:T(8,128)S(1)} %get-tuple-element.65), channel_id=1, source_target_pairs={{64,0},{128,64},{192,128},{256,192},{320,256},{384,320},{448,384},... | collective-permute-start | bytes 147464 | tf_op jit(solution)/shard_map/ppermute | solution.py:361
  78.5 2.5 %coefs_3.1 = (f32[30,4,4,8,128]{4,3,2,1,0:T(8,128)S(1)}, f32[4,4,8,128]{3,2,1,0:T(8,128)S(1)}) custom-call(f32[4,4,8,128]{3,2,1,0:T(8,128)S(1)} %get-tuple-element.43.refs_3_.refs_0_, f32[12,4,8,128]{3,2,1,0:T(8,128)S(1)} %collective-permute-done.refs_1_, f32[12,4,8,128]{3,2,1,0:T(8,128)S(1)} %collective-permute-done.1.refs_2_, ...), custom_call_target="tpu_custom_call" | custom-call | tf_op jit(solution)/shard_map/coefs_3/pallas_call | solution.py:349
  81.0 1.5 %collective-permute-done.7.hi_ref = f32[3,4,8,128]{3,2,1,0:T(8,128)S(1)} collective-permute-done((f32[3,4,8,128]{3,2,1,0:T(8,128)S(1)}, f32[3,4,8,128]{3,2,1,0:T(8,128)S(1)}, u32[]{:S(2)}, u32[]{:S(2)}) %collective-permute-start.7) | collective-permute-done | bytes 49184 | tf_op jit(solution)/shard_map/ppermute | solution.py:361
  82.5 2.2 %stage_four.1 = (f32[4,4,8,128]{3,2,1,0:T(8,128)S(1)}, f32[3,4,8,128]{3,2,1,0:T(8,128)S(1)}, f32[3,4,8,128]{3,2,1,0:T(8,128)S(1)}, f32[4,4,8,128]{3,2,1,0:T(8,128)}, f32[4,4,8,128]{3,2,1,0:T(8,128)S(1)}) custom-call(f32[4,4,8,128]{3,2,1,0:T(8,128)S(1)} %get-tuple-element.62.middle_ref, f32[4,4,8,128]{3,2,1,0:T(8,128)S(1)} %get-tuple-element.63.own_in, ...), custom_call_target="tpu_custom_call" | custom-call | tf_op jit(solution)/shard_map/stage_four/pallas_call | solution.py:349
  84.7 3.1 %collective-permute-start.8 = (f32[3,4,8,128]{3,2,1,0:T(8,128)S(1)}, f32[3,4,8,128]{3,2,1,0:T(8,128)S(1)}, u32[]{:S(2)}, u32[]{:S(2)}) collective-permute-start(f32[3,4,8,128]{3,2,1,0:T(8,128)S(1)} %get-tuple-element.70), channel_id=1, source_target_pairs={{0,64},{64,128},{128,192},{192,256},{256,320},{320,384},{384,448},... | collective-permute-start | bytes 147464 | tf_op jit(solution)/shard_map/ppermute | solution.py:361
  87.8 2.4 %collective-permute-start.9 = (f32[3,4,8,128]{3,2,1,0:T(8,128)S(1)}, f32[3,4,8,128]{3,2,1,0:T(8,128)S(1)}, u32[]{:S(2)}, u32[]{:S(2)}) collective-permute-start(f32[3,4,8,128]{3,2,1,0:T(8,128)S(1)} %get-tuple-element.71), channel_id=1, source_target_pairs={{64,0},{128,64},{192,128},{256,192},{320,256},{384,320},{448,384},... | collective-permute-start | bytes 147464 | tf_op jit(solution)/shard_map/ppermute | solution.py:361
  90.3 3.5 %collective-permute-done.9.hi_ref = f32[3,4,8,128]{3,2,1,0:T(8,128)S(1)} collective-permute-done((f32[3,4,8,128]{3,2,1,0:T(8,128)S(1)}, f32[3,4,8,128]{3,2,1,0:T(8,128)S(1)}, u32[]{:S(2)}, u32[]{:S(2)}) %collective-permute-start.9) | collective-permute-done | bytes 49184 | tf_op jit(solution)/shard_map/ppermute | solution.py:361
  93.8 24.8 %all_to_all.11.refs_1_ = f32[32,4,128]{2,1,0:T(4,128)S(1)} all-to-all(f32[32,4,128]{2,1,0:T(4,128)S(1)} %finish.1), channel_id=1, replica_groups=mesh['gx'=8,'gy'=4,'gz'=16] {'gy','gx'}, dimensions={0} | all-to-all | bytes 131072 | tf_op jit(solution)/shard_map/all_to_all | solution.py:403
  (20 shorter events, 6.5 us)
Async XLA Ops:
  0.0 0.8 copy-start
  0.8 0.8 copy-start.1
  1.7 0.8 copy-start.2
  2.5 0.8 copy-start.3
  3.4 0.8 copy-start.4
  37.0 8.0 %collective-permute-start = (f32[12,4,8,128]{3,2,1,0:T(8,128)S(1)}, f32[12,4,8,128]{3,2,1,0:T(8,128)S(1)}, u32[]{:S(2)}, u32[]{:S(2)}) collective-permute-start(f32[12,4,8,128]{3,2,1,0:T(8,128)S(1)} %get-tuple-element.41), channel_id=1, source_target_pairs={{0,64},{64,128},{128,192},{192,256},{256,320},{320,384},{384,448},... | collective-permute-start | bytes 589832 | tf_op jit(solution)/shard_map/ppermute | solution.py:361
  40.7 7.6 %collective-permute-start.1 = (f32[12,4,8,128]{3,2,1,0:T(8,128)S(1)}, f32[12,4,8,128]{3,2,1,0:T(8,128)S(1)}, u32[]{:S(2)}, u32[]{:S(2)}) collective-permute-start(f32[12,4,8,128]{3,2,1,0:T(8,128)S(1)} %get-tuple-element.42), channel_id=1, source_target_pairs={{64,0},{128,64},{192,128},{256,192},{320,256},{384,320},{448,384},... | collective-permute-start | bytes 589832 | tf_op jit(solution)/shard_map/ppermute | solution.py:361
  52.3 8.1 %collective-permute-start.2 = (f32[3,4,8,128]{3,2,1,0:T(8,128)S(1)}, f32[3,4,8,128]{3,2,1,0:T(8,128)S(1)}, u32[]{:S(2)}, u32[]{:S(2)}) collective-permute-start(f32[3,4,8,128]{3,2,1,0:T(8,128)S(1)} %get-tuple-element.48), channel_id=1, source_target_pairs={{0,64},{64,128},{128,192},{192,256},{256,320},{320,384},{384,448},... | collective-permute-start | bytes 147464 | tf_op jit(solution)/shard_map/ppermute | solution.py:361
  54.6 6.0 %collective-permute-start.3 = (f32[3,4,8,128]{3,2,1,0:T(8,128)S(1)}, f32[3,4,8,128]{3,2,1,0:T(8,128)S(1)}, u32[]{:S(2)}, u32[]{:S(2)}) collective-permute-start(f32[3,4,8,128]{3,2,1,0:T(8,128)S(1)} %get-tuple-element.49), channel_id=1, source_target_pairs={{64,0},{128,64},{192,128},{256,192},{320,256},{384,320},{448,384},... | collective-permute-start | bytes 147464 | tf_op jit(solution)/shard_map/ppermute | solution.py:361
  62.1 8.1 %collective-permute-start.4 = (f32[3,4,8,128]{3,2,1,0:T(8,128)S(1)}, f32[3,4,8,128]{3,2,1,0:T(8,128)S(1)}, u32[]{:S(2)}, u32[]{:S(2)}) collective-permute-start(f32[3,4,8,128]{3,2,1,0:T(8,128)S(1)} %get-tuple-element.56), channel_id=1, source_target_pairs={{0,64},{64,128},{128,192},{192,256},{256,320},{320,384},{384,448},... | collective-permute-start | bytes 147464 | tf_op jit(solution)/shard_map/ppermute | solution.py:361
  65.1 6.0 %collective-permute-start.5 = (f32[3,4,8,128]{3,2,1,0:T(8,128)S(1)}, f32[3,4,8,128]{3,2,1,0:T(8,128)S(1)}, u32[]{:S(2)}, u32[]{:S(2)}) collective-permute-start(f32[3,4,8,128]{3,2,1,0:T(8,128)S(1)} %get-tuple-element.57), channel_id=1, source_target_pairs={{64,0},{128,64},{192,128},{256,192},{320,256},{384,320},{448,384},... | collective-permute-start | bytes 147464 | tf_op jit(solution)/shard_map/ppermute | solution.py:361
  72.6 8.4 %collective-permute-start.6 = (f32[3,4,8,128]{3,2,1,0:T(8,128)S(1)}, f32[3,4,8,128]{3,2,1,0:T(8,128)S(1)}, u32[]{:S(2)}, u32[]{:S(2)}) collective-permute-start(f32[3,4,8,128]{3,2,1,0:T(8,128)S(1)} %get-tuple-element.64), channel_id=1, source_target_pairs={{0,64},{64,128},{128,192},{192,256},{256,320},{320,384},{384,448},... | collective-permute-start | bytes 147464 | tf_op jit(solution)/shard_map/ppermute | solution.py:361
  76.5 6.0 %collective-permute-start.7 = (f32[3,4,8,128]{3,2,1,0:T(8,128)S(1)}, f32[3,4,8,128]{3,2,1,0:T(8,128)S(1)}, u32[]{:S(2)}, u32[]{:S(2)}) collective-permute-start(f32[3,4,8,128]{3,2,1,0:T(8,128)S(1)} %get-tuple-element.65), channel_id=1, source_target_pairs={{64,0},{128,64},{192,128},{256,192},{320,256},{384,320},{448,384},... | collective-permute-start | bytes 147464 | tf_op jit(solution)/shard_map/ppermute | solution.py:361
  84.7 5.6 %collective-permute-start.8 = (f32[3,4,8,128]{3,2,1,0:T(8,128)S(1)}, f32[3,4,8,128]{3,2,1,0:T(8,128)S(1)}, u32[]{:S(2)}, u32[]{:S(2)}) collective-permute-start(f32[3,4,8,128]{3,2,1,0:T(8,128)S(1)} %get-tuple-element.70), channel_id=1, source_target_pairs={{0,64},{64,128},{128,192},{192,256},{256,320},{320,384},{384,448},... | collective-permute-start | bytes 147464 | tf_op jit(solution)/shard_map/ppermute | solution.py:361
  87.8 6.0 %collective-permute-start.9 = (f32[3,4,8,128]{3,2,1,0:T(8,128)S(1)}, f32[3,4,8,128]{3,2,1,0:T(8,128)S(1)}, u32[]{:S(2)}, u32[]{:S(2)}) collective-permute-start(f32[3,4,8,128]{3,2,1,0:T(8,128)S(1)} %get-tuple-element.71), channel_id=1, source_target_pairs={{64,0},{128,64},{192,128},{256,192},{320,256},{384,320},{448,384},... | collective-permute-start | bytes 147464 | tf_op jit(solution)/shard_map/ppermute | solution.py:361

commit v3 on v2

--- a/solution.py
+++ b/solution.py
@@ -8,6 +8,7 @@
 TAU = 0.3
 WENO_EPS = 1e-06
 SMOOTH_EPS = 0.01
+UNROLL = 1
 LANES = 128
 BX, BY = 8, 16
 F32 = jnp.float32
@@ -110,33 +111,34 @@
 PER_AXIS = 10
 
 
-def coef_kernel(section, f_ref, lo_ref, hi_ref, phi_ref, co_ref, pc_ref):
-    fref = f_ref
-
-    def keep(axis, z, minus_plus, jac_m, jac_p):
-        for n, part in enumerate(minus_plus + jac_m + jac_p):
-            co_ref[PER_AXIS * axis + n, z] = part
-
+def side_of(phi):
+    return jnp.where(phi > 0, 1.0, -1.0).astype(F32)
+
+
+def coef_plane_kernel(f_ref, phi_ref, co_ref, sum_ref):
     def plane(z, carry):
-        f = fref[z]
-        side = jnp.where(phi_ref[z] > 0, 1.0, -1.0).astype(F32)
+        f = f_ref[z]
+        side = side_of(phi_ref[z])
         total = None
         for axis, shift in ((0, shift_x), (1, shift_y)):
             b = f - shift(f, -1)
             d = b - shift(b, -1)
             minus, plus, jac_m, jac_p = weno_center(b, shift(d, -1), d, shift(d, 1), shift(d, 2))
             term, by_minus, by_plus = upwind_term(minus, shift(plus, 1), side)
-            keep(axis, z, (by_minus, by_plus), jac_m, jac_p)
+            for n, part in enumerate((by_minus, by_plus) + jac_m + jac_p):
+                co_ref[PER_AXIS * axis + n, z] = part
             total = term if total is None else total + term
-        pc_ref[z] = total
+        sum_ref[z] = total
         return carry
 
     lax.fori_loop(0, 4, plane, 0)
 
+
+def coef_depth_kernel(section, f_ref, lo_ref, hi_ref, phi_ref, sum_ref, co_ref, scale_ref, pc_ref):
     def column(g, carry):
         f = (
             [lo_ref[3 * section + i, g] for i in range(3)]
-            + [fref[i, g] for i in range(4)]
+            + [f_ref[i, g] for i in range(4)]
             + [hi_ref[3 * section + i, g] for i in range(3)]
         )
         b = [None] + [f[i] - f[i - 1] for i in range(1, 10)]
@@ -144,32 +146,26 @@
         centers = [weno_center(b[m + 3], d[m + 2], d[m + 3], d[m + 4], d[m + 5]) for m in range(5)]
         for z in range(4):
             phi = phi_ref[z, g]
-            side = jnp.where(phi > 0, 1.0, -1.0).astype(F32)
-            term, by_minus, by_plus = upwind_term(centers[z][0], centers[z + 1][1], side)
-            square = phi * phi + 1.0
-            root = lax.rsqrt(square)
-            ham2 = pc_ref[z, g] + term
-            inv = lax.rsqrt(ham2)
-            ham = ham2 * inv
-            scale = (-0.25 * TAU) * ((phi * root) * inv)
-            pc_ref[z, g] = (-TAU) * ((root * root * root) * (ham - 1.0))
-            for axis in (0, 1):
-                for n in (0, 1):
-                    co_ref[PER_AXIS * axis + n, z, g] = co_ref[PER_AXIS * axis + n, z, g] * scale
-            parts = (by_minus * scale, by_plus * scale) + centers[z][2] + centers[z + 1][3]
+            term, by_minus, by_plus = upwind_term(centers[z][0], centers[z + 1][1], side_of(phi))
+            root = lax.rsqrt(phi * phi + 1.0)
+            square = sum_ref[z, g] + term
+            inv = lax.rsqrt(square)
+            scale_ref[z, g] = (-0.25 * TAU) * ((phi * root) * inv)
+            pc_ref[z, g] = (-TAU) * ((root * root * root) * (square * inv - 1.0))
+            parts = (by_minus, by_plus) + centers[z][2] + centers[z + 1][3]
             for n, part in enumerate(parts):
-                co_ref[PER_AXIS * 2 + n, z, g] = part
+                co_ref[n, z, g] = part
         return carry
 
     lax.fori_loop(0, 4, column, 0)
 
 
-def apply_local(c_ref, co_ref, out_ref, up_ref, dn_ref):
+def apply_local(c_ref, cxy_ref, cz_ref, scale_ref, out_ref, up_ref, dn_ref):
     def plane(z, carry):
-        c = c_ref[z]
+        c = c_ref[z] * scale_ref[z]
         total = None
         for axis, shift in ((0, shift_x), (1, shift_y)):
-            co = lambda n: co_ref[PER_AXIS * axis + n, z]
+            co = lambda n: cxy_ref[PER_AXIS * axis + n, z]
             a = c * co(0)
             g = shift(c * co(1), -1)
             t = [a * co(2 + k) + g * co(6 + k) for k in range(4)]
@@ -180,7 +176,7 @@
         out_ref[z] = total
         return carry
 
-    lax.fori_loop(0, 4, plane, 0)
+    lax.fori_loop(0, 4, plane, 0, unroll=UNROLL)
 
     def column(g, carry):
         dbar = [None] * 8
@@ -190,8 +186,8 @@
             into[at] = value if into[at] is None else into[at] + value
 
         for z in range(4):
-            c = c_ref[z, g]
-            co = lambda n: co_ref[PER_AXIS * 2 + n, z, g]
+            c = c_ref[z, g] * scale_ref[z, g]
+            co = lambda n: cz_ref[n, z, g]
             a, p = c * co(0), c * co(1)
             for k in range(4):
                 add(dbar, z + k, a * co(2 + k))
@@ -208,7 +204,7 @@
             dn_ref[k, g] = bbar[k]
         return carry
 
-    lax.fori_loop(0, 4, column, 0)
+    lax.fori_loop(0, 4, column, 0, unroll=UNROLL)
 
 
 def joined(own_ref, lo_ref, hi_ref):
@@ -222,35 +218,35 @@
     )
 
 
-def stage_one(cot_ref, co_ref, pc_ref, own_ref, up_ref, dn_ref, c_ref, acc_ref):
+def stage_one(cot_ref, cxy_ref, cz_ref, scale_ref, pc_ref, own_ref, up_ref, dn_ref, c_ref, acc_ref):
     half = 0.5 * cot_ref[...]
     c_ref[...] = half
     acc_ref[...] = pc_ref[...] * half
-    apply_local(c_ref, co_ref, own_ref, up_ref, dn_ref)
-
-
-def stage_two(half_ref, own_in, lo_ref, hi_ref, acc_in, co_ref, pc_ref, own_ref, up_ref, dn_ref, c_ref, acc_ref):
+    apply_local(c_ref, cxy_ref, cz_ref, scale_ref, own_ref, up_ref, dn_ref)
+
+
+def stage_two(half_ref, own_in, lo_ref, hi_ref, acc_in, cxy_ref, cz_ref, scale_ref, pc_ref, own_ref, up_ref, dn_ref, c_ref, acc_ref):
     for z, back in enumerate(joined(own_in, lo_ref, hi_ref)):
         c = half_ref[z] + back
         c_ref[z] = c
         acc_ref[z] = acc_in[z] + pc_ref[z] * c
-    apply_local(c_ref, co_ref, own_ref, up_ref, dn_ref)
-
-
-def stage_three(half_ref, second_ref, own_in, lo_ref, hi_ref, acc_in, co_ref, pc_ref, own_ref, up_ref, dn_ref, c_ref, acc_ref):
+    apply_local(c_ref, cxy_ref, cz_ref, scale_ref, own_ref, up_ref, dn_ref)
+
+
+def stage_three(half_ref, second_ref, own_in, lo_ref, hi_ref, acc_in, cxy_ref, cz_ref, scale_ref, pc_ref, own_ref, up_ref, dn_ref, c_ref, acc_ref):
     for z, back in enumerate(joined(own_in, lo_ref, hi_ref)):
         c = 0.5 * (half_ref[z] + second_ref[z] + back)
         c_ref[z] = c
         acc_ref[z] = acc_in[z] + pc_ref[z] * c
-    apply_local(c_ref, co_ref, own_ref, up_ref, dn_ref)
-
-
-def stage_four(middle_ref, own_in, lo_ref, hi_ref, acc_in, co_ref, pc_ref, own_ref, up_ref, dn_ref, c_ref, acc_ref):
+    apply_local(c_ref, cxy_ref, cz_ref, scale_ref, own_ref, up_ref, dn_ref)
+
+
+def stage_four(middle_ref, own_in, lo_ref, hi_ref, acc_in, cxy_ref, cz_ref, scale_ref, pc_ref, own_ref, up_ref, dn_ref, c_ref, acc_ref):
     for z, back in enumerate(joined(own_in, lo_ref, hi_ref)):
         c = middle_ref[z] + back
         c_ref[z] = c
         acc_ref[z] = acc_in[z] + pc_ref[z] * c + (middle_ref[z] + c)
-    apply_local(c_ref, co_ref, own_ref, up_ref, dn_ref)
+    apply_local(c_ref, cxy_ref, cz_ref, scale_ref, own_ref, up_ref, dn_ref)
 
 
 def finish(own_in, lo_ref, hi_ref, acc_in, out_ref):
@@ -342,10 +338,9 @@
 
     def call(kernel, out_shape, *args, first=vmem, scratch=(), name=None, far=False):
         many = isinstance(out_shape, list)
-        if not (far or interpret):
-            args = [
-                x if x.ndim == 1 else pltpu.with_memory_space_constraint(x, pltpu.VMEM) for x in args
-            ]
+        if not interpret:
+            space = pltpu.HBM if far else pltpu.VMEM
+            args = [x if x.ndim == 1 else pltpu.with_memory_space_constraint(x, space) for x in args]
         return pl.pallas_call(
             kernel,
             out_shape=out_shape,
@@ -379,25 +374,37 @@
         phi, cot = fields[3], fields[4]
         rim_lo, rim_hi = exchange(rim_up, rim_dn)
 
+        def coef_plane(n):
+            return call(
+                coef_plane_kernel, [near(2 * PER_AXIS, *slab), near(*slab)],
+                fields[n], phi, name=f"coef_plane_{n}",
+            )
+
+        def coef_depth(n, total):
+            return call(
+                lambda *refs: coef_depth_kernel(n, *refs),
+                [near(PER_AXIS, *slab), near(*slab), near(*slab)],
+                fields[n], rim_lo, rim_hi, phi, total, name=f"coef_depth_{n}",
+            )
+
         def coefs(n):
-            return call(
-                lambda *refs: coef_kernel(n, *refs),
-                [near(3 * PER_AXIS, *slab), near(*slab)],
-                fields[n], rim_lo, rim_hi, phi, name=f"coefs_{n}",
-            )
+            flat, total = coef_plane(n)
+            return (flat, *coef_depth(n, total))
 
         results = [near(*slab), near(*rim), near(*rim), near(*slab), near(*slab)]
-        co, pc = coefs(0)
-        own, up, dn, half, acc = call(stage_one, results, cot, co, pc, name="stage_one")
+        own, up, dn, half, acc = call(stage_one, results, cot, *coefs(0), name="stage_one")
         lo, hi = exchange(up, dn)
-        co, pc = coefs(1)
-        own, up, dn, second, acc = call(stage_two, results, half, own, lo, hi, acc, co, pc, name="stage_two")
+        own, up, dn, second, acc = call(
+            stage_two, results, half, own, lo, hi, acc, *coefs(1), name="stage_two"
+        )
         lo, hi = exchange(up, dn)
-        co, pc = coefs(2)
-        own, up, dn, middle, acc = call(stage_three, results, half, second, own, lo, hi, acc, co, pc, name="stage_three")
+        own, up, dn, middle, acc = call(
+            stage_three, results, half, second, own, lo, hi, acc, *coefs(2), name="stage_three"
+        )
         lo, hi = exchange(up, dn)
-        co, pc = coefs(3)
-        own, up, dn, _, acc = call(stage_four, results, middle, own, lo, hi, acc, co, pc, name="stage_four")
+        own, up, dn, _, acc = call(
+            stage_four, results, middle, own, lo, hi, acc, *coefs(3), name="stage_four"
+        )
         lo, hi = exchange(up, dn)
         slabs = call(finish, near(count, depth, LANES), own, lo, hi, acc, name="finish")
         slabs = lax.all_to_all(slabs, ("gy", "gx"), 0, 0)

time: 121 us -> 115 us (0.950)
  local copies, waits for them, and re-layouts: 4.19 us -> 0 us
  waiting for transfers between devices: 11.8 us -> 9.86 us
    unnamed x10 -> x0, local copies, waits for them, and re-layouts: 4.19 us -> none
    ppermute x5, waiting for transfers between devices: 2.36 us -> 0.41 us  [exchange(): lax.ppermute(up, everywhere, upward)]
    pallas_call x12 -> x16, Pallas kernels: 18 us -> 19 us  [call(): pl.pallas_call(kernel, out_shape=out_shape, in_specs=[first] + [vmem] * (...]
  transfers between devices with their start and end apart: 10 -> 10, of which waited for: 6 -> 6; matrix products, arithmetic and copies ran while one was open for 0% -> 0% of each run, Pallas kernels for 6% -> 8%
where the time goes in v3:
time: 115 us; the launch traced here: 114 us
  blocking collectives  57.2 us (50%)
  starting transfers between devices  28.1 us (24%)
  Pallas kernels  19 us (17%)
  waiting for transfers between devices  9.86 us (9%)
    all_to_all x1, blocking collectives, shards(): packed = lax.all_to_all(packed, ('gy', 'gx'), 0, 0)  32.4 us
    all_to_all x1, blocking collectives, shards(): slabs = lax.all_to_all(slabs, ('gy', 'gx'), 0, 0)  24.8 us
    pallas_call x16, Pallas kernels, call(): pl.pallas_call(kernel, out_shape=out_shape, in_specs=[first] + [vmem] * (...  19 us
    ppermute x5, starting transfers between devices, exchange(): lax.ppermute(up, everywhere, upward)  16 us
    ppermute x5, starting transfers between devices, exchange(): lax.ppermute(dn, everywhere, downward)  12.1 us
    ppermute x5, waiting for transfers between devices, exchange(): lax.ppermute(dn, everywhere, downward)  9.45 us
  transfers between devices with their start and end apart: 10, of which 6 were waited for; matrix products, arithmetic and copies ran while one was open for 0% of the time, Pallas kernels for 8%

profile of v3, /device:TPU:6, one launch (start us, length us, event | category | flops | bytes accessed | tf_op | source)
XLA Modules:
  0.0 114.3 jit_solution(17467034806752921704)
XLA Ops:
  0.0 1.2 %to_slabs.1 = f32[32,20,128]{2,1,0:T(8,128)S(1)} custom-call(s32[1]{0:T(128)} %bitcast.refs_0_, f32[8,16,128]{2,1,0:T(8,128)} %refs_1_.1, f32[8,16,128]{2,1,0:T(8,128)} %refs_2_.1, f32[8,16,128]{2,1,0:T(8,128)} %refs_3_.1, f32[8,16,128]{2,1,0:T(8,128)} %refs_4_.1, f32[8,16,128]{2,1,0:T(8,128)} %refs_5_.1), custom_call_target="tpu_custom_call" | custom-call | tf_op jit(solution)/shard_map/to_slabs/pallas_call | solution.py:344
  1.2 32.4 %all_to_all.10.refs_0_ = f32[32,20,128]{2,1,0:T(8,128)S(1)} all-to-all(f32[32,20,128]{2,1,0:T(8,128)S(1)} %to_slabs.1), channel_id=1, replica_groups=mesh['gx'=8,'gy'=4,'gz'=16] {'gy','gx'}, dimensions={0} | all-to-all | bytes 655360 | tf_op jit(solution)/shard_map/all_to_all | solution.py:368
  33.8 3.7 %collective-permute-start = (f32[12,4,8,128]{3,2,1,0:T(8,128)S(1)}, f32[12,4,8,128]{3,2,1,0:T(8,128)S(1)}, u32[]{:S(2)}, u32[]{:S(2)}) collective-permute-start(f32[12,4,8,128]{3,2,1,0:T(8,128)S(1)} %get-tuple-element.55), channel_id=1, source_target_pairs={{0,64},{64,128},{128,192},{192,256},{256,320},{320,384},{384,448},... | collective-permute-start | bytes 589832 | tf_op jit(solution)/shard_map/ppermute | solution.py:356
  37.4 1.9 %collective-permute-start.1 = (f32[12,4,8,128]{3,2,1,0:T(8,128)S(1)}, f32[12,4,8,128]{3,2,1,0:T(8,128)S(1)}, u32[]{:S(2)}, u32[]{:S(2)}) collective-permute-start(f32[12,4,8,128]{3,2,1,0:T(8,128)S(1)} %get-tuple-element.56), channel_id=1, source_target_pairs={{64,0},{128,64},{192,128},{256,192},{320,256},{384,320},{448,384},... | collective-permute-start | bytes 589832 | tf_op jit(solution)/shard_map/ppermute | solution.py:356
  39.4 1.9 %coef_plane_0.1 = (f32[20,4,4,8,128]{4,3,2,1,0:T(8,128)S(1)}, f32[4,4,8,128]{3,2,1,0:T(8,128)S(1)}) custom-call(f32[4,4,8,128]{3,2,1,0:T(8,128)S(1)} %get-tuple-element.52.f_ref.refs_0_, f32[4,4,8,128]{3,2,1,0:T(8,128)S(1)} %get-tuple-element.53.phi_ref.refs_3_.f_ref.refs_0_), custom_call_target="tpu_custom_call" | custom-call | tf_op jit(solution)/shard_map/coef_plane_0/pallas_call | solution.py:344
  41.7 3.3 %collective-permute-done.1.refs_2_ = f32[12,4,8,128]{3,2,1,0:T(8,128)S(1)} collective-permute-done((f32[12,4,8,128]{3,2,1,0:T(8,128)S(1)}, f32[12,4,8,128]{3,2,1,0:T(8,128)S(1)}, u32[]{:S(2)}, u32[]{:S(2)}) %collective-permute-start.1) | collective-permute-done | bytes 196640 | tf_op jit(solution)/shard_map/ppermute | solution.py:356
  45.5 1.5 %stage_one.1 = (f32[4,4,8,128]{3,2,1,0:T(8,128)S(1)}, f32[3,4,8,128]{3,2,1,0:T(8,128)S(1)}, f32[3,4,8,128]{3,2,1,0:T(8,128)S(1)}, f32[4,4,8,128]{3,2,1,0:T(8,128)S(1)}, f32[4,4,8,128]{3,2,1,0:T(8,128)S(1)}) custom-call(f32[4,4,8,128]{3,2,1,0:T(8,128)S(1)} %get-tuple-element.51.cot_ref, f32[20,4,4,8,128]{4,3,2,1,0:T(8,128)S(1)} %get-tuple-element.54.cxy_ref, ...), custom_call_target="tpu_custom_call" | custom-call | tf_op jit(solution)/shard_map/stage_one/pallas_call | solution.py:344
  47.1 2.3 %collective-permute-start.2 = (f32[3,4,8,128]{3,2,1,0:T(8,128)S(1)}, f32[3,4,8,128]{3,2,1,0:T(8,128)S(1)}, u32[]{:S(2)}, u32[]{:S(2)}) collective-permute-start(f32[3,4,8,128]{3,2,1,0:T(8,128)S(1)} %get-tuple-element.63), channel_id=1, source_target_pairs={{0,64},{64,128},{128,192},{192,256},{256,320},{320,384},{384,448},... | collective-permute-start | bytes 147464 | tf_op jit(solution)/shard_map/ppermute | solution.py:356
  49.4 3.3 %collective-permute-start.3 = (f32[3,4,8,128]{3,2,1,0:T(8,128)S(1)}, f32[3,4,8,128]{3,2,1,0:T(8,128)S(1)}, u32[]{:S(2)}, u32[]{:S(2)}) collective-permute-start(f32[3,4,8,128]{3,2,1,0:T(8,128)S(1)} %get-tuple-element.64), channel_id=1, source_target_pairs={{64,0},{128,64},{192,128},{256,192},{320,256},{384,320},{448,384},... | collective-permute-start | bytes 147464 | tf_op jit(solution)/shard_map/ppermute | solution.py:356
  52.7 1.9 %coef_plane_1.1 = (f32[20,4,4,8,128]{4,3,2,1,0:T(8,128)S(1)}, f32[4,4,8,128]{3,2,1,0:T(8,128)S(1)}) custom-call(f32[4,4,8,128]{3,2,1,0:T(8,128)S(1)} %get-tuple-element.66.f_ref.refs_0_, f32[4,4,8,128]{3,2,1,0:T(8,128)S(1)} %get-tuple-element.53.phi_ref.refs_3_.f_ref.refs_0_), custom_call_target="tpu_custom_call" | custom-call | tf_op jit(solution)/shard_map/coef_plane_1/pallas_call | solution.py:344
  55.4 1.5 %stage_two.1 = (f32[4,4,8,128]{3,2,1,0:T(8,128)S(1)}, f32[3,4,8,128]{3,2,1,0:T(8,128)S(1)}, f32[3,4,8,128]{3,2,1,0:T(8,128)S(1)}, f32[4,4,8,128]{3,2,1,0:T(8,128)S(1)}, f32[4,4,8,128]{3,2,1,0:T(8,128)S(1)}) custom-call(f32[4,4,8,128]{3,2,1,0:T(8,128)S(1)} %get-tuple-element.61.half_ref, f32[4,4,8,128]{3,2,1,0:T(8,128)S(1)} %get-tuple-element.62.own_in, ...), custom_call_target="tpu_custom_call" | custom-call | tf_op jit(solution)/shard_map/stage_two/pallas_call | solution.py:344
  56.9 3.0 %collective-permute-start.4 = (f32[3,4,8,128]{3,2,1,0:T(8,128)S(1)}, f32[3,4,8,128]{3,2,1,0:T(8,128)S(1)}, u32[]{:S(2)}, u32[]{:S(2)}) collective-permute-start(f32[3,4,8,128]{3,2,1,0:T(8,128)S(1)} %get-tuple-element.74), channel_id=1, source_target_pairs={{0,64},{64,128},{128,192},{192,256},{256,320},{320,384},{384,448},... | collective-permute-start | bytes 147464 | tf_op jit(solution)/shard_map/ppermute | solution.py:356
  59.9 2.6 %collective-permute-start.5 = (f32[3,4,8,128]{3,2,1,0:T(8,128)S(1)}, f32[3,4,8,128]{3,2,1,0:T(8,128)S(1)}, u32[]{:S(2)}, u32[]{:S(2)}) collective-permute-start(f32[3,4,8,128]{3,2,1,0:T(8,128)S(1)} %get-tuple-element.75), channel_id=1, source_target_pairs={{64,0},{128,64},{192,128},{256,192},{320,256},{384,320},{448,384},... | collective-permute-start | bytes 147464 | tf_op jit(solution)/shard_map/ppermute | solution.py:356
  62.5 1.9 %coef_plane_2.1 = (f32[20,4,4,8,128]{4,3,2,1,0:T(8,128)S(1)}, f32[4,4,8,128]{3,2,1,0:T(8,128)S(1)}) custom-call(f32[4,4,8,128]{3,2,1,0:T(8,128)S(1)} %get-tuple-element.77.f_ref.refs_0_, f32[4,4,8,128]{3,2,1,0:T(8,128)S(1)} %get-tuple-element.53.phi_ref.refs_3_.f_ref.refs_0_), custom_call_target="tpu_custom_call" | custom-call | tf_op jit(solution)/shard_map/coef_plane_2/pallas_call | solution.py:344
  65.9 1.5 %stage_three.1 = (f32[4,4,8,128]{3,2,1,0:T(8,128)S(1)}, f32[3,4,8,128]{3,2,1,0:T(8,128)S(1)}, f32[3,4,8,128]{3,2,1,0:T(8,128)S(1)}, f32[4,4,8,128]{3,2,1,0:T(8,128)S(1)}, f32[4,4,8,128]{3,2,1,0:T(8,128)S(1)}) custom-call(f32[4,4,8,128]{3,2,1,0:T(8,128)S(1)} %get-tuple-element.61.half_ref, f32[4,4,8,128]{3,2,1,0:T(8,128)S(1)} %get-tuple-element.72.second_ref, ...), custom_call_target="tpu_custom_call" | custom-call | tf_op jit(solution)/shard_map/stage_three/pallas_call | solution.py:344
  67.4 3.9 %collective-permute-start.6 = (f32[3,4,8,128]{3,2,1,0:T(8,128)S(1)}, f32[3,4,8,128]{3,2,1,0:T(8,128)S(1)}, u32[]{:S(2)}, u32[]{:S(2)}) collective-permute-start(f32[3,4,8,128]{3,2,1,0:T(8,128)S(1)} %get-tuple-element.85), channel_id=1, source_target_pairs={{0,64},{64,128},{128,192},{192,256},{256,320},{320,384},{384,448},... | collective-permute-start | bytes 147464 | tf_op jit(solution)/shard_map/ppermute | solution.py:356
  71.4 1.9 %collective-permute-start.7 = (f32[3,4,8,128]{3,2,1,0:T(8,128)S(1)}, f32[3,4,8,128]{3,2,1,0:T(8,128)S(1)}, u32[]{:S(2)}, u32[]{:S(2)}) collective-permute-start(f32[3,4,8,128]{3,2,1,0:T(8,128)S(1)} %get-tuple-element.86), channel_id=1, source_target_pairs={{64,0},{128,64},{192,128},{256,192},{320,256},{384,320},{448,384},... | collective-permute-start | bytes 147464 | tf_op jit(solution)/shard_map/ppermute | solution.py:356
  73.3 1.9 %coef_plane_3.1 = (f32[20,4,4,8,128]{4,3,2,1,0:T(8,128)S(1)}, f32[4,4,8,128]{3,2,1,0:T(8,128)S(1)}) custom-call(f32[4,4,8,128]{3,2,1,0:T(8,128)S(1)} %get-tuple-element.53.phi_ref.refs_3_.f_ref.refs_0_, f32[4,4,8,128]{3,2,1,0:T(8,128)S(1)} %get-tuple-element.53.phi_ref.refs_3_.f_ref.refs_0_), custom_call_target="tpu_custom_call" | custom-call | tf_op jit(solution)/shard_map/coef_plane_3/pallas_call | solution.py:344
  75.8 1.6 %collective-permute-done.7.hi_ref = f32[3,4,8,128]{3,2,1,0:T(8,128)S(1)} collective-permute-done((f32[3,4,8,128]{3,2,1,0:T(8,128)S(1)}, f32[3,4,8,128]{3,2,1,0:T(8,128)S(1)}, u32[]{:S(2)}, u32[]{:S(2)}) %collective-permute-start.7) | collective-permute-done | bytes 49184 | tf_op jit(solution)/shard_map/ppermute | solution.py:356
  77.4 2.2 %stage_four.1 = (f32[4,4,8,128]{3,2,1,0:T(8,128)S(1)}, f32[3,4,8,128]{3,2,1,0:T(8,128)S(1)}, f32[3,4,8,128]{3,2,1,0:T(8,128)S(1)}, f32[4,4,8,128]{3,2,1,0:T(8,128)}, f32[4,4,8,128]{3,2,1,0:T(8,128)S(1)}) custom-call(f32[4,4,8,128]{3,2,1,0:T(8,128)S(1)} %get-tuple-element.83.middle_ref, f32[4,4,8,128]{3,2,1,0:T(8,128)S(1)} %get-tuple-element.84.own_in, ...), custom_call_target="tpu_custom_call" | custom-call | tf_op jit(solution)/shard_map/stage_four/pallas_call | solution.py:344
  79.5 3.1 %collective-permute-start.8 = (f32[3,4,8,128]{3,2,1,0:T(8,128)S(1)}, f32[3,4,8,128]{3,2,1,0:T(8,128)S(1)}, u32[]{:S(2)}, u32[]{:S(2)}) collective-permute-start(f32[3,4,8,128]{3,2,1,0:T(8,128)S(1)} %get-tuple-element.94), channel_id=1, source_target_pairs={{0,64},{64,128},{128,192},{192,256},{256,320},{320,384},{384,448},... | collective-permute-start | bytes 147464 | tf_op jit(solution)/shard_map/ppermute | solution.py:356
  82.7 2.4 %collective-permute-start.9 = (f32[3,4,8,128]{3,2,1,0:T(8,128)S(1)}, f32[3,4,8,128]{3,2,1,0:T(8,128)S(1)}, u32[]{:S(2)}, u32[]{:S(2)}) collective-permute-start(f32[3,4,8,128]{3,2,1,0:T(8,128)S(1)} %get-tuple-element.95), channel_id=1, source_target_pairs={{64,0},{128,64},{192,128},{256,192},{320,256},{384,320},{448,384},... | collective-permute-start | bytes 147464 | tf_op jit(solution)/shard_map/ppermute | solution.py:356
  85.1 3.5 %collective-permute-done.9.hi_ref = f32[3,4,8,128]{3,2,1,0:T(8,128)S(1)} collective-permute-done((f32[3,4,8,128]{3,2,1,0:T(8,128)S(1)}, f32[3,4,8,128]{3,2,1,0:T(8,128)S(1)}, u32[]{:S(2)}, u32[]{:S(2)}) %collective-permute-start.9) | collective-permute-done | bytes 49184 | tf_op jit(solution)/shard_map/ppermute | solution.py:356
  88.7 24.8 %all_to_all.11.refs_1_ = f32[32,4,128]{2,1,0:T(4,128)S(1)} all-to-all(f32[32,4,128]{2,1,0:T(4,128)S(1)} %finish.1), channel_id=1, replica_groups=mesh['gx'=8,'gy'=4,'gz'=16] {'gy','gx'}, dimensions={0} | all-to-all | bytes 131072 | tf_op jit(solution)/shard_map/all_to_all | solution.py:410
  (14 shorter events, 4.7 us)
Async XLA Ops:
  33.8 8.0 %collective-permute-start = (f32[12,4,8,128]{3,2,1,0:T(8,128)S(1)}, f32[12,4,8,128]{3,2,1,0:T(8,128)S(1)}, u32[]{:S(2)}, u32[]{:S(2)}) collective-permute-start(f32[12,4,8,128]{3,2,1,0:T(8,128)S(1)} %get-tuple-element.55), channel_id=1, source_target_pairs={{0,64},{64,128},{128,192},{192,256},{256,320},{320,384},{384,448},... | collective-permute-start | bytes 589832 | tf_op jit(solution)/shard_map/ppermute | solution.py:356
  37.4 7.6 %collective-permute-start.1 = (f32[12,4,8,128]{3,2,1,0:T(8,128)S(1)}, f32[12,4,8,128]{3,2,1,0:T(8,128)S(1)}, u32[]{:S(2)}, u32[]{:S(2)}) collective-permute-start(f32[12,4,8,128]{3,2,1,0:T(8,128)S(1)} %get-tuple-element.56), channel_id=1, source_target_pairs={{64,0},{128,64},{192,128},{256,192},{320,256},{384,320},{448,384},... | collective-permute-start | bytes 589832 | tf_op jit(solution)/shard_map/ppermute | solution.py:356
  47.1 8.1 %collective-permute-start.2 = (f32[3,4,8,128]{3,2,1,0:T(8,128)S(1)}, f32[3,4,8,128]{3,2,1,0:T(8,128)S(1)}, u32[]{:S(2)}, u32[]{:S(2)}) collective-permute-start(f32[3,4,8,128]{3,2,1,0:T(8,128)S(1)} %get-tuple-element.63), channel_id=1, source_target_pairs={{0,64},{64,128},{128,192},{192,256},{256,320},{320,384},{384,448},... | collective-permute-start | bytes 147464 | tf_op jit(solution)/shard_map/ppermute | solution.py:356
  49.4 6.0 %collective-permute-start.3 = (f32[3,4,8,128]{3,2,1,0:T(8,128)S(1)}, f32[3,4,8,128]{3,2,1,0:T(8,128)S(1)}, u32[]{:S(2)}, u32[]{:S(2)}) collective-permute-start(f32[3,4,8,128]{3,2,1,0:T(8,128)S(1)} %get-tuple-element.64), channel_id=1, source_target_pairs={{64,0},{128,64},{192,128},{256,192},{320,256},{384,320},{448,384},... | collective-permute-start | bytes 147464 | tf_op jit(solution)/shard_map/ppermute | solution.py:356
  56.9 8.1 %collective-permute-start.4 = (f32[3,4,8,128]{3,2,1,0:T(8,128)S(1)}, f32[3,4,8,128]{3,2,1,0:T(8,128)S(1)}, u32[]{:S(2)}, u32[]{:S(2)}) collective-permute-start(f32[3,4,8,128]{3,2,1,0:T(8,128)S(1)} %get-tuple-element.74), channel_id=1, source_target_pairs={{0,64},{64,128},{128,192},{192,256},{256,320},{320,384},{384,448},... | collective-permute-start | bytes 147464 | tf_op jit(solution)/shard_map/ppermute | solution.py:356
  59.9 6.0 %collective-permute-start.5 = (f32[3,4,8,128]{3,2,1,0:T(8,128)S(1)}, f32[3,4,8,128]{3,2,1,0:T(8,128)S(1)}, u32[]{:S(2)}, u32[]{:S(2)}) collective-permute-start(f32[3,4,8,128]{3,2,1,0:T(8,128)S(1)} %get-tuple-element.75), channel_id=1, source_target_pairs={{64,0},{128,64},{192,128},{256,192},{320,256},{384,320},{448,384},... | collective-permute-start | bytes 147464 | tf_op jit(solution)/shard_map/ppermute | solution.py:356
  67.4 8.4 %collective-permute-start.6 = (f32[3,4,8,128]{3,2,1,0:T(8,128)S(1)}, f32[3,4,8,128]{3,2,1,0:T(8,128)S(1)}, u32[]{:S(2)}, u32[]{:S(2)}) collective-permute-start(f32[3,4,8,128]{3,2,1,0:T(8,128)S(1)} %get-tuple-element.85), channel_id=1, source_target_pairs={{0,64},{64,128},{128,192},{192,256},{256,320},{320,384},{384,448},... | collective-permute-start | bytes 147464 | tf_op jit(solution)/shard_map/ppermute | solution.py:356
  71.4 6.0 %collective-permute-start.7 = (f32[3,4,8,128]{3,2,1,0:T(8,128)S(1)}, f32[3,4,8,128]{3,2,1,0:T(8,128)S(1)}, u32[]{:S(2)}, u32[]{:S(2)}) collective-permute-start(f32[3,4,8,128]{3,2,1,0:T(8,128)S(1)} %get-tuple-element.86), channel_id=1, source_target_pairs={{64,0},{128,64},{192,128},{256,192},{320,256},{384,320},{448,384},... | collective-permute-start | bytes 147464 | tf_op jit(solution)/shard_map/ppermute | solution.py:356
  79.5 5.6 %collective-permute-start.8 = (f32[3,4,8,128]{3,2,1,0:T(8,128)S(1)}, f32[3,4,8,128]{3,2,1,0:T(8,128)S(1)}, u32[]{:S(2)}, u32[]{:S(2)}) collective-permute-start(f32[3,4,8,128]{3,2,1,0:T(8,128)S(1)} %get-tuple-element.94), channel_id=1, source_target_pairs={{0,64},{64,128},{128,192},{192,256},{256,320},{320,384},{384,448},... | collective-permute-start | bytes 147464 | tf_op jit(solution)/shard_map/ppermute | solution.py:356
  82.7 6.0 %collective-permute-start.9 = (f32[3,4,8,128]{3,2,1,0:T(8,128)S(1)}, f32[3,4,8,128]{3,2,1,0:T(8,128)S(1)}, u32[]{:S(2)}, u32[]{:S(2)}) collective-permute-start(f32[3,4,8,128]{3,2,1,0:T(8,128)S(1)} %get-tuple-element.95), channel_id=1, source_target_pairs={{64,0},{128,64},{192,128},{256,192},{320,256},{384,320},{448,384},... | collective-permute-start | bytes 147464 | tf_op jit(solution)/shard_map/ppermute | solution.py:356

commit v4 on v3

--- a/solution.py
+++ b/solution.py
@@ -8,7 +8,9 @@
 TAU = 0.3
 WENO_EPS = 1e-06
 SMOOTH_EPS = 0.01
-UNROLL = 1
+UNROLL_COEF = 2
+UNROLL_DEPTH = 2
+UNROLL_APPLY = 4
 LANES = 128
 BX, BY = 8, 16
 F32 = jnp.float32
@@ -39,6 +41,57 @@
         return jnp.where(inner >= BY - k, carried, rolled)
     carried = major_roll(pltpu.roll(v, (-BY - k) % LANES, 2), -1)
     return jnp.where(inner < -k, carried, rolled)
+
+
+def shifts_x(v, steps):
+    lane = lane_iota(v.shape)
+    n = v.shape[1]
+    rolled = {k: pltpu.roll(v, (-BY * k) % LANES, 2) for k in steps}
+    out = {}
+    for k, r in rolled.items():
+        carried = pltpu.roll(r, (-1 if k > 0 else 1) % n, 1)
+        out[k] = jnp.where(lane >= LANES - BY * k if k > 0 else lane < -BY * k, carried, r)
+    return out, rolled
+
+
+def shifts_y(v, steps, rolled):
+    inner = lane_iota(v.shape) % BY
+    ahead, behind = major_roll(rolled[-1], 1), major_roll(rolled[1], -1)
+    out = {}
+    for k in steps:
+        mixed = jnp.where(inner < k, ahead, v) if k > 0 else jnp.where(inner >= BY + k, behind, v)
+        out[k] = pltpu.roll(mixed, (-k) % LANES, 2)
+    return out
+
+
+def gather_x(parts):
+    total = parts[0]
+    for k, part in parts.items():
+        if k:
+            total = total + shift_x(part, k)
+    return total
+
+
+def gather_y(parts):
+    total = parts[0]
+    inner = lane_iota(total.shape) % BY
+    ahead = behind = None
+    for k, part in parts.items():
+        if k == 0:
+            continue
+        moved = pltpu.roll(part, (-k) % LANES, 2)
+        crossing = inner >= BY - k if k > 0 else inner < -k
+        total = total + jnp.where(crossing, 0.0, moved)
+        over = jnp.where(crossing, moved, 0.0)
+        if k > 0:
+            ahead = over if ahead is None else ahead + over
+        else:
+            behind = over if behind is None else behind + over
+    if ahead is not None:
+        total = total + major_roll(pltpu.roll(ahead, BY, 2), 1)
+    if behind is not None:
+        total = total + major_roll(pltpu.roll(behind, LANES - BY, 2), -1)
+    return total
 
 
 def weno_center(b, dm, d0, d1, d2):
@@ -115,15 +168,18 @@
     return jnp.where(phi > 0, 1.0, -1.0).astype(F32)
 
 
-def coef_plane_kernel(f_ref, phi_ref, co_ref, sum_ref):
+def coef_planes(f_ref, phi_ref, co_ref, sum_ref):
     def plane(z, carry):
         f = f_ref[z]
         side = side_of(phi_ref[z])
+        steps = (-3, -2, -1, 1, 2)
+        along_x, rolled = shifts_x(f, steps)
+        along_y = shifts_y(f, steps, rolled)
         total = None
-        for axis, shift in ((0, shift_x), (1, shift_y)):
-            b = f - shift(f, -1)
-            d = b - shift(b, -1)
-            minus, plus, jac_m, jac_p = weno_center(b, shift(d, -1), d, shift(d, 1), shift(d, 2))
+        for axis, shift, near in ((0, shift_x, along_x), (1, shift_y, along_y)):
+            b = [near[-2] - near[-3], near[-1] - near[-2], f - near[-1], near[1] - f, near[2] - near[1]]
+            d = [b[i + 1] - b[i] for i in range(4)]
+            minus, plus, jac_m, jac_p = weno_center(b[2], *d)
             term, by_minus, by_plus = upwind_term(minus, shift(plus, 1), side)
             for n, part in enumerate((by_minus, by_plus) + jac_m + jac_p):
                 co_ref[PER_AXIS * axis + n, z] = part
@@ -131,10 +187,10 @@
         sum_ref[z] = total
         return carry
 
-    lax.fori_loop(0, 4, plane, 0)
-
-
-def coef_depth_kernel(section, f_ref, lo_ref, hi_ref, phi_ref, sum_ref, co_ref, scale_ref, pc_ref):
+    lax.fori_loop(0, 4, plane, 0, unroll=UNROLL_COEF)
+
+
+def coef_depth(section, f_ref, lo_ref, hi_ref, phi_ref, sum_ref, co_ref, scale_ref, pc_ref):
     def column(g, carry):
         f = (
             [lo_ref[3 * section + i, g] for i in range(3)]
@@ -160,24 +216,7 @@
     lax.fori_loop(0, 4, column, 0)
 
 
-def apply_local(c_ref, cxy_ref, cz_ref, scale_ref, out_ref, up_ref, dn_ref):
-    def plane(z, carry):
-        c = c_ref[z] * scale_ref[z]
-        total = None
-        for axis, shift in ((0, shift_x), (1, shift_y)):
-            co = lambda n: cxy_ref[PER_AXIS * axis + n, z]
-            a = c * co(0)
-            g = shift(c * co(1), -1)
-            t = [a * co(2 + k) + g * co(6 + k) for k in range(4)]
-            dbar = t[1] + shift(t[0], 1) + shift(t[2], -1) + shift(t[3], -2)
-            bbar = (a + g) + (dbar - shift(dbar, 1))
-            part = bbar - shift(bbar, 1)
-            total = part if total is None else total + part
-        out_ref[z] = total
-        return carry
-
-    lax.fori_loop(0, 4, plane, 0, unroll=UNROLL)
-
+def apply_depth(c_ref, co_ref, scale_ref, out_ref, up_ref, dn_ref):
     def column(g, carry):
         dbar = [None] * 8
         bbar = [None] * 9
@@ -187,7 +226,7 @@
 
         for z in range(4):
             c = c_ref[z, g] * scale_ref[z, g]
-            co = lambda n: cz_ref[n, z, g]
+            co = lambda n: co_ref[n, z, g]
             a, p = c * co(0), c * co(1)
             for k in range(4):
                 add(dbar, z + k, a * co(2 + k))
@@ -198,13 +237,35 @@
             add(bbar, j + 1, dbar[j])
             add(bbar, j, -dbar[j])
         for z in range(4):
-            out_ref[z, g] = out_ref[z, g] + (bbar[z + 2] - bbar[z + 3])
+            out_ref[z, g] = bbar[z + 2] - bbar[z + 3]
         for k in range(3):
             up_ref[k, g] = bbar[6 + k]
             dn_ref[k, g] = bbar[k]
         return carry
 
-    lax.fori_loop(0, 4, column, 0, unroll=UNROLL)
+    lax.fori_loop(0, 4, column, 0, unroll=UNROLL_DEPTH)
+
+
+def apply_planes(c_ref, co_ref, scale_ref, pc_ref, part_ref, acc_ref, out_ref, acc_out_ref):
+    def plane(z, carry):
+        whole = c_ref[z]
+        c = whole * scale_ref[z]
+        total = part_ref[z]
+        for axis, shift, gather in ((0, shift_x, gather_x), (1, shift_y, gather_y)):
+            co = lambda n: co_ref[PER_AXIS * axis + n, z]
+            a = c * co(0)
+            g = shift(c * co(1), -1)
+            t = [a * co(2 + k) + g * co(6 + k) for k in range(4)]
+            b = [-t[0], t[0] - t[1], (a + g) + (t[1] - t[2]), t[2] - t[3], t[3]]
+            total = total + gather(
+                {0: b[2] - b[3], -1: b[3] - b[4], -2: b[4], 1: b[1] - b[2], 2: b[0] - b[1], 3: t[0]}
+            )
+        out_ref[z] = total
+        local = pc_ref[z] * whole
+        acc_out_ref[z] = local if acc_ref is None else acc_ref[z] + local
+        return carry
+
+    lax.fori_loop(0, 4, plane, 0, unroll=UNROLL_APPLY)
 
 
 def joined(own_ref, lo_ref, hi_ref):
@@ -218,40 +279,52 @@
     )
 
 
-def stage_one(cot_ref, cxy_ref, cz_ref, scale_ref, pc_ref, own_ref, up_ref, dn_ref, c_ref, acc_ref):
-    half = 0.5 * cot_ref[...]
-    c_ref[...] = half
-    acc_ref[...] = pc_ref[...] * half
-    apply_local(c_ref, cxy_ref, cz_ref, scale_ref, own_ref, up_ref, dn_ref)
-
-
-def stage_two(half_ref, own_in, lo_ref, hi_ref, acc_in, cxy_ref, cz_ref, scale_ref, pc_ref, own_ref, up_ref, dn_ref, c_ref, acc_ref):
+def planes_kernel(*refs):
+    phi_ref = refs[3]
+    for n in range(3):
+        coef_planes(refs[n], phi_ref, refs[4 + 2 * n], refs[5 + 2 * n])
+
+
+def first_stage(f_ref, lo_ref, hi_ref, phi_ref, sum_ref, cot_ref, c_ref, part_ref, up_ref, dn_ref, scale_ref, pc_ref, co_ref):
+    coef_depth(0, f_ref, lo_ref, hi_ref, phi_ref, sum_ref, co_ref, scale_ref, pc_ref)
+    c_ref[...] = 0.5 * cot_ref[...]
+    apply_depth(c_ref, co_ref, scale_ref, part_ref, up_ref, dn_ref)
+
+
+def later_stage(halve, *refs):
+    earlier, (own_in, lo_ref, hi_ref, co_ref, scale_ref) = refs[:-9], refs[-9:-4]
+    c_ref, part_ref, up_ref, dn_ref = refs[-4:]
     for z, back in enumerate(joined(own_in, lo_ref, hi_ref)):
-        c = half_ref[z] + back
-        c_ref[z] = c
-        acc_ref[z] = acc_in[z] + pc_ref[z] * c
-    apply_local(c_ref, cxy_ref, cz_ref, scale_ref, own_ref, up_ref, dn_ref)
-
-
-def stage_three(half_ref, second_ref, own_in, lo_ref, hi_ref, acc_in, cxy_ref, cz_ref, scale_ref, pc_ref, own_ref, up_ref, dn_ref, c_ref, acc_ref):
+        c = back
+        for ref in earlier:
+            c = c + ref[z]
+        c_ref[z] = 0.5 * c if halve else c
+    apply_depth(c_ref, co_ref, scale_ref, part_ref, up_ref, dn_ref)
+
+
+def window_one(c_ref, co_ref, scale_ref, pc_ref, part_ref, f_ref, lo_ref, hi_ref, phi_ref, sum_ref, own_ref, acc_ref, *coef_refs):
+    apply_planes(c_ref, co_ref, scale_ref, pc_ref, part_ref, None, own_ref, acc_ref)
+    coef_depth(1, f_ref, lo_ref, hi_ref, phi_ref, sum_ref, *coef_refs)
+
+
+def window_two(c_ref, co_ref, scale_ref, pc_ref, part_ref, acc_in, f_ref, lo_ref, hi_ref, phi_ref, sum_ref, own_ref, acc_ref, *coef_refs):
+    apply_planes(c_ref, co_ref, scale_ref, pc_ref, part_ref, acc_in, own_ref, acc_ref)
+    coef_depth(2, f_ref, lo_ref, hi_ref, phi_ref, sum_ref, *coef_refs[:3])
+    coef_planes(phi_ref, phi_ref, *coef_refs[3:])
+
+
+def window_three(c_ref, co_ref, scale_ref, pc_ref, part_ref, acc_in, lo_ref, hi_ref, phi_ref, sum_ref, own_ref, acc_ref, *coef_refs):
+    apply_planes(c_ref, co_ref, scale_ref, pc_ref, part_ref, acc_in, own_ref, acc_ref)
+    coef_depth(3, phi_ref, lo_ref, hi_ref, phi_ref, sum_ref, *coef_refs)
+
+
+def window_four(c_ref, co_ref, scale_ref, pc_ref, part_ref, acc_in, own_ref, acc_ref):
+    apply_planes(c_ref, co_ref, scale_ref, pc_ref, part_ref, acc_in, own_ref, acc_ref)
+
+
+def finish(first_ref, middle_ref, own_in, lo_ref, hi_ref, acc_in, out_ref):
     for z, back in enumerate(joined(own_in, lo_ref, hi_ref)):
-        c = 0.5 * (half_ref[z] + second_ref[z] + back)
-        c_ref[z] = c
-        acc_ref[z] = acc_in[z] + pc_ref[z] * c
-    apply_local(c_ref, cxy_ref, cz_ref, scale_ref, own_ref, up_ref, dn_ref)
-
-
-def stage_four(middle_ref, own_in, lo_ref, hi_ref, acc_in, cxy_ref, cz_ref, scale_ref, pc_ref, own_ref, up_ref, dn_ref, c_ref, acc_ref):
-    for z, back in enumerate(joined(own_in, lo_ref, hi_ref)):
-        c = middle_ref[z] + back
-        c_ref[z] = c
-        acc_ref[z] = acc_in[z] + pc_ref[z] * c + (middle_ref[z] + c)
-    apply_local(c_ref, cxy_ref, cz_ref, scale_ref, own_ref, up_ref, dn_ref)
-
-
-def finish(own_in, lo_ref, hi_ref, acc_in, out_ref):
-    for z, back in enumerate(joined(own_in, lo_ref, hi_ref)):
-        whole = acc_in[z] + back
+        whole = (acc_in[z] + back) + (first_ref[z] + middle_ref[z])
         for gy in range(whole.shape[0]):
             for gx in range(whole.shape[1]):
                 out_ref[gy * whole.shape[1] + gx, z] = whole[gy, gx]
@@ -374,39 +447,50 @@
         phi, cot = fields[3], fields[4]
         rim_lo, rim_hi = exchange(rim_up, rim_dn)
 
-        def coef_plane(n):
-            return call(
-                coef_plane_kernel, [near(2 * PER_AXIS, *slab), near(*slab)],
-                fields[n], phi, name=f"coef_plane_{n}",
-            )
-
-        def coef_depth(n, total):
-            return call(
-                lambda *refs: coef_depth_kernel(n, *refs),
-                [near(PER_AXIS, *slab), near(*slab), near(*slab)],
-                fields[n], rim_lo, rim_hi, phi, total, name=f"coef_depth_{n}",
-            )
-
-        def coefs(n):
-            flat, total = coef_plane(n)
-            return (flat, *coef_depth(n, total))
-
-        results = [near(*slab), near(*rim), near(*rim), near(*slab), near(*slab)]
-        own, up, dn, half, acc = call(stage_one, results, cot, *coefs(0), name="stage_one")
+        coef_flat = [near(2 * PER_AXIS, *slab), near(*slab)]
+        coef_deep = [near(PER_AXIS, *slab), near(*slab), near(*slab)]
+        stage_out = [near(*slab), near(*slab), near(*rim), near(*rim)]
+        window_out = [near(*slab), near(*slab)]
+
+        flat0, sum0, flat1, sum1, flat2, sum2 = call(
+            planes_kernel, coef_flat * 3, *fields[:3], phi, name="coef_planes"
+        )
+        c1, part, up, dn, scale0, pc0, _ = call(
+            first_stage, stage_out + [near(*slab), near(*slab), near(PER_AXIS, *slab)],
+            fields[0], rim_lo, rim_hi, phi, sum0, cot, name="stage_one",
+        )
         lo, hi = exchange(up, dn)
-        own, up, dn, second, acc = call(
-            stage_two, results, half, own, lo, hi, acc, *coefs(1), name="stage_two"
+        own, acc, deep, scale, pc = call(
+            window_one, window_out + coef_deep,
+            c1, flat0, scale0, pc0, part, fields[1], rim_lo, rim_hi, phi, sum1, name="window_one",
+        )
+        c2, part, up, dn = call(
+            lambda *refs: later_stage(False, *refs), stage_out,
+            c1, own, lo, hi, deep, scale, name="stage_two",
         )
         lo, hi = exchange(up, dn)
-        own, up, dn, middle, acc = call(
-            stage_three, results, half, second, own, lo, hi, acc, *coefs(2), name="stage_three"
+        own, acc, deep, scale2, pc2, flat3, sum3 = call(
+            window_two, window_out + coef_deep + coef_flat,
+            c2, flat1, scale, pc, part, acc, fields[2], rim_lo, rim_hi, phi, sum2, name="window_two",
+        )
+        c3, part, up, dn = call(
+            lambda *refs: later_stage(True, *refs), stage_out,
+            c1, c2, own, lo, hi, deep, scale2, name="stage_three",
         )
         lo, hi = exchange(up, dn)
-        own, up, dn, _, acc = call(
-            stage_four, results, middle, own, lo, hi, acc, *coefs(3), name="stage_four"
+        own, acc, deep, scale, pc = call(
+            window_three, window_out + coef_deep,
+            c3, flat2, scale2, pc2, part, acc, rim_lo, rim_hi, phi, sum3, name="window_three",
+        )
+        c4, part, up, dn = call(
+            lambda *refs: later_stage(False, *refs), stage_out,
+            c3, own, lo, hi, deep, scale, name="stage_four",
         )
         lo, hi = exchange(up, dn)
-        slabs = call(finish, near(count, depth, LANES), own, lo, hi, acc, name="finish")
+        own, acc = call(
+            window_four, window_out, c4, flat3, scale, pc, part, acc, name="window_four",
+        )
+        slabs = call(finish, near(count, depth, LANES), c4, c3, own, lo, hi, acc, name="finish")
         slabs = lax.all_to_all(slabs, ("gy", "gx"), 0, 0)
         return call(
             lambda *refs: from_slabs(count, depth, flat_position, *refs),

time: 115 us -> 109 us (0.948)
  Pallas kernels: 19 us -> 12.5 us
    pallas_call x16 -> x13, Pallas kernels: 19 us -> 12.5 us  [call(): pl.pallas_call(kernel, out_shape=out_shape, in_specs=[first] + [vmem] * (...]
    ppermute x5, waiting for transfers between devices: 9.45 us -> 10.8 us  [exchange(): lax.ppermute(dn, everywhere, downward)]
  transfers between devices with their start and end apart: 10 -> 10, of which waited for: 6 -> 5; matrix products, arithmetic and copies ran while one was open for 0% -> 0% of each run, Pallas kernels for 8% -> 8%
where the time goes in v4:
time: 109 us; the launch traced here: 108 us
  blocking collectives  56.4 us (52%)
  starting transfers between devices  28.1 us (26%)
  Pallas kernels  12.5 us (11%)
  waiting for transfers between devices  10.8 us (10%)
    all_to_all x1, blocking collectives, shards(): packed = lax.all_to_all(packed, ('gy', 'gx'), 0, 0)  32.4 us
    all_to_all x1, blocking collectives, shards(): slabs = lax.all_to_all(slabs, ('gy', 'gx'), 0, 0)  24 us
    ppermute x5, starting transfers between devices, exchange(): lax.ppermute(up, everywhere, upward)  16 us
    pallas_call x13, Pallas kernels, call(): pl.pallas_call(kernel, out_shape=out_shape, in_specs=[first] + [vmem] * (...  12.5 us
    ppermute x5, starting transfers between devices, exchange(): lax.ppermute(dn, everywhere, downward)  12.1 us
    ppermute x5, waiting for transfers between devices, exchange(): lax.ppermute(dn, everywhere, downward)  10.8 us
  transfers between devices with their start and end apart: 10, of which 5 were waited for; matrix products, arithmetic and copies ran while one was open for 0% of the time, Pallas kernels for 8%

profile of v4, /device:TPU:6, one launch (start us, length us, event | category | flops | bytes accessed | tf_op | source)
XLA Modules:
  0.0 108.0 jit_solution(5384590418430569139)
XLA Ops:
  0.0 1.2 %to_slabs.1 = f32[32,20,128]{2,1,0:T(8,128)S(1)} custom-call(s32[1]{0:T(128)} %bitcast.refs_0_, f32[8,16,128]{2,1,0:T(8,128)} %refs_1_.1, f32[8,16,128]{2,1,0:T(8,128)} %refs_2_.1, f32[8,16,128]{2,1,0:T(8,128)} %refs_3_.1, f32[8,16,128]{2,1,0:T(8,128)} %refs_4_.1, f32[8,16,128]{2,1,0:T(8,128)} %refs_5_.1), custom_call_target="tpu_custom_call" | custom-call | tf_op jit(solution)/shard_map/to_slabs/pallas_call | solution.py:417
  1.2 32.4 %all_to_all.10.refs_0_ = f32[32,20,128]{2,1,0:T(8,128)S(1)} all-to-all(f32[32,20,128]{2,1,0:T(8,128)S(1)} %to_slabs.1), channel_id=1, replica_groups=mesh['gx'=8,'gy'=4,'gz'=16] {'gy','gx'}, dimensions={0} | all-to-all | bytes 655360 | tf_op jit(solution)/shard_map/all_to_all | solution.py:441
  33.8 3.7 %collective-permute-start = (f32[12,4,8,128]{3,2,1,0:T(8,128)S(1)}, f32[12,4,8,128]{3,2,1,0:T(8,128)S(1)}, u32[]{:S(2)}, u32[]{:S(2)}) collective-permute-start(f32[12,4,8,128]{3,2,1,0:T(8,128)S(1)} %get-tuple-element.56), channel_id=1, source_target_pairs={{0,64},{64,128},{128,192},{192,256},{256,320},{320,384},{384,448},... | collective-permute-start | bytes 589832 | tf_op jit(solution)/shard_map/ppermute | solution.py:429
  37.4 1.9 %collective-permute-start.1 = (f32[12,4,8,128]{3,2,1,0:T(8,128)S(1)}, f32[12,4,8,128]{3,2,1,0:T(8,128)S(1)}, u32[]{:S(2)}, u32[]{:S(2)}) collective-permute-start(f32[12,4,8,128]{3,2,1,0:T(8,128)S(1)} %get-tuple-element.57), channel_id=1, source_target_pairs={{64,0},{128,64},{192,128},{256,192},{320,256},{384,320},{448,384},... | collective-permute-start | bytes 589832 | tf_op jit(solution)/shard_map/ppermute | solution.py:429
  39.4 3.3 %coef_planes.1 = (f32[20,4,4,8,128]{4,3,2,1,0:T(8,128)S(1)}, f32[4,4,8,128]{3,2,1,0:T(8,128)S(1)}, f32[20,4,4,8,128]{4,3,2,1,0:T(8,128)S(1)}, f32[4,4,8,128]{3,2...) custom-call(f32[4,4,8,128]{3,2,1,0:T(8,128)S(1)} %get-tuple-element.55.refs_0_.f_ref, ...), custom_call_target="tpu_custom_call" | custom-call | tf_op jit(solution)/shard_map/coef_planes/pallas_call | solution.py:417
  42.7 2.3 %collective-permute-done.1.hi_ref = f32[12,4,8,128]{3,2,1,0:T(8,128)S(1)} collective-permute-done((f32[12,4,8,128]{3,2,1,0:T(8,128)S(1)}, f32[12,4,8,128]{3,2,1,0:T(8,128)S(1)}, u32[]{:S(2)}, u32[]{:S(2)}) %collective-permute-start.1) | collective-permute-done | bytes 196640 | tf_op jit(solution)/shard_map/ppermute | solution.py:429
  45.0 1.5 %stage_one.1 = (f32[4,4,8,128]{3,2,1,0:T(8,128)S(1)}, f32[4,4,8,128]{3,2,1,0:T(8,128)S(1)}, f32[3,4,8,128]{3,2,1,0:T(8,128)S(1)}, f32[3,4,8,128]{3,2,1,0:T(8,128...) custom-call(f32[4,4,8,128]{3,2,1,0:T(8,128)S(1)} %get-tuple-element.55.refs_0_.f_re, ...), custom_call_target="tpu_custom_call" | custom-call | tf_op jit(solution)/shard_map/stage_one/pallas_call | solution.py:417
  46.5 2.3 %collective-permute-start.2 = (f32[3,4,8,128]{3,2,1,0:T(8,128)S(1)}, f32[3,4,8,128]{3,2,1,0:T(8,128)S(1)}, u32[]{:S(2)}, u32[]{:S(2)}) collective-permute-start(f32[3,4,8,128]{3,2,1,0:T(8,128)S(1)} %get-tuple-element.70), channel_id=1, source_target_pairs={{0,64},{64,128},{128,192},{192,256},{256,320},{320,384},{384,448},... | collective-permute-start | bytes 147464 | tf_op jit(solution)/shard_map/ppermute | solution.py:429
  48.8 3.3 %collective-permute-start.3 = (f32[3,4,8,128]{3,2,1,0:T(8,128)S(1)}, f32[3,4,8,128]{3,2,1,0:T(8,128)S(1)}, u32[]{:S(2)}, u32[]{:S(2)}) collective-permute-start(f32[3,4,8,128]{3,2,1,0:T(8,128)S(1)} %get-tuple-element.71), channel_id=1, source_target_pairs={{64,0},{128,64},{192,128},{256,192},{320,256},{384,320},{448,384},... | collective-permute-start | bytes 147464 | tf_op jit(solution)/shard_map/ppermute | solution.py:429
  52.1 1.1 %window_one.1 = (f32[4,4,8,128]{3,2,1,0:T(8,128)S(1)}, f32[4,4,8,128]{3,2,1,0:T(8,128)S(1)}, f32[10,4,4,8,128]{4,3,2,1,0:T(8,128)S(1)}, f32[4,4,8,128]{3,2,1,0:T(8,128)S(1)}, f32[4,4,8,128]{3,2,1,0:T(8,128)S(1)}) custom-call(f32[4,4,8,128]{3,2,1,0:T(8,128)S(1)} %get-tuple-element.63.c_ref.refs_0_, f32[20,4,4,8,128]{4,3,2,1,0:T(8,128)S(1)} %get-tuple-element.64.co_ref, ...), custom_call_target="tpu_custom_call" | custom-call | tf_op jit(solution)/shard_map/window_one/pallas_call | solution.py:417
  53.2 1.5 %collective-permute-done.3.refs_3_ = f32[3,4,8,128]{3,2,1,0:T(8,128)S(1)} collective-permute-done((f32[3,4,8,128]{3,2,1,0:T(8,128)S(1)}, f32[3,4,8,128]{3,2,1,0:T(8,128)S(1)}, u32[]{:S(2)}, u32[]{:S(2)}) %collective-permute-start.3) | collective-permute-done | bytes 49184 | tf_op jit(solution)/shard_map/ppermute | solution.py:429
  54.9 3.0 %collective-permute-start.4 = (f32[3,4,8,128]{3,2,1,0:T(8,128)S(1)}, f32[3,4,8,128]{3,2,1,0:T(8,128)S(1)}, u32[]{:S(2)}, u32[]{:S(2)}) collective-permute-start(f32[3,4,8,128]{3,2,1,0:T(8,128)S(1)} %get-tuple-element.81), channel_id=1, source_target_pairs={{0,64},{64,128},{128,192},{192,256},{256,320},{320,384},{384,448},... | collective-permute-start | bytes 147464 | tf_op jit(solution)/shard_map/ppermute | solution.py:429
  57.9 2.6 %collective-permute-start.5 = (f32[3,4,8,128]{3,2,1,0:T(8,128)S(1)}, f32[3,4,8,128]{3,2,1,0:T(8,128)S(1)}, u32[]{:S(2)}, u32[]{:S(2)}) collective-permute-start(f32[3,4,8,128]{3,2,1,0:T(8,128)S(1)} %get-tuple-element.82), channel_id=1, source_target_pairs={{64,0},{128,64},{192,128},{256,192},{320,256},{384,320},{448,384},... | collective-permute-start | bytes 147464 | tf_op jit(solution)/shard_map/ppermute | solution.py:429
  60.4 2.3 %window_two.1 = (f32[4,4,8,128]{3,2,1,0:T(8,128)S(1)}, f32[4,4,8,128]{3,2,1,0:T(8,128)S(1)}, f32[10,4,4,8,128]{4,3,2,1,0:T(8,128)S(1)}, f32[4,4,8,128]{3,2,1,0:T...) custom-call(f32[4,4,8,128]{3,2,1,0:T(8,128)S(1)} %get-tuple-element.74.c_, ...), custom_call_target="tpu_custom_call" | custom-call | tf_op jit(solution)/shard_map/window_two/pallas_call | solution.py:417
  62.7 1.1 %collective-permute-done.5.refs_4_ = f32[3,4,8,128]{3,2,1,0:T(8,128)S(1)} collective-permute-done((f32[3,4,8,128]{3,2,1,0:T(8,128)S(1)}, f32[3,4,8,128]{3,2,1,0:T(8,128)S(1)}, u32[]{:S(2)}, u32[]{:S(2)}) %collective-permute-start.5) | collective-permute-done | bytes 49184 | tf_op jit(solution)/shard_map/ppermute | solution.py:429
  64.0 3.9 %collective-permute-start.6 = (f32[3,4,8,128]{3,2,1,0:T(8,128)S(1)}, f32[3,4,8,128]{3,2,1,0:T(8,128)S(1)}, u32[]{:S(2)}, u32[]{:S(2)}) collective-permute-start(f32[3,4,8,128]{3,2,1,0:T(8,128)S(1)} %get-tuple-element.92), channel_id=1, source_target_pairs={{0,64},{64,128},{128,192},{192,256},{256,320},{320,384},{384,448},... | collective-permute-start | bytes 147464 | tf_op jit(solution)/shard_map/ppermute | solution.py:429
  67.9 1.9 %collective-permute-start.7 = (f32[3,4,8,128]{3,2,1,0:T(8,128)S(1)}, f32[3,4,8,128]{3,2,1,0:T(8,128)S(1)}, u32[]{:S(2)}, u32[]{:S(2)}) collective-permute-start(f32[3,4,8,128]{3,2,1,0:T(8,128)S(1)} %get-tuple-element.93), channel_id=1, source_target_pairs={{64,0},{128,64},{192,128},{256,192},{320,256},{384,320},{448,384},... | collective-permute-start | bytes 147464 | tf_op jit(solution)/shard_map/ppermute | solution.py:429
  69.8 1.1 %window_three.1 = (f32[4,4,8,128]{3,2,1,0:T(8,128)S(1)}, f32[4,4,8,128]{3,2,1,0:T(8,128)S(1)}, f32[10,4,4,8,128]{4,3,2,1,0:T(8,128)S(1)}, f32[4,4,8,128]{3,2,1,0:T(8,128)S(1)}, f32[4,4,8,128]{3,2,1,0:T(8,128)S(1)}) custom-call(f32[4,4,8,128]{3,2,1,0:T(8,128)S(1)} %get-tuple-element.85.c_ref.refs_0_.middle_ref, ...), custom_call_target="tpu_custom_call" | custom-call | tf_op jit(solution)/shard_map/window_three/pallas_call | solution.py:417
  71.0 2.9 %collective-permute-done.7.refs_3_ = f32[3,4,8,128]{3,2,1,0:T(8,128)S(1)} collective-permute-done((f32[3,4,8,128]{3,2,1,0:T(8,128)S(1)}, f32[3,4,8,128]{3,2,1,0:T(8,128)S(1)}, u32[]{:S(2)}, u32[]{:S(2)}) %collective-permute-start.7) | collective-permute-done | bytes 49184 | tf_op jit(solution)/shard_map/ppermute | solution.py:429
  74.0 3.1 %collective-permute-start.8 = (f32[3,4,8,128]{3,2,1,0:T(8,128)S(1)}, f32[3,4,8,128]{3,2,1,0:T(8,128)S(1)}, u32[]{:S(2)}, u32[]{:S(2)}) collective-permute-start(f32[3,4,8,128]{3,2,1,0:T(8,128)S(1)} %get-tuple-element.102), channel_id=1, source_target_pairs={{0,64},{64,128},{128,192},{192,256},{256,320},{320,384},{384,448},... | collective-permute-start | bytes 147464 | tf_op jit(solution)/shard_map/ppermute | solution.py:429
  77.1 2.4 %collective-permute-start.9 = (f32[3,4,8,128]{3,2,1,0:T(8,128)S(1)}, f32[3,4,8,128]{3,2,1,0:T(8,128)S(1)}, u32[]{:S(2)}, u32[]{:S(2)}) collective-permute-start(f32[3,4,8,128]{3,2,1,0:T(8,128)S(1)} %get-tuple-element.103), channel_id=1, source_target_pairs={{64,0},{128,64},{192,128},{256,192},{320,256},{384,320},{448,384},... | collective-permute-start | bytes 147464 | tf_op jit(solution)/shard_map/ppermute | solution.py:429
  80.2 2.9 %collective-permute-done.9.hi_ref = f32[3,4,8,128]{3,2,1,0:T(8,128)S(1)} collective-permute-done((f32[3,4,8,128]{3,2,1,0:T(8,128)S(1)}, f32[3,4,8,128]{3,2,1,0:T(8,128)S(1)}, u32[]{:S(2)}, u32[]{:S(2)}) %collective-permute-start.9) | collective-permute-done | bytes 49184 | tf_op jit(solution)/shard_map/ppermute | solution.py:429
  83.1 24.0 %all_to_all.11.refs_1_ = f32[32,4,128]{2,1,0:T(4,128)S(1)} all-to-all(f32[32,4,128]{2,1,0:T(4,128)S(1)} %finish.1), channel_id=1, replica_groups=mesh['gx'=8,'gy'=4,'gz'=16] {'gy','gx'}, dimensions={0} | all-to-all | bytes 131072 | tf_op jit(solution)/shard_map/all_to_all | solution.py:494
  107.2 0.9 from_slabs.1
  (11 shorter events, 1.2 us)
Async XLA Ops:
  33.8 9.0 %collective-permute-start = (f32[12,4,8,128]{3,2,1,0:T(8,128)S(1)}, f32[12,4,8,128]{3,2,1,0:T(8,128)S(1)}, u32[]{:S(2)}, u32[]{:S(2)}) collective-permute-start(f32[12,4,8,128]{3,2,1,0:T(8,128)S(1)} %get-tuple-element.56), channel_id=1, source_target_pairs={{0,64},{64,128},{128,192},{192,256},{256,320},{320,384},{384,448},... | collective-permute-start | bytes 589832 | tf_op jit(solution)/shard_map/ppermute | solution.py:429
  37.4 7.6 %collective-permute-start.1 = (f32[12,4,8,128]{3,2,1,0:T(8,128)S(1)}, f32[12,4,8,128]{3,2,1,0:T(8,128)S(1)}, u32[]{:S(2)}, u32[]{:S(2)}) collective-permute-start(f32[12,4,8,128]{3,2,1,0:T(8,128)S(1)} %get-tuple-element.57), channel_id=1, source_target_pairs={{64,0},{128,64},{192,128},{256,192},{320,256},{384,320},{448,384},... | collective-permute-start | bytes 589832 | tf_op jit(solution)/shard_map/ppermute | solution.py:429
  46.5 6.7 %collective-permute-start.2 = (f32[3,4,8,128]{3,2,1,0:T(8,128)S(1)}, f32[3,4,8,128]{3,2,1,0:T(8,128)S(1)}, u32[]{:S(2)}, u32[]{:S(2)}) collective-permute-start(f32[3,4,8,128]{3,2,1,0:T(8,128)S(1)} %get-tuple-element.70), channel_id=1, source_target_pairs={{0,64},{64,128},{128,192},{192,256},{256,320},{320,384},{384,448},... | collective-permute-start | bytes 147464 | tf_op jit(solution)/shard_map/ppermute | solution.py:429
  48.8 6.0 %collective-permute-start.3 = (f32[3,4,8,128]{3,2,1,0:T(8,128)S(1)}, f32[3,4,8,128]{3,2,1,0:T(8,128)S(1)}, u32[]{:S(2)}, u32[]{:S(2)}) collective-permute-start(f32[3,4,8,128]{3,2,1,0:T(8,128)S(1)} %get-tuple-element.71), channel_id=1, source_target_pairs={{64,0},{128,64},{192,128},{256,192},{320,256},{384,320},{448,384},... | collective-permute-start | bytes 147464 | tf_op jit(solution)/shard_map/ppermute | solution.py:429
  54.9 7.8 %collective-permute-start.4 = (f32[3,4,8,128]{3,2,1,0:T(8,128)S(1)}, f32[3,4,8,128]{3,2,1,0:T(8,128)S(1)}, u32[]{:S(2)}, u32[]{:S(2)}) collective-permute-start(f32[3,4,8,128]{3,2,1,0:T(8,128)S(1)} %get-tuple-element.81), channel_id=1, source_target_pairs={{0,64},{64,128},{128,192},{192,256},{256,320},{320,384},{384,448},... | collective-permute-start | bytes 147464 | tf_op jit(solution)/shard_map/ppermute | solution.py:429
  57.9 6.0 %collective-permute-start.5 = (f32[3,4,8,128]{3,2,1,0:T(8,128)S(1)}, f32[3,4,8,128]{3,2,1,0:T(8,128)S(1)}, u32[]{:S(2)}, u32[]{:S(2)}) collective-permute-start(f32[3,4,8,128]{3,2,1,0:T(8,128)S(1)} %get-tuple-element.82), channel_id=1, source_target_pairs={{64,0},{128,64},{192,128},{256,192},{320,256},{384,320},{448,384},... | collective-permute-start | bytes 147464 | tf_op jit(solution)/shard_map/ppermute | solution.py:429
  64.0 7.0 %collective-permute-start.6 = (f32[3,4,8,128]{3,2,1,0:T(8,128)S(1)}, f32[3,4,8,128]{3,2,1,0:T(8,128)S(1)}, u32[]{:S(2)}, u32[]{:S(2)}) collective-permute-start(f32[3,4,8,128]{3,2,1,0:T(8,128)S(1)} %get-tuple-element.92), channel_id=1, source_target_pairs={{0,64},{64,128},{128,192},{192,256},{256,320},{320,384},{384,448},... | collective-permute-start | bytes 147464 | tf_op jit(solution)/shard_map/ppermute | solution.py:429
  67.9 6.0 %collective-permute-start.7 = (f32[3,4,8,128]{3,2,1,0:T(8,128)S(1)}, f32[3,4,8,128]{3,2,1,0:T(8,128)S(1)}, u32[]{:S(2)}, u32[]{:S(2)}) collective-permute-start(f32[3,4,8,128]{3,2,1,0:T(8,128)S(1)} %get-tuple-element.93), channel_id=1, source_target_pairs={{64,0},{128,64},{192,128},{256,192},{320,256},{384,320},{448,384},... | collective-permute-start | bytes 147464 | tf_op jit(solution)/shard_map/ppermute | solution.py:429
  74.0 6.2 %collective-permute-start.8 = (f32[3,4,8,128]{3,2,1,0:T(8,128)S(1)}, f32[3,4,8,128]{3,2,1,0:T(8,128)S(1)}, u32[]{:S(2)}, u32[]{:S(2)}) collective-permute-start(f32[3,4,8,128]{3,2,1,0:T(8,128)S(1)} %get-tuple-element.102), channel_id=1, source_target_pairs={{0,64},{64,128},{128,192},{192,256},{256,320},{320,384},{384,448},... | collective-permute-start | bytes 147464 | tf_op jit(solution)/shard_map/ppermute | solution.py:429
  77.1 6.0 %collective-permute-start.9 = (f32[3,4,8,128]{3,2,1,0:T(8,128)S(1)}, f32[3,4,8,128]{3,2,1,0:T(8,128)S(1)}, u32[]{:S(2)}, u32[]{:S(2)}) collective-permute-start(f32[3,4,8,128]{3,2,1,0:T(8,128)S(1)} %get-tuple-element.103), channel_id=1, source_target_pairs={{64,0},{128,64},{192,128},{256,192},{320,256},{384,320},{448,384},... | collective-permute-start | bytes 147464 | tf_op jit(solution)/shard_map/ppermute | solution.py:429

commit v5 on v4

--- a/solution.py
+++ b/solution.py
@@ -10,7 +10,6 @@
 SMOOTH_EPS = 0.01
 UNROLL_COEF = 2
 UNROLL_DEPTH = 2
-UNROLL_APPLY = 4
 LANES = 128
 BX, BY = 8, 16
 F32 = jnp.float32
@@ -168,10 +167,20 @@
     return jnp.where(phi > 0, 1.0, -1.0).astype(F32)
 
 
-def coef_planes(f_ref, phi_ref, co_ref, sum_ref):
+class Halves:
+    def __init__(self, low, high, at):
+        self.refs, self.at = (low, high), at
+
+    def __getitem__(self, index):
+        index = index if isinstance(index, tuple) else (index,)
+        half, plane = divmod(index[self.at], 2)
+        return self.refs[half][index[: self.at] + (plane,) + index[self.at + 1 :]]
+
+
+def coef_planes(f_ref, phi_ref, co_ref, sum_ref, first=0, count=4):
     def plane(z, carry):
-        f = f_ref[z]
-        side = side_of(phi_ref[z])
+        f = f_ref[first + z]
+        side = side_of(phi_ref[first + z])
         steps = (-3, -2, -1, 1, 2)
         along_x, rolled = shifts_x(f, steps)
         along_y = shifts_y(f, steps, rolled)
@@ -187,7 +196,7 @@
         sum_ref[z] = total
         return carry
 
-    lax.fori_loop(0, 4, plane, 0, unroll=UNROLL_COEF)
+    lax.fori_loop(0, count, plane, 0, unroll=UNROLL_COEF)
 
 
 def coef_depth(section, f_ref, lo_ref, hi_ref, phi_ref, sum_ref, co_ref, scale_ref, pc_ref):
@@ -247,7 +256,7 @@
 
 
 def apply_planes(c_ref, co_ref, scale_ref, pc_ref, part_ref, acc_ref, out_ref, acc_out_ref):
-    def plane(z, carry):
+    for z in range(4):
         whole = c_ref[z]
         c = whole * scale_ref[z]
         total = part_ref[z]
@@ -263,9 +272,6 @@
         out_ref[z] = total
         local = pc_ref[z] * whole
         acc_out_ref[z] = local if acc_ref is None else acc_ref[z] + local
-        return carry
-
-    lax.fori_loop(0, 4, plane, 0, unroll=UNROLL_APPLY)
 
 
 def joined(own_ref, lo_ref, hi_ref):
@@ -304,22 +310,23 @@
 
 def window_one(c_ref, co_ref, scale_ref, pc_ref, part_ref, f_ref, lo_ref, hi_ref, phi_ref, sum_ref, own_ref, acc_ref, *coef_refs):
     apply_planes(c_ref, co_ref, scale_ref, pc_ref, part_ref, None, own_ref, acc_ref)
-    coef_depth(1, f_ref, lo_ref, hi_ref, phi_ref, sum_ref, *coef_refs)
+    coef_depth(1, f_ref, lo_ref, hi_ref, phi_ref, sum_ref, *coef_refs[:3])
+    coef_planes(phi_ref, phi_ref, *coef_refs[3:], first=0, count=2)
 
 
 def window_two(c_ref, co_ref, scale_ref, pc_ref, part_ref, acc_in, f_ref, lo_ref, hi_ref, phi_ref, sum_ref, own_ref, acc_ref, *coef_refs):
     apply_planes(c_ref, co_ref, scale_ref, pc_ref, part_ref, acc_in, own_ref, acc_ref)
     coef_depth(2, f_ref, lo_ref, hi_ref, phi_ref, sum_ref, *coef_refs[:3])
-    coef_planes(phi_ref, phi_ref, *coef_refs[3:])
-
-
-def window_three(c_ref, co_ref, scale_ref, pc_ref, part_ref, acc_in, lo_ref, hi_ref, phi_ref, sum_ref, own_ref, acc_ref, *coef_refs):
+    coef_planes(phi_ref, phi_ref, *coef_refs[3:], first=2, count=2)
+
+
+def window_three(c_ref, co_ref, scale_ref, pc_ref, part_ref, acc_in, lo_ref, hi_ref, phi_ref, sum_low, sum_high, own_ref, acc_ref, *coef_refs):
     apply_planes(c_ref, co_ref, scale_ref, pc_ref, part_ref, acc_in, own_ref, acc_ref)
-    coef_depth(3, phi_ref, lo_ref, hi_ref, phi_ref, sum_ref, *coef_refs)
-
-
-def window_four(c_ref, co_ref, scale_ref, pc_ref, part_ref, acc_in, own_ref, acc_ref):
-    apply_planes(c_ref, co_ref, scale_ref, pc_ref, part_ref, acc_in, own_ref, acc_ref)
+    coef_depth(3, phi_ref, lo_ref, hi_ref, phi_ref, Halves(sum_low, sum_high, 0), *coef_refs)
+
+
+def window_four(c_ref, co_low, co_high, scale_ref, pc_ref, part_ref, acc_in, own_ref, acc_ref):
+    apply_planes(c_ref, Halves(co_low, co_high, 1), scale_ref, pc_ref, part_ref, acc_in, own_ref, acc_ref)
 
 
 def finish(first_ref, middle_ref, own_in, lo_ref, hi_ref, acc_in, out_ref):
@@ -448,6 +455,7 @@
         rim_lo, rim_hi = exchange(rim_up, rim_dn)
 
         coef_flat = [near(2 * PER_AXIS, *slab), near(*slab)]
+        coef_half = [near(2 * PER_AXIS, 2, *slab[1:]), near(2, *slab[1:])]
         coef_deep = [near(PER_AXIS, *slab), near(*slab), near(*slab)]
         stage_out = [near(*slab), near(*slab), near(*rim), near(*rim)]
         window_out = [near(*slab), near(*slab)]
@@ -455,13 +463,14 @@
         flat0, sum0, flat1, sum1, flat2, sum2 = call(
             planes_kernel, coef_flat * 3, *fields[:3], phi, name="coef_planes"
         )
-        c1, part, up, dn, scale0, pc0, _ = call(
-            first_stage, stage_out + [near(*slab), near(*slab), near(PER_AXIS, *slab)],
-            fields[0], rim_lo, rim_hi, phi, sum0, cot, name="stage_one",
+        c1, part, up, dn, scale0, pc0 = call(
+            first_stage, stage_out + [near(*slab), near(*slab)],
+            fields[0], rim_lo, rim_hi, phi, sum0, cot,
+            scratch=[pltpu.VMEM((PER_AXIS, *slab), F32)], name="stage_one",
         )
         lo, hi = exchange(up, dn)
-        own, acc, deep, scale, pc = call(
-            window_one, window_out + coef_deep,
+        own, acc, deep, scale, pc, flat3a, sum3a = call(
+            window_one, window_out + coef_deep + coef_half,
             c1, flat0, scale0, pc0, part, fields[1], rim_lo, rim_hi, phi, sum1, name="window_one",
         )
         c2, part, up, dn = call(
@@ -469,8 +478,8 @@
             c1, own, lo, hi, deep, scale, name="stage_two",
         )
         lo, hi = exchange(up, dn)
-        own, acc, deep, scale2, pc2, flat3, sum3 = call(
-            window_two, window_out + coef_deep + coef_flat,
+        own, acc, deep, scale2, pc2, flat3b, sum3b = call(
+            window_two, window_out + coef_deep + coef_half,
             c2, flat1, scale, pc, part, acc, fields[2], rim_lo, rim_hi, phi, sum2, name="window_two",
         )
         c3, part, up, dn = call(
@@ -480,7 +489,7 @@
         lo, hi = exchange(up, dn)
         own, acc, deep, scale, pc = call(
             window_three, window_out + coef_deep,
-            c3, flat2, scale2, pc2, part, acc, rim_lo, rim_hi, phi, sum3, name="window_three",
+            c3, flat2, scale2, pc2, part, acc, rim_lo, rim_hi, phi, sum3a, sum3b, name="window_three",
         )
         c4, part, up, dn = call(
             lambda *refs: later_stage(False, *refs), stage_out,
@@ -488,7 +497,7 @@
         )
         lo, hi = exchange(up, dn)
         own, acc = call(
-            window_four, window_out, c4, flat3, scale, pc, part, acc, name="window_four",
+            window_four, window_out, c4, flat3a, flat3b, scale, pc, part, acc, name="window_four",
         )
         slabs = call(finish, near(count, depth, LANES), c4, c3, own, lo, hi, acc, name="finish")
         slabs = lax.all_to_all(slabs, ("gy", "gx"), 0, 0)

time: 109 us -> 107 us (0.982)
  no operation moved by 1% of the time
where the time goes in v5:
time: 107 us
  blocking collectives  56.2 us (53%)
  starting transfers between devices  28.1 us (26%)
  Pallas kernels  11.6 us (11%)
  waiting for transfers between devices  10.8 us (10%)
    all_to_all x1, blocking collectives, shards(): packed = lax.all_to_all(packed, ('gy', 'gx'), 0, 0)  32.4 us
    all_to_all x1, blocking collectives, shards(): slabs = lax.all_to_all(slabs, ('gy', 'gx'), 0, 0)  23.8 us
    ppermute x5, starting transfers between devices, exchange(): lax.ppermute(up, everywhere, upward)  16 us
    ppermute x5, starting transfers between devices, exchange(): lax.ppermute(dn, everywhere, downward)  12.1 us
    pallas_call x13, Pallas kernels, call(): pl.pallas_call(kernel, out_shape=out_shape, in_specs=[first] + [vmem] * (...  11.6 us
    ppermute x5, waiting for transfers between devices, exchange(): lax.ppermute(dn, everywhere, downward)  10.8 us
  transfers between devices with their start and end apart: 10, of which 5 were waited for; matrix products, arithmetic and copies ran while one was open for 0% of the time, Pallas kernels for 8%

profile of v5, /device:TPU:6, one launch (start us, length us, event | category | flops | bytes accessed | tf_op | source)
XLA Modules:
  0.0 107.0 jit_solution(11990596625451511947)
XLA Ops:
  0.0 1.2 %to_slabs.1 = f32[32,20,128]{2,1,0:T(8,128)S(1)} custom-call(s32[1]{0:T(128)} %bitcast.refs_0_, f32[8,16,128]{2,1,0:T(8,128)} %refs_1_.1, f32[8,16,128]{2,1,0:T(8,128)} %refs_2_.1, f32[8,16,128]{2,1,0:T(8,128)} %refs_3_.1, f32[8,16,128]{2,1,0:T(8,128)} %refs_4_.1, f32[8,16,128]{2,1,0:T(8,128)} %refs_5_.1), custom_call_target="tpu_custom_call" | custom-call | tf_op jit(solution)/shard_map/to_slabs/pallas_call | solution.py:424
  1.2 32.4 %all_to_all.10.refs_0_ = f32[32,20,128]{2,1,0:T(8,128)S(1)} all-to-all(f32[32,20,128]{2,1,0:T(8,128)S(1)} %to_slabs.1), channel_id=1, replica_groups=mesh['gx'=8,'gy'=4,'gz'=16] {'gy','gx'}, dimensions={0} | all-to-all | bytes 655360 | tf_op jit(solution)/shard_map/all_to_all | solution.py:448
  33.8 3.7 %collective-permute-start = (f32[12,4,8,128]{3,2,1,0:T(8,128)S(1)}, f32[12,4,8,128]{3,2,1,0:T(8,128)S(1)}, u32[]{:S(2)}, u32[]{:S(2)}) collective-permute-start(f32[12,4,8,128]{3,2,1,0:T(8,128)S(1)} %get-tuple-element.58), channel_id=1, source_target_pairs={{0,64},{64,128},{128,192},{192,256},{256,320},{320,384},{384,448},... | collective-permute-start | bytes 589832 | tf_op jit(solution)/shard_map/ppermute | solution.py:436
  37.4 1.9 %collective-permute-start.1 = (f32[12,4,8,128]{3,2,1,0:T(8,128)S(1)}, f32[12,4,8,128]{3,2,1,0:T(8,128)S(1)}, u32[]{:S(2)}, u32[]{:S(2)}) collective-permute-start(f32[12,4,8,128]{3,2,1,0:T(8,128)S(1)} %get-tuple-element.59), channel_id=1, source_target_pairs={{64,0},{128,64},{192,128},{256,192},{320,256},{384,320},{448,384},... | collective-permute-start | bytes 589832 | tf_op jit(solution)/shard_map/ppermute | solution.py:436
  39.4 3.3 %coef_planes.1 = (f32[20,4,4,8,128]{4,3,2,1,0:T(8,128)S(1)}, f32[4,4,8,128]{3,2,1,0:T(8,128)S(1)}, f32[20,4,4,8,128]{4,3,2,1,0:T(8,128)S(1)}, f32[4,4,8,128]{3,2...) custom-call(f32[4,4,8,128]{3,2,1,0:T(8,128)S(1)} %get-tuple-element.57.refs_0_.f_ref, ...), custom_call_target="tpu_custom_call" | custom-call | tf_op jit(solution)/shard_map/coef_planes/pallas_call | solution.py:424
  42.7 2.3 %collective-permute-done.1.hi_ref = f32[12,4,8,128]{3,2,1,0:T(8,128)S(1)} collective-permute-done((f32[12,4,8,128]{3,2,1,0:T(8,128)S(1)}, f32[12,4,8,128]{3,2,1,0:T(8,128)S(1)}, u32[]{:S(2)}, u32[]{:S(2)}) %collective-permute-start.1) | collective-permute-done | bytes 196640 | tf_op jit(solution)/shard_map/ppermute | solution.py:436
  45.0 0.6 stage_one.1
  45.6 2.3 %collective-permute-start.2 = (f32[3,4,8,128]{3,2,1,0:T(8,128)S(1)}, f32[3,4,8,128]{3,2,1,0:T(8,128)S(1)}, u32[]{:S(2)}, u32[]{:S(2)}) collective-permute-start(f32[3,4,8,128]{3,2,1,0:T(8,128)S(1)} %get-tuple-element.72), channel_id=1, source_target_pairs={{0,64},{64,128},{128,192},{192,256},{256,320},{320,384},{384,448},... | collective-permute-start | bytes 147464 | tf_op jit(solution)/shard_map/ppermute | solution.py:436
  47.9 3.3 %collective-permute-start.3 = (f32[3,4,8,128]{3,2,1,0:T(8,128)S(1)}, f32[3,4,8,128]{3,2,1,0:T(8,128)S(1)}, u32[]{:S(2)}, u32[]{:S(2)}) collective-permute-start(f32[3,4,8,128]{3,2,1,0:T(8,128)S(1)} %get-tuple-element.73), channel_id=1, source_target_pairs={{64,0},{128,64},{192,128},{256,192},{320,256},{384,320},{448,384},... | collective-permute-start | bytes 147464 | tf_op jit(solution)/shard_map/ppermute | solution.py:436
  51.2 1.7 %window_one.1 = (f32[4,4,8,128]{3,2,1,0:T(8,128)S(1)}, f32[4,4,8,128]{3,2,1,0:T(8,128)S(1)}, f32[10,4,4,8,128]{4,3,2,1,0:T(8,128)S(1)}, f32[4,4,8,128]{3,2,1,0:T...) custom-call(f32[4,4,8,128]{3,2,1,0:T(8,128)S(1)} %get-tuple-element.65.c_, ...), custom_call_target="tpu_custom_call" | custom-call | tf_op jit(solution)/shard_map/window_one/pallas_call | solution.py:424
  52.9 1.0 collective-permute-done.3.refs_3_
  54.0 3.0 %collective-permute-start.4 = (f32[3,4,8,128]{3,2,1,0:T(8,128)S(1)}, f32[3,4,8,128]{3,2,1,0:T(8,128)S(1)}, u32[]{:S(2)}, u32[]{:S(2)}) collective-permute-start(f32[3,4,8,128]{3,2,1,0:T(8,128)S(1)} %get-tuple-element.83), channel_id=1, source_target_pairs={{0,64},{64,128},{128,192},{192,256},{256,320},{320,384},{384,448},... | collective-permute-start | bytes 147464 | tf_op jit(solution)/shard_map/ppermute | solution.py:436
  57.0 2.6 %collective-permute-start.5 = (f32[3,4,8,128]{3,2,1,0:T(8,128)S(1)}, f32[3,4,8,128]{3,2,1,0:T(8,128)S(1)}, u32[]{:S(2)}, u32[]{:S(2)}) collective-permute-start(f32[3,4,8,128]{3,2,1,0:T(8,128)S(1)} %get-tuple-element.84), channel_id=1, source_target_pairs={{64,0},{128,64},{192,128},{256,192},{320,256},{384,320},{448,384},... | collective-permute-start | bytes 147464 | tf_op jit(solution)/shard_map/ppermute | solution.py:436
  59.6 1.7 %window_two.1 = (f32[4,4,8,128]{3,2,1,0:T(8,128)S(1)}, f32[4,4,8,128]{3,2,1,0:T(8,128)S(1)}, f32[10,4,4,8,128]{4,3,2,1,0:T(8,128)S(1)}, f32[4,4,8,128]{3,2,1,0:T...) custom-call(f32[4,4,8,128]{3,2,1,0:T(8,128)S(1)} %get-tuple-element.76.c_, ...), custom_call_target="tpu_custom_call" | custom-call | tf_op jit(solution)/shard_map/window_two/pallas_call | solution.py:424
  61.3 1.7 %collective-permute-done.5.refs_4_ = f32[3,4,8,128]{3,2,1,0:T(8,128)S(1)} collective-permute-done((f32[3,4,8,128]{3,2,1,0:T(8,128)S(1)}, f32[3,4,8,128]{3,2,1,0:T(8,128)S(1)}, u32[]{:S(2)}, u32[]{:S(2)}) %collective-permute-start.5) | collective-permute-done | bytes 49184 | tf_op jit(solution)/shard_map/ppermute | solution.py:436
  63.1 3.9 %collective-permute-start.6 = (f32[3,4,8,128]{3,2,1,0:T(8,128)S(1)}, f32[3,4,8,128]{3,2,1,0:T(8,128)S(1)}, u32[]{:S(2)}, u32[]{:S(2)}) collective-permute-start(f32[3,4,8,128]{3,2,1,0:T(8,128)S(1)} %get-tuple-element.95), channel_id=1, source_target_pairs={{0,64},{64,128},{128,192},{192,256},{256,320},{320,384},{384,448},... | collective-permute-start | bytes 147464 | tf_op jit(solution)/shard_map/ppermute | solution.py:436
  67.1 1.9 %collective-permute-start.7 = (f32[3,4,8,128]{3,2,1,0:T(8,128)S(1)}, f32[3,4,8,128]{3,2,1,0:T(8,128)S(1)}, u32[]{:S(2)}, u32[]{:S(2)}) collective-permute-start(f32[3,4,8,128]{3,2,1,0:T(8,128)S(1)} %get-tuple-element.96), channel_id=1, source_target_pairs={{64,0},{128,64},{192,128},{256,192},{320,256},{384,320},{448,384},... | collective-permute-start | bytes 147464 | tf_op jit(solution)/shard_map/ppermute | solution.py:436
  69.0 1.1 %window_three.1 = (f32[4,4,8,128]{3,2,1,0:T(8,128)S(1)}, f32[4,4,8,128]{3,2,1,0:T(8,128)S(1)}, f32[10,4,4,8,128]{4,3,2,1,0:T(8,128)S(1)}, f32[4,4,8,128]{3,2,1,0:T(8,128)S(1)}, f32[4,4,8,128]{3,2,1,0:T(8,128)S(1)}) custom-call(f32[4,4,8,128]{3,2,1,0:T(8,128)S(1)} %get-tuple-element.87.c_ref.refs_0_.middle_ref, ...), custom_call_target="tpu_custom_call" | custom-call | tf_op jit(solution)/shard_map/window_three/pallas_call | solution.py:424
  70.1 2.9 %collective-permute-done.7.refs_3_ = f32[3,4,8,128]{3,2,1,0:T(8,128)S(1)} collective-permute-done((f32[3,4,8,128]{3,2,1,0:T(8,128)S(1)}, f32[3,4,8,128]{3,2,1,0:T(8,128)S(1)}, u32[]{:S(2)}, u32[]{:S(2)}) %collective-permute-start.7) | collective-permute-done | bytes 49184 | tf_op jit(solution)/shard_map/ppermute | solution.py:436
  73.2 3.1 %collective-permute-start.8 = (f32[3,4,8,128]{3,2,1,0:T(8,128)S(1)}, f32[3,4,8,128]{3,2,1,0:T(8,128)S(1)}, u32[]{:S(2)}, u32[]{:S(2)}) collective-permute-start(f32[3,4,8,128]{3,2,1,0:T(8,128)S(1)} %get-tuple-element.106), channel_id=1, source_target_pairs={{0,64},{64,128},{128,192},{192,256},{256,320},{320,384},{384,448},... | collective-permute-start | bytes 147464 | tf_op jit(solution)/shard_map/ppermute | solution.py:436
  76.3 2.4 %collective-permute-start.9 = (f32[3,4,8,128]{3,2,1,0:T(8,128)S(1)}, f32[3,4,8,128]{3,2,1,0:T(8,128)S(1)}, u32[]{:S(2)}, u32[]{:S(2)}) collective-permute-start(f32[3,4,8,128]{3,2,1,0:T(8,128)S(1)} %get-tuple-element.107), channel_id=1, source_target_pairs={{64,0},{128,64},{192,128},{256,192},{320,256},{384,320},{448,384},... | collective-permute-start | bytes 147464 | tf_op jit(solution)/shard_map/ppermute | solution.py:436
  79.3 2.9 %collective-permute-done.9.hi_ref = f32[3,4,8,128]{3,2,1,0:T(8,128)S(1)} collective-permute-done((f32[3,4,8,128]{3,2,1,0:T(8,128)S(1)}, f32[3,4,8,128]{3,2,1,0:T(8,128)S(1)}, u32[]{:S(2)}, u32[]{:S(2)}) %collective-permute-start.9) | collective-permute-done | bytes 49184 | tf_op jit(solution)/shard_map/ppermute | solution.py:436
  82.3 23.8 %all_to_all.11.refs_1_ = f32[32,4,128]{2,1,0:T(4,128)S(1)} all-to-all(f32[32,4,128]{2,1,0:T(4,128)S(1)} %finish.1), channel_id=1, replica_groups=mesh['gx'=8,'gy'=4,'gz'=16] {'gy','gx'}, dimensions={0} | all-to-all | bytes 131072 | tf_op jit(solution)/shard_map/all_to_all | solution.py:503
  106.1 0.9 from_slabs.1
  (11 shorter events, 1.2 us)
Async XLA Ops:
  33.8 9.0 %collective-permute-start = (f32[12,4,8,128]{3,2,1,0:T(8,128)S(1)}, f32[12,4,8,128]{3,2,1,0:T(8,128)S(1)}, u32[]{:S(2)}, u32[]{:S(2)}) collective-permute-start(f32[12,4,8,128]{3,2,1,0:T(8,128)S(1)} %get-tuple-element.58), channel_id=1, source_target_pairs={{0,64},{64,128},{128,192},{192,256},{256,320},{320,384},{384,448},... | collective-permute-start | bytes 589832 | tf_op jit(solution)/shard_map/ppermute | solution.py:436
  37.4 7.6 %collective-permute-start.1 = (f32[12,4,8,128]{3,2,1,0:T(8,128)S(1)}, f32[12,4,8,128]{3,2,1,0:T(8,128)S(1)}, u32[]{:S(2)}, u32[]{:S(2)}) collective-permute-start(f32[12,4,8,128]{3,2,1,0:T(8,128)S(1)} %get-tuple-element.59), channel_id=1, source_target_pairs={{64,0},{128,64},{192,128},{256,192},{320,256},{384,320},{448,384},... | collective-permute-start | bytes 589832 | tf_op jit(solution)/shard_map/ppermute | solution.py:436
  45.6 7.3 %collective-permute-start.2 = (f32[3,4,8,128]{3,2,1,0:T(8,128)S(1)}, f32[3,4,8,128]{3,2,1,0:T(8,128)S(1)}, u32[]{:S(2)}, u32[]{:S(2)}) collective-permute-start(f32[3,4,8,128]{3,2,1,0:T(8,128)S(1)} %get-tuple-element.72), channel_id=1, source_target_pairs={{0,64},{64,128},{128,192},{192,256},{256,320},{320,384},{384,448},... | collective-permute-start | bytes 147464 | tf_op jit(solution)/shard_map/ppermute | solution.py:436
  47.9 6.0 %collective-permute-start.3 = (f32[3,4,8,128]{3,2,1,0:T(8,128)S(1)}, f32[3,4,8,128]{3,2,1,0:T(8,128)S(1)}, u32[]{:S(2)}, u32[]{:S(2)}) collective-permute-start(f32[3,4,8,128]{3,2,1,0:T(8,128)S(1)} %get-tuple-element.73), channel_id=1, source_target_pairs={{64,0},{128,64},{192,128},{256,192},{320,256},{384,320},{448,384},... | collective-permute-start | bytes 147464 | tf_op jit(solution)/shard_map/ppermute | solution.py:436
  54.0 7.3 %collective-permute-start.4 = (f32[3,4,8,128]{3,2,1,0:T(8,128)S(1)}, f32[3,4,8,128]{3,2,1,0:T(8,128)S(1)}, u32[]{:S(2)}, u32[]{:S(2)}) collective-permute-start(f32[3,4,8,128]{3,2,1,0:T(8,128)S(1)} %get-tuple-element.83), channel_id=1, source_target_pairs={{0,64},{64,128},{128,192},{192,256},{256,320},{320,384},{384,448},... | collective-permute-start | bytes 147464 | tf_op jit(solution)/shard_map/ppermute | solution.py:436
  57.0 6.0 %collective-permute-start.5 = (f32[3,4,8,128]{3,2,1,0:T(8,128)S(1)}, f32[3,4,8,128]{3,2,1,0:T(8,128)S(1)}, u32[]{:S(2)}, u32[]{:S(2)}) collective-permute-start(f32[3,4,8,128]{3,2,1,0:T(8,128)S(1)} %get-tuple-element.84), channel_id=1, source_target_pairs={{64,0},{128,64},{192,128},{256,192},{320,256},{384,320},{448,384},... | collective-permute-start | bytes 147464 | tf_op jit(solution)/shard_map/ppermute | solution.py:436
  63.1 7.0 %collective-permute-start.6 = (f32[3,4,8,128]{3,2,1,0:T(8,128)S(1)}, f32[3,4,8,128]{3,2,1,0:T(8,128)S(1)}, u32[]{:S(2)}, u32[]{:S(2)}) collective-permute-start(f32[3,4,8,128]{3,2,1,0:T(8,128)S(1)} %get-tuple-element.95), channel_id=1, source_target_pairs={{0,64},{64,128},{128,192},{192,256},{256,320},{320,384},{384,448},... | collective-permute-start | bytes 147464 | tf_op jit(solution)/shard_map/ppermute | solution.py:436
  67.1 6.0 %collective-permute-start.7 = (f32[3,4,8,128]{3,2,1,0:T(8,128)S(1)}, f32[3,4,8,128]{3,2,1,0:T(8,128)S(1)}, u32[]{:S(2)}, u32[]{:S(2)}) collective-permute-start(f32[3,4,8,128]{3,2,1,0:T(8,128)S(1)} %get-tuple-element.96), channel_id=1, source_target_pairs={{64,0},{128,64},{192,128},{256,192},{320,256},{384,320},{448,384},... | collective-permute-start | bytes 147464 | tf_op jit(solution)/shard_map/ppermute | solution.py:436
  73.2 6.2 %collective-permute-start.8 = (f32[3,4,8,128]{3,2,1,0:T(8,128)S(1)}, f32[3,4,8,128]{3,2,1,0:T(8,128)S(1)}, u32[]{:S(2)}, u32[]{:S(2)}) collective-permute-start(f32[3,4,8,128]{3,2,1,0:T(8,128)S(1)} %get-tuple-element.106), channel_id=1, source_target_pairs={{0,64},{64,128},{128,192},{192,256},{256,320},{320,384},{384,448},... | collective-permute-start | bytes 147464 | tf_op jit(solution)/shard_map/ppermute | solution.py:436
  76.3 6.0 %collective-permute-start.9 = (f32[3,4,8,128]{3,2,1,0:T(8,128)S(1)}, f32[3,4,8,128]{3,2,1,0:T(8,128)S(1)}, u32[]{:S(2)}, u32[]{:S(2)}) collective-permute-start(f32[3,4,8,128]{3,2,1,0:T(8,128)S(1)} %get-tuple-element.107), channel_id=1, source_target_pairs={{64,0},{128,64},{192,128},{256,192},{320,256},{384,320},{448,384},... | collective-permute-start | bytes 147464 | tf_op jit(solution)/shard_map/ppermute | solution.py:436

commit v6 on v5

--- a/solution.py
+++ b/solution.py
@@ -9,6 +9,7 @@
 WENO_EPS = 1e-06
 SMOOTH_EPS = 0.01
 UNROLL_COEF = 2
+EVEN_TURNS, ODD_TURNS = (1, 1, -1, -1), (-1, -1, 1, 1)
 UNROLL_DEPTH = 2
 LANES = 128
 BX, BY = 8, 16
@@ -222,7 +223,7 @@
                 co_ref[n, z, g] = part
         return carry
 
-    lax.fori_loop(0, 4, column, 0)
+    lax.fori_loop(0, 4, column, 0, unroll=UNROLL_COEF)
 
 
 def apply_depth(c_ref, co_ref, scale_ref, out_ref, up_ref, dn_ref):
@@ -337,42 +338,32 @@
                 out_ref[gy * whole.shape[1] + gx, z] = whole[gy, gx]
 
 
-def slab_path(n_gx, n_gy):
-    position = {}
+def slab_line(n_gx, n_gy, turns):
+    gx, line = 0, []
     for gy in range(n_gy):
-        for step in range(n_gx):
-            gx = step if gy % 2 == 0 else n_gx - 1 - step
-            position[gy, gx] = gy * n_gx + step
-    return position
-
-
-def to_slabs(count, depth, position, *refs):
+        turn = turns[gy % len(turns)]
+        line += [(gy, (gx + turn * step) % n_gx) for step in range(n_gx)]
+        gx = (gx - turn) % n_gx
+    return line
+
+
+def to_slabs(count, depth, even_at, odd_at, *refs):
     odd_ref, ins, out_ref, scratch = refs[0], refs[1:-2], refs[-2], refs[-1]
     odd = odd_ref[0] == 1
     for n, ref in enumerate(ins):
         block = ref[...].reshape(BX * BY, LANES)
         scratch[...] = block.T
         for j in range(count):
-            at = position[j]
-            even_rows = scratch[pl.ds(depth * at, depth), :]
-            odd_rows = scratch[pl.ds(depth * (count - 1 - at), depth), :]
+            even_rows = scratch[pl.ds(depth * even_at[j], depth), :]
+            odd_rows = scratch[pl.ds(depth * odd_at[j], depth), :]
             out_ref[j, pl.ds(depth * n, depth), :] = jnp.where(odd, odd_rows, even_rows)
 
 
-def from_slabs(count, depth, position, odd_ref, in_ref, out_ref, scratch):
+def from_slabs(count, depth, even_at, odd_at, odd_ref, in_ref, out_ref, scratch):
     odd = odd_ref[0] == 1
-    for j in range(count):
-        at = position[j]
-        rows = in_ref[j]
-
-        @pl.when(odd)
-        def _():
-            scratch[pl.ds(depth * (count - 1 - at), depth), :] = rows
-
-        @pl.when(jnp.logical_not(odd))
-        def _():
-            scratch[pl.ds(depth * at, depth), :] = rows
-
+    for at in range(count):
+        even_rows, odd_rows = in_ref[even_at.index(at)], in_ref[odd_at.index(at)]
+        scratch[pl.ds(depth * at, depth), :] = jnp.where(odd, odd_rows, even_rows)
     out_ref[...] = scratch[...].T.reshape(BX, BY, LANES)
 
 
@@ -395,12 +386,13 @@
     count = n_gx * n_gy
     depth = LANES // count
     assert depth == 4
-    position = slab_path(n_gx, n_gy)
-    flat_position = [position[j // n_gx, j % n_gx] for j in range(count)]
+    even_line = slab_line(n_gx, n_gy, EVEN_TURNS)
+    odd_line = slab_line(n_gx, n_gy, ODD_TURNS)[::-1]
+    even_at = [even_line.index((j // n_gx, j % n_gx)) for j in range(count)]
+    odd_at = [odd_line.index((j // n_gx, j % n_gx)) for j in range(count)]
     order = []
     for gz in range(n_gz):
-        line = sorted(position, key=position.get, reverse=gz % 2 == 1)
-        order += [(gx * n_gy + gy) * n_gz + gz for gy, gx in line]
+        order += [(gx * n_gy + gy) * n_gz + gz for gy, gx in (odd_line if gz % 2 else even_line)]
     total = len(order)
     upward = [(order[i], order[(i + 1) % total]) for i in range(total)]
     downward = [(order[(i + 1) % total], order[i]) for i in range(total)]
@@ -440,7 +432,7 @@
         turn = pltpu.VMEM((LANES, LANES), F32)
 
         packed = call(
-            lambda *refs: to_slabs(count, depth, flat_position, *refs),
+            lambda *refs: to_slabs(count, depth, even_at, odd_at, *refs),
             near(count, 5 * depth, LANES),
             odd, section_second, section_middle, section_first, phi_start, cot_final,
             first=smem, far=True, scratch=[turn], name="to_slabs",
@@ -502,7 +494,7 @@
         slabs = call(finish, near(count, depth, LANES), c4, c3, own, lo, hi, acc, name="finish")
         slabs = lax.all_to_all(slabs, ("gy", "gx"), 0, 0)
         return call(
-            lambda *refs: from_slabs(count, depth, flat_position, *refs),
+            lambda *refs: from_slabs(count, depth, even_at, odd_at, *refs),
             like(BX, BY, LANES), odd, slabs, first=smem, scratch=[turn], name="from_slabs",
         )
 

time: 107 us -> 107 us (level)
  no operation moved by 1% of the time
where the time goes in v6:
time: 107 us; the launch traced here: 106 us
  blocking collectives  55.7 us (52%)
  starting transfers between devices  28.1 us (26%)
  Pallas kernels  11.3 us (11%)
  waiting for transfers between devices  10.9 us (10%)
    all_to_all x1, blocking collectives, shards(): packed = lax.all_to_all(packed, ('gy', 'gx'), 0, 0)  32.4 us
    all_to_all x1, blocking collectives, shards(): slabs = lax.all_to_all(slabs, ('gy', 'gx'), 0, 0)  23.3 us
    ppermute x5, starting transfers between devices, exchange(): lax.ppermute(up, everywhere, upward)  16 us
    ppermute x5, starting transfers between devices, exchange(): lax.ppermute(dn, everywhere, downward)  12.1 us
    pallas_call x13, Pallas kernels, call(): pl.pallas_call(kernel, out_shape=out_shape, in_specs=[first] + [vmem] * (...  11.3 us
    ppermute x5, waiting for transfers between devices, exchange(): lax.ppermute(dn, everywhere, downward)  10.9 us
  transfers between devices with their start and end apart: 10, of which 5 were waited for; matrix products, arithmetic and copies ran while one was open for 0% of the time, Pallas kernels for 8%

profile of v6, /device:TPU:6, one launch (start us, length us, event | category | flops | bytes accessed | tf_op | source)
XLA Modules:
  0.0 106.3 jit_solution(6963542525605838700)
XLA Ops:
  0.0 1.2 %to_slabs.1 = f32[32,20,128]{2,1,0:T(8,128)S(1)} custom-call(s32[1]{0:T(128)} %bitcast.refs_0_, f32[8,16,128]{2,1,0:T(8,128)} %refs_1_.1, f32[8,16,128]{2,1,0:T(8,128)} %refs_2_.1, f32[8,16,128]{2,1,0:T(8,128)} %refs_3_.1, f32[8,16,128]{2,1,0:T(8,128)} %refs_4_.1, f32[8,16,128]{2,1,0:T(8,128)} %refs_5_.1), custom_call_target="tpu_custom_call" | custom-call | tf_op jit(solution)/shard_map/to_slabs/pallas_call | solution.py:416
  1.2 32.4 %all_to_all.10.refs_0_ = f32[32,20,128]{2,1,0:T(8,128)S(1)} all-to-all(f32[32,20,128]{2,1,0:T(8,128)S(1)} %to_slabs.1), channel_id=1, replica_groups=mesh['gx'=8,'gy'=4,'gz'=16] {'gy','gx'}, dimensions={0} | all-to-all | bytes 655360 | tf_op jit(solution)/shard_map/all_to_all | solution.py:440
  33.8 3.7 %collective-permute-start = (f32[12,4,8,128]{3,2,1,0:T(8,128)S(1)}, f32[12,4,8,128]{3,2,1,0:T(8,128)S(1)}, u32[]{:S(2)}, u32[]{:S(2)}) collective-permute-start(f32[12,4,8,128]{3,2,1,0:T(8,128)S(1)} %get-tuple-element.58), channel_id=1, source_target_pairs={{0,64},{64,128},{128,192},{192,256},{256,320},{320,384},{384,448},... | collective-permute-start | bytes 589832 | tf_op jit(solution)/shard_map/ppermute | solution.py:428
  37.4 1.9 %collective-permute-start.1 = (f32[12,4,8,128]{3,2,1,0:T(8,128)S(1)}, f32[12,4,8,128]{3,2,1,0:T(8,128)S(1)}, u32[]{:S(2)}, u32[]{:S(2)}) collective-permute-start(f32[12,4,8,128]{3,2,1,0:T(8,128)S(1)} %get-tuple-element.59), channel_id=1, source_target_pairs={{64,0},{128,64},{192,128},{256,192},{320,256},{384,320},{448,384},... | collective-permute-start | bytes 589832 | tf_op jit(solution)/shard_map/ppermute | solution.py:428
  39.4 3.3 %coef_planes.1 = (f32[20,4,4,8,128]{4,3,2,1,0:T(8,128)S(1)}, f32[4,4,8,128]{3,2,1,0:T(8,128)S(1)}, f32[20,4,4,8,128]{4,3,2,1,0:T(8,128)S(1)}, f32[4,4,8,128]{3,2...) custom-call(f32[4,4,8,128]{3,2,1,0:T(8,128)S(1)} %get-tuple-element.57.refs_0_.f_ref, ...), custom_call_target="tpu_custom_call" | custom-call | tf_op jit(solution)/shard_map/coef_planes/pallas_call | solution.py:416
  42.7 2.3 %collective-permute-done.1.hi_ref = f32[12,4,8,128]{3,2,1,0:T(8,128)S(1)} collective-permute-done((f32[12,4,8,128]{3,2,1,0:T(8,128)S(1)}, f32[12,4,8,128]{3,2,1,0:T(8,128)S(1)}, u32[]{:S(2)}, u32[]{:S(2)}) %collective-permute-start.1) | collective-permute-done | bytes 196640 | tf_op jit(solution)/shard_map/ppermute | solution.py:428
  45.6 2.3 %collective-permute-start.2 = (f32[3,4,8,128]{3,2,1,0:T(8,128)S(1)}, f32[3,4,8,128]{3,2,1,0:T(8,128)S(1)}, u32[]{:S(2)}, u32[]{:S(2)}) collective-permute-start(f32[3,4,8,128]{3,2,1,0:T(8,128)S(1)} %get-tuple-element.72), channel_id=1, source_target_pairs={{0,64},{64,128},{128,192},{192,256},{256,320},{320,384},{384,448},... | collective-permute-start | bytes 147464 | tf_op jit(solution)/shard_map/ppermute | solution.py:428
  47.9 3.3 %collective-permute-start.3 = (f32[3,4,8,128]{3,2,1,0:T(8,128)S(1)}, f32[3,4,8,128]{3,2,1,0:T(8,128)S(1)}, u32[]{:S(2)}, u32[]{:S(2)}) collective-permute-start(f32[3,4,8,128]{3,2,1,0:T(8,128)S(1)} %get-tuple-element.73), channel_id=1, source_target_pairs={{64,0},{128,64},{192,128},{256,192},{320,256},{384,320},{448,384},... | collective-permute-start | bytes 147464 | tf_op jit(solution)/shard_map/ppermute | solution.py:428
  51.2 1.6 %window_one.1 = (f32[4,4,8,128]{3,2,1,0:T(8,128)S(1)}, f32[4,4,8,128]{3,2,1,0:T(8,128)S(1)}, f32[10,4,4,8,128]{4,3,2,1,0:T(8,128)S(1)}, f32[4,4,8,128]{3,2,1,0:T...) custom-call(f32[4,4,8,128]{3,2,1,0:T(8,128)S(1)} %get-tuple-element.65.c_, ...), custom_call_target="tpu_custom_call" | custom-call | tf_op jit(solution)/shard_map/window_one/pallas_call | solution.py:416
  52.8 1.0 collective-permute-done.3.refs_3_
  54.0 3.0 %collective-permute-start.4 = (f32[3,4,8,128]{3,2,1,0:T(8,128)S(1)}, f32[3,4,8,128]{3,2,1,0:T(8,128)S(1)}, u32[]{:S(2)}, u32[]{:S(2)}) collective-permute-start(f32[3,4,8,128]{3,2,1,0:T(8,128)S(1)} %get-tuple-element.83), channel_id=1, source_target_pairs={{0,64},{64,128},{128,192},{192,256},{256,320},{320,384},{384,448},... | collective-permute-start | bytes 147464 | tf_op jit(solution)/shard_map/ppermute | solution.py:428
  57.0 2.6 %collective-permute-start.5 = (f32[3,4,8,128]{3,2,1,0:T(8,128)S(1)}, f32[3,4,8,128]{3,2,1,0:T(8,128)S(1)}, u32[]{:S(2)}, u32[]{:S(2)}) collective-permute-start(f32[3,4,8,128]{3,2,1,0:T(8,128)S(1)} %get-tuple-element.84), channel_id=1, source_target_pairs={{64,0},{128,64},{192,128},{256,192},{320,256},{384,320},{448,384},... | collective-permute-start | bytes 147464 | tf_op jit(solution)/shard_map/ppermute | solution.py:428
  59.6 1.6 %window_two.1 = (f32[4,4,8,128]{3,2,1,0:T(8,128)S(1)}, f32[4,4,8,128]{3,2,1,0:T(8,128)S(1)}, f32[10,4,4,8,128]{4,3,2,1,0:T(8,128)S(1)}, f32[4,4,8,128]{3,2,1,0:T...) custom-call(f32[4,4,8,128]{3,2,1,0:T(8,128)S(1)} %get-tuple-element.76.c_, ...), custom_call_target="tpu_custom_call" | custom-call | tf_op jit(solution)/shard_map/window_two/pallas_call | solution.py:416
  61.2 1.7 %collective-permute-done.5.refs_4_ = f32[3,4,8,128]{3,2,1,0:T(8,128)S(1)} collective-permute-done((f32[3,4,8,128]{3,2,1,0:T(8,128)S(1)}, f32[3,4,8,128]{3,2,1,0:T(8,128)S(1)}, u32[]{:S(2)}, u32[]{:S(2)}) %collective-permute-start.5) | collective-permute-done | bytes 49184 | tf_op jit(solution)/shard_map/ppermute | solution.py:428
  63.1 3.9 %collective-permute-start.6 = (f32[3,4,8,128]{3,2,1,0:T(8,128)S(1)}, f32[3,4,8,128]{3,2,1,0:T(8,128)S(1)}, u32[]{:S(2)}, u32[]{:S(2)}) collective-permute-start(f32[3,4,8,128]{3,2,1,0:T(8,128)S(1)} %get-tuple-element.95), channel_id=1, source_target_pairs={{0,64},{64,128},{128,192},{192,256},{256,320},{320,384},{384,448},... | collective-permute-start | bytes 147464 | tf_op jit(solution)/shard_map/ppermute | solution.py:428
  67.0 1.9 %collective-permute-start.7 = (f32[3,4,8,128]{3,2,1,0:T(8,128)S(1)}, f32[3,4,8,128]{3,2,1,0:T(8,128)S(1)}, u32[]{:S(2)}, u32[]{:S(2)}) collective-permute-start(f32[3,4,8,128]{3,2,1,0:T(8,128)S(1)} %get-tuple-element.96), channel_id=1, source_target_pairs={{64,0},{128,64},{192,128},{256,192},{320,256},{384,320},{448,384},... | collective-permute-start | bytes 147464 | tf_op jit(solution)/shard_map/ppermute | solution.py:428
  68.9 1.1 %window_three.1 = (f32[4,4,8,128]{3,2,1,0:T(8,128)S(1)}, f32[4,4,8,128]{3,2,1,0:T(8,128)S(1)}, f32[10,4,4,8,128]{4,3,2,1,0:T(8,128)S(1)}, f32[4,4,8,128]{3,2,1,0:T(8,128)S(1)}, f32[4,4,8,128]{3,2,1,0:T(8,128)S(1)}) custom-call(f32[4,4,8,128]{3,2,1,0:T(8,128)S(1)} %get-tuple-element.87.c_ref.refs_0_.middle_ref, ...), custom_call_target="tpu_custom_call" | custom-call | tf_op jit(solution)/shard_map/window_three/pallas_call | solution.py:416
  70.0 2.9 %collective-permute-done.7.refs_3_ = f32[3,4,8,128]{3,2,1,0:T(8,128)S(1)} collective-permute-done((f32[3,4,8,128]{3,2,1,0:T(8,128)S(1)}, f32[3,4,8,128]{3,2,1,0:T(8,128)S(1)}, u32[]{:S(2)}, u32[]{:S(2)}) %collective-permute-start.7) | collective-permute-done | bytes 49184 | tf_op jit(solution)/shard_map/ppermute | solution.py:428
  73.1 3.1 %collective-permute-start.8 = (f32[3,4,8,128]{3,2,1,0:T(8,128)S(1)}, f32[3,4,8,128]{3,2,1,0:T(8,128)S(1)}, u32[]{:S(2)}, u32[]{:S(2)}) collective-permute-start(f32[3,4,8,128]{3,2,1,0:T(8,128)S(1)} %get-tuple-element.106), channel_id=1, source_target_pairs={{0,64},{64,128},{128,192},{192,256},{256,320},{320,384},{384,448},... | collective-permute-start | bytes 147464 | tf_op jit(solution)/shard_map/ppermute | solution.py:428
  76.2 2.4 %collective-permute-start.9 = (f32[3,4,8,128]{3,2,1,0:T(8,128)S(1)}, f32[3,4,8,128]{3,2,1,0:T(8,128)S(1)}, u32[]{:S(2)}, u32[]{:S(2)}) collective-permute-start(f32[3,4,8,128]{3,2,1,0:T(8,128)S(1)} %get-tuple-element.107), channel_id=1, source_target_pairs={{64,0},{128,64},{192,128},{256,192},{320,256},{384,320},{448,384},... | collective-permute-start | bytes 147464 | tf_op jit(solution)/shard_map/ppermute | solution.py:428
  78.7 0.6 window_four.1
  79.3 2.9 %collective-permute-done.9.hi_ref = f32[3,4,8,128]{3,2,1,0:T(8,128)S(1)} collective-permute-done((f32[3,4,8,128]{3,2,1,0:T(8,128)S(1)}, f32[3,4,8,128]{3,2,1,0:T(8,128)S(1)}, u32[]{:S(2)}, u32[]{:S(2)}) %collective-permute-start.9) | collective-permute-done | bytes 49184 | tf_op jit(solution)/shard_map/ppermute | solution.py:428
  82.3 23.3 %all_to_all.11.refs_1_ = f32[32,4,128]{2,1,0:T(4,128)S(1)} all-to-all(f32[32,4,128]{2,1,0:T(4,128)S(1)} %finish.1), channel_id=1, replica_groups=mesh['gx'=8,'gy'=4,'gz'=16] {'gy','gx'}, dimensions={0} | all-to-all | bytes 131072 | tf_op jit(solution)/shard_map/all_to_all | solution.py:495
  105.6 0.7 from_slabs.1
  (11 shorter events, 1.1 us)
Async XLA Ops:
  33.8 9.0 %collective-permute-start = (f32[12,4,8,128]{3,2,1,0:T(8,128)S(1)}, f32[12,4,8,128]{3,2,1,0:T(8,128)S(1)}, u32[]{:S(2)}, u32[]{:S(2)}) collective-permute-start(f32[12,4,8,128]{3,2,1,0:T(8,128)S(1)} %get-tuple-element.58), channel_id=1, source_target_pairs={{0,64},{64,128},{128,192},{192,256},{256,320},{320,384},{384,448},... | collective-permute-start | bytes 589832 | tf_op jit(solution)/shard_map/ppermute | solution.py:428
  37.4 7.6 %collective-permute-start.1 = (f32[12,4,8,128]{3,2,1,0:T(8,128)S(1)}, f32[12,4,8,128]{3,2,1,0:T(8,128)S(1)}, u32[]{:S(2)}, u32[]{:S(2)}) collective-permute-start(f32[12,4,8,128]{3,2,1,0:T(8,128)S(1)} %get-tuple-element.59), channel_id=1, source_target_pairs={{64,0},{128,64},{192,128},{256,192},{320,256},{384,320},{448,384},... | collective-permute-start | bytes 589832 | tf_op jit(solution)/shard_map/ppermute | solution.py:428
  45.6 7.2 %collective-permute-start.2 = (f32[3,4,8,128]{3,2,1,0:T(8,128)S(1)}, f32[3,4,8,128]{3,2,1,0:T(8,128)S(1)}, u32[]{:S(2)}, u32[]{:S(2)}) collective-permute-start(f32[3,4,8,128]{3,2,1,0:T(8,128)S(1)} %get-tuple-element.72), channel_id=1, source_target_pairs={{0,64},{64,128},{128,192},{192,256},{256,320},{320,384},{384,448},... | collective-permute-start | bytes 147464 | tf_op jit(solution)/shard_map/ppermute | solution.py:428
  47.9 6.0 %collective-permute-start.3 = (f32[3,4,8,128]{3,2,1,0:T(8,128)S(1)}, f32[3,4,8,128]{3,2,1,0:T(8,128)S(1)}, u32[]{:S(2)}, u32[]{:S(2)}) collective-permute-start(f32[3,4,8,128]{3,2,1,0:T(8,128)S(1)} %get-tuple-element.73), channel_id=1, source_target_pairs={{64,0},{128,64},{192,128},{256,192},{320,256},{384,320},{448,384},... | collective-permute-start | bytes 147464 | tf_op jit(solution)/shard_map/ppermute | solution.py:428
  54.0 7.2 %collective-permute-start.4 = (f32[3,4,8,128]{3,2,1,0:T(8,128)S(1)}, f32[3,4,8,128]{3,2,1,0:T(8,128)S(1)}, u32[]{:S(2)}, u32[]{:S(2)}) collective-permute-start(f32[3,4,8,128]{3,2,1,0:T(8,128)S(1)} %get-tuple-element.83), channel_id=1, source_target_pairs={{0,64},{64,128},{128,192},{192,256},{256,320},{320,384},{384,448},... | collective-permute-start | bytes 147464 | tf_op jit(solution)/shard_map/ppermute | solution.py:428
  57.0 6.0 %collective-permute-start.5 = (f32[3,4,8,128]{3,2,1,0:T(8,128)S(1)}, f32[3,4,8,128]{3,2,1,0:T(8,128)S(1)}, u32[]{:S(2)}, u32[]{:S(2)}) collective-permute-start(f32[3,4,8,128]{3,2,1,0:T(8,128)S(1)} %get-tuple-element.84), channel_id=1, source_target_pairs={{64,0},{128,64},{192,128},{256,192},{320,256},{384,320},{448,384},... | collective-permute-start | bytes 147464 | tf_op jit(solution)/shard_map/ppermute | solution.py:428
  63.1 7.0 %collective-permute-start.6 = (f32[3,4,8,128]{3,2,1,0:T(8,128)S(1)}, f32[3,4,8,128]{3,2,1,0:T(8,128)S(1)}, u32[]{:S(2)}, u32[]{:S(2)}) collective-permute-start(f32[3,4,8,128]{3,2,1,0:T(8,128)S(1)} %get-tuple-element.95), channel_id=1, source_target_pairs={{0,64},{64,128},{128,192},{192,256},{256,320},{320,384},{384,448},... | collective-permute-start | bytes 147464 | tf_op jit(solution)/shard_map/ppermute | solution.py:428
  67.0 6.0 %collective-permute-start.7 = (f32[3,4,8,128]{3,2,1,0:T(8,128)S(1)}, f32[3,4,8,128]{3,2,1,0:T(8,128)S(1)}, u32[]{:S(2)}, u32[]{:S(2)}) collective-permute-start(f32[3,4,8,128]{3,2,1,0:T(8,128)S(1)} %get-tuple-element.96), channel_id=1, source_target_pairs={{64,0},{128,64},{192,128},{256,192},{320,256},{384,320},{448,384},... | collective-permute-start | bytes 147464 | tf_op jit(solution)/shard_map/ppermute | solution.py:428
  73.1 6.2 %collective-permute-start.8 = (f32[3,4,8,128]{3,2,1,0:T(8,128)S(1)}, f32[3,4,8,128]{3,2,1,0:T(8,128)S(1)}, u32[]{:S(2)}, u32[]{:S(2)}) collective-permute-start(f32[3,4,8,128]{3,2,1,0:T(8,128)S(1)} %get-tuple-element.106), channel_id=1, source_target_pairs={{0,64},{64,128},{128,192},{192,256},{256,320},{320,384},{384,448},... | collective-permute-start | bytes 147464 | tf_op jit(solution)/shard_map/ppermute | solution.py:428
  76.2 6.0 %collective-permute-start.9 = (f32[3,4,8,128]{3,2,1,0:T(8,128)S(1)}, f32[3,4,8,128]{3,2,1,0:T(8,128)S(1)}, u32[]{:S(2)}, u32[]{:S(2)}) collective-permute-start(f32[3,4,8,128]{3,2,1,0:T(8,128)S(1)} %get-tuple-element.107), channel_id=1, source_target_pairs={{64,0},{128,64},{192,128},{256,192},{320,256},{384,320},{448,384},... | collective-permute-start | bytes 147464 | tf_op jit(solution)/shard_map/ppermute | solution.py:428

commit v7 on v6

--- a/solution.py
+++ b/solution.py
@@ -9,7 +9,7 @@
 WENO_EPS = 1e-06
 SMOOTH_EPS = 0.01
 UNROLL_COEF = 2
-EVEN_TURNS, ODD_TURNS = (1, 1, -1, -1), (-1, -1, 1, 1)
+EVEN_TURNS, ODD_TURNS, FIRST_GX = (-1, 1, -1, 1), (1, 1, -1, -1), 7
 UNROLL_DEPTH = 2
 LANES = 128
 BX, BY = 8, 16
@@ -335,11 +335,11 @@
         whole = (acc_in[z] + back) + (first_ref[z] + middle_ref[z])
         for gy in range(whole.shape[0]):
             for gx in range(whole.shape[1]):
-                out_ref[gy * whole.shape[1] + gx, z] = whole[gy, gx]
-
-
-def slab_line(n_gx, n_gy, turns):
-    gx, line = 0, []
+                out_ref[gx * whole.shape[0] + gy, z] = whole[gy, gx]
+
+
+def slab_line(n_gx, n_gy, turns, gx):
+    line = []
     for gy in range(n_gy):
         turn = turns[gy % len(turns)]
         line += [(gy, (gx + turn * step) % n_gx) for step in range(n_gx)]
@@ -372,7 +372,7 @@
     for n, out in enumerate(outs):
         for z in range(4):
             for gy in range(n_gy):
-                rows = in_ref[pl.ds(gy * n_gx, n_gx), 4 * n + z, :]
+                rows = in_ref[pl.ds(gy, n_gx, stride=n_gy), 4 * n + z, :]
                 out[z, gy] = rows
                 if n < 4:
                     if z >= 1:
@@ -386,10 +386,10 @@
     count = n_gx * n_gy
     depth = LANES // count
     assert depth == 4
-    even_line = slab_line(n_gx, n_gy, EVEN_TURNS)
-    odd_line = slab_line(n_gx, n_gy, ODD_TURNS)[::-1]
-    even_at = [even_line.index((j // n_gx, j % n_gx)) for j in range(count)]
-    odd_at = [odd_line.index((j // n_gx, j % n_gx)) for j in range(count)]
+    even_line = slab_line(n_gx, n_gy, EVEN_TURNS, FIRST_GX % n_gx)
+    odd_line = slab_line(n_gx, n_gy, ODD_TURNS, FIRST_GX % n_gx)[::-1]
+    even_at = [even_line.index((j % n_gy, j // n_gy)) for j in range(count)]
+    odd_at = [odd_line.index((j % n_gy, j // n_gy)) for j in range(count)]
     order = []
     for gz in range(n_gz):
         order += [(gx * n_gy + gy) * n_gz + gz for gy, gx in (odd_line if gz % 2 else even_line)]
@@ -437,7 +437,7 @@
             odd, section_second, section_middle, section_first, phi_start, cot_final,
             first=smem, far=True, scratch=[turn], name="to_slabs",
         )
-        packed = lax.all_to_all(packed, ("gy", "gx"), 0, 0)
+        packed = lax.all_to_all(packed, ("gx", "gy"), 0, 0)
         *fields, rim_up, rim_dn = call(
             lambda *refs: unpack(n_gy, n_gx, *refs),
             [near(*slab)] * 5 + [near(12, *slab[1:])] * 2,
@@ -492,7 +492,7 @@
             window_four, window_out, c4, flat3a, flat3b, scale, pc, part, acc, name="window_four",
         )
         slabs = call(finish, near(count, depth, LANES), c4, c3, own, lo, hi, acc, name="finish")
-        slabs = lax.all_to_all(slabs, ("gy", "gx"), 0, 0)
+        slabs = lax.all_to_all(slabs, ("gx", "gy"), 0, 0)
         return call(
             lambda *refs: from_slabs(count, depth, even_at, odd_at, *refs),
             like(BX, BY, LANES), odd, slabs, first=smem, scratch=[turn], name="from_slabs",

time: 107 us -> 106 us (level)
  blocking collectives: 55.7 us -> 53.7 us
  starting transfers between devices: 28.1 us -> 30 us
    ppermute x5, starting transfers between devices: 12.1 us -> 17.1 us  [exchange(): lax.ppermute(dn, everywhere, downward)]
    ppermute x5, starting transfers between devices: 16 us -> 12.8 us  [exchange(): lax.ppermute(up, everywhere, upward)]
    all_to_all x2, blocking collectives: 55.7 us -> 53.7 us  [the longest x1 32.5 us: shards(): packed = lax.all_to_all(packed, ('gx', 'gy'), 0, 0)]
where the time goes in v7:
time: 106 us
  blocking collectives  53.7 us (51%)
  starting transfers between devices  30 us (28%)
  Pallas kernels  11.3 us (11%)
  waiting for transfers between devices  10.4 us (10%)
    all_to_all x1, blocking collectives, shards(): packed = lax.all_to_all(packed, ('gx', 'gy'), 0, 0)  32.5 us
    all_to_all x1, blocking collectives, shards(): slabs = lax.all_to_all(slabs, ('gx', 'gy'), 0, 0)  21.2 us
    ppermute x5, starting transfers between devices, exchange(): lax.ppermute(dn, everywhere, downward)  17.1 us
    ppermute x5, starting transfers between devices, exchange(): lax.ppermute(up, everywhere, upward)  12.8 us
    pallas_call x13, Pallas kernels, call(): pl.pallas_call(kernel, out_shape=out_shape, in_specs=[first] + [vmem] * (...  11.3 us
    ppermute x5, waiting for transfers between devices, exchange(): lax.ppermute(dn, everywhere, downward)  10.4 us
  transfers between devices with their start and end apart: 10, of which 5 were waited for; matrix products, arithmetic and copies ran while one was open for 0% of the time, Pallas kernels for 8%

profile of v7, /device:TPU:6, one launch (start us, length us, event | category | flops | bytes accessed | tf_op | source)
XLA Modules:
  0.0 105.6 jit_solution(2837107575574594328)
XLA Ops:
  0.0 1.2 %to_slabs.1 = f32[32,20,128]{2,1,0:T(8,128)S(1)} custom-call(s32[1]{0:T(128)} %bitcast.refs_0_, f32[8,16,128]{2,1,0:T(8,128)} %refs_1_.1, f32[8,16,128]{2,1,0:T(8,128)} %refs_2_.1, f32[8,16,128]{2,1,0:T(8,128)} %refs_3_.1, f32[8,16,128]{2,1,0:T(8,128)} %refs_4_.1, f32[8,16,128]{2,1,0:T(8,128)} %refs_5_.1), custom_call_target="tpu_custom_call" | custom-call | tf_op jit(solution)/shard_map/to_slabs/pallas_call | solution.py:416
  1.2 32.5 %all_to_all.10.refs_0_ = f32[32,20,128]{2,1,0:T(8,128)S(1)} all-to-all(f32[32,20,128]{2,1,0:T(8,128)S(1)} %to_slabs.1), channel_id=1, replica_groups=mesh['gx'=8,'gy'=4,'gz'=16] {'gx','gy'}, dimensions={0} | all-to-all | bytes 655360 | tf_op jit(solution)/shard_map/all_to_all | solution.py:440
  33.8 4.7 %collective-permute-start = (f32[12,4,8,128]{3,2,1,0:T(8,128)S(1)}, f32[12,4,8,128]{3,2,1,0:T(8,128)S(1)}, u32[]{:S(2)}, u32[]{:S(2)}) collective-permute-start(f32[12,4,8,128]{3,2,1,0:T(8,128)S(1)} %get-tuple-element.58), channel_id=1, source_target_pairs={{448,384},{384,320},{320,256},{256,192},{192,128},{128,64},{64,0},... | collective-permute-start | bytes 589832 | tf_op jit(solution)/shard_map/ppermute | solution.py:428
  38.5 1.9 %collective-permute-start.1 = (f32[12,4,8,128]{3,2,1,0:T(8,128)S(1)}, f32[12,4,8,128]{3,2,1,0:T(8,128)S(1)}, u32[]{:S(2)}, u32[]{:S(2)}) collective-permute-start(f32[12,4,8,128]{3,2,1,0:T(8,128)S(1)} %get-tuple-element.59), channel_id=1, source_target_pairs={{384,448},{320,384},{256,320},{192,256},{128,192},{64,128},{0,64},... | collective-permute-start | bytes 589832 | tf_op jit(solution)/shard_map/ppermute | solution.py:428
  40.4 3.3 %coef_planes.1 = (f32[20,4,4,8,128]{4,3,2,1,0:T(8,128)S(1)}, f32[4,4,8,128]{3,2,1,0:T(8,128)S(1)}, f32[20,4,4,8,128]{4,3,2,1,0:T(8,128)S(1)}, f32[4,4,8,128]{3,2...) custom-call(f32[4,4,8,128]{3,2,1,0:T(8,128)S(1)} %get-tuple-element.57.refs_0_.f_ref, ...), custom_call_target="tpu_custom_call" | custom-call | tf_op jit(solution)/shard_map/coef_planes/pallas_call | solution.py:416
  43.8 3.2 %collective-permute-done.1.hi_ref = f32[12,4,8,128]{3,2,1,0:T(8,128)S(1)} collective-permute-done((f32[12,4,8,128]{3,2,1,0:T(8,128)S(1)}, f32[12,4,8,128]{3,2,1,0:T(8,128)S(1)}, u32[]{:S(2)}, u32[]{:S(2)}) %collective-permute-start.1) | collective-permute-done | bytes 196640 | tf_op jit(solution)/shard_map/ppermute | solution.py:428
  47.6 2.0 %collective-permute-start.2 = (f32[3,4,8,128]{3,2,1,0:T(8,128)S(1)}, f32[3,4,8,128]{3,2,1,0:T(8,128)S(1)}, u32[]{:S(2)}, u32[]{:S(2)}) collective-permute-start(f32[3,4,8,128]{3,2,1,0:T(8,128)S(1)} %get-tuple-element.72), channel_id=1, source_target_pairs={{448,384},{384,320},{320,256},{256,192},{192,128},{128,64},{64,0},... | collective-permute-start | bytes 147464 | tf_op jit(solution)/shard_map/ppermute | solution.py:428
  49.5 3.9 %collective-permute-start.3 = (f32[3,4,8,128]{3,2,1,0:T(8,128)S(1)}, f32[3,4,8,128]{3,2,1,0:T(8,128)S(1)}, u32[]{:S(2)}, u32[]{:S(2)}) collective-permute-start(f32[3,4,8,128]{3,2,1,0:T(8,128)S(1)} %get-tuple-element.73), channel_id=1, source_target_pairs={{384,448},{320,384},{256,320},{192,256},{128,192},{64,128},{0,64},... | collective-permute-start | bytes 147464 | tf_op jit(solution)/shard_map/ppermute | solution.py:428
  53.4 1.6 %window_one.1 = (f32[4,4,8,128]{3,2,1,0:T(8,128)S(1)}, f32[4,4,8,128]{3,2,1,0:T(8,128)S(1)}, f32[10,4,4,8,128]{4,3,2,1,0:T(8,128)S(1)}, f32[4,4,8,128]{3,2,1,0:T...) custom-call(f32[4,4,8,128]{3,2,1,0:T(8,128)S(1)} %get-tuple-element.65.c_, ...), custom_call_target="tpu_custom_call" | custom-call | tf_op jit(solution)/shard_map/window_one/pallas_call | solution.py:416
  55.1 1.3 %collective-permute-done.3.refs_3_ = f32[3,4,8,128]{3,2,1,0:T(8,128)S(1)} collective-permute-done((f32[3,4,8,128]{3,2,1,0:T(8,128)S(1)}, f32[3,4,8,128]{3,2,1,0:T(8,128)S(1)}, u32[]{:S(2)}, u32[]{:S(2)}) %collective-permute-start.3) | collective-permute-done | bytes 49184 | tf_op jit(solution)/shard_map/ppermute | solution.py:428
  56.5 1.9 %collective-permute-start.4 = (f32[3,4,8,128]{3,2,1,0:T(8,128)S(1)}, f32[3,4,8,128]{3,2,1,0:T(8,128)S(1)}, u32[]{:S(2)}, u32[]{:S(2)}) collective-permute-start(f32[3,4,8,128]{3,2,1,0:T(8,128)S(1)} %get-tuple-element.83), channel_id=1, source_target_pairs={{448,384},{384,320},{320,256},{256,192},{192,128},{128,64},{64,0},... | collective-permute-start | bytes 147464 | tf_op jit(solution)/shard_map/ppermute | solution.py:428
  58.5 3.9 %collective-permute-start.5 = (f32[3,4,8,128]{3,2,1,0:T(8,128)S(1)}, f32[3,4,8,128]{3,2,1,0:T(8,128)S(1)}, u32[]{:S(2)}, u32[]{:S(2)}) collective-permute-start(f32[3,4,8,128]{3,2,1,0:T(8,128)S(1)} %get-tuple-element.84), channel_id=1, source_target_pairs={{384,448},{320,384},{256,320},{192,256},{128,192},{64,128},{0,64},... | collective-permute-start | bytes 147464 | tf_op jit(solution)/shard_map/ppermute | solution.py:428
  62.4 1.6 %window_two.1 = (f32[4,4,8,128]{3,2,1,0:T(8,128)S(1)}, f32[4,4,8,128]{3,2,1,0:T(8,128)S(1)}, f32[10,4,4,8,128]{4,3,2,1,0:T(8,128)S(1)}, f32[4,4,8,128]{3,2,1,0:T...) custom-call(f32[4,4,8,128]{3,2,1,0:T(8,128)S(1)} %get-tuple-element.76.c_, ...), custom_call_target="tpu_custom_call" | custom-call | tf_op jit(solution)/shard_map/window_two/pallas_call | solution.py:416
  64.1 1.3 %collective-permute-done.5.refs_4_ = f32[3,4,8,128]{3,2,1,0:T(8,128)S(1)} collective-permute-done((f32[3,4,8,128]{3,2,1,0:T(8,128)S(1)}, f32[3,4,8,128]{3,2,1,0:T(8,128)S(1)}, u32[]{:S(2)}, u32[]{:S(2)}) %collective-permute-start.5) | collective-permute-done | bytes 49184 | tf_op jit(solution)/shard_map/ppermute | solution.py:428
  65.5 1.9 %collective-permute-start.6 = (f32[3,4,8,128]{3,2,1,0:T(8,128)S(1)}, f32[3,4,8,128]{3,2,1,0:T(8,128)S(1)}, u32[]{:S(2)}, u32[]{:S(2)}) collective-permute-start(f32[3,4,8,128]{3,2,1,0:T(8,128)S(1)} %get-tuple-element.95), channel_id=1, source_target_pairs={{448,384},{384,320},{320,256},{256,192},{192,128},{128,64},{64,0},... | collective-permute-start | bytes 147464 | tf_op jit(solution)/shard_map/ppermute | solution.py:428
  67.4 3.9 %collective-permute-start.7 = (f32[3,4,8,128]{3,2,1,0:T(8,128)S(1)}, f32[3,4,8,128]{3,2,1,0:T(8,128)S(1)}, u32[]{:S(2)}, u32[]{:S(2)}) collective-permute-start(f32[3,4,8,128]{3,2,1,0:T(8,128)S(1)} %get-tuple-element.96), channel_id=1, source_target_pairs={{384,448},{320,384},{256,320},{192,256},{128,192},{64,128},{0,64},... | collective-permute-start | bytes 147464 | tf_op jit(solution)/shard_map/ppermute | solution.py:428
  71.3 1.1 %window_three.1 = (f32[4,4,8,128]{3,2,1,0:T(8,128)S(1)}, f32[4,4,8,128]{3,2,1,0:T(8,128)S(1)}, f32[10,4,4,8,128]{4,3,2,1,0:T(8,128)S(1)}, f32[4,4,8,128]{3,2,1,0:T(8,128)S(1)}, f32[4,4,8,128]{3,2,1,0:T(8,128)S(1)}) custom-call(f32[4,4,8,128]{3,2,1,0:T(8,128)S(1)} %get-tuple-element.87.c_ref.refs_0_.middle_ref, ...), custom_call_target="tpu_custom_call" | custom-call | tf_op jit(solution)/shard_map/window_three/pallas_call | solution.py:416
  72.4 1.8 %collective-permute-done.7.refs_3_ = f32[3,4,8,128]{3,2,1,0:T(8,128)S(1)} collective-permute-done((f32[3,4,8,128]{3,2,1,0:T(8,128)S(1)}, f32[3,4,8,128]{3,2,1,0:T(8,128)S(1)}, u32[]{:S(2)}, u32[]{:S(2)}) %collective-permute-start.7) | collective-permute-done | bytes 49184 | tf_op jit(solution)/shard_map/ppermute | solution.py:428
  74.4 2.3 %collective-permute-start.8 = (f32[3,4,8,128]{3,2,1,0:T(8,128)S(1)}, f32[3,4,8,128]{3,2,1,0:T(8,128)S(1)}, u32[]{:S(2)}, u32[]{:S(2)}) collective-permute-start(f32[3,4,8,128]{3,2,1,0:T(8,128)S(1)} %get-tuple-element.106), channel_id=1, source_target_pairs={{448,384},{384,320},{320,256},{256,192},{192,128},{128,64},{64,0},... | collective-permute-start | bytes 147464 | tf_op jit(solution)/shard_map/ppermute | solution.py:428
  76.7 3.5 %collective-permute-start.9 = (f32[3,4,8,128]{3,2,1,0:T(8,128)S(1)}, f32[3,4,8,128]{3,2,1,0:T(8,128)S(1)}, u32[]{:S(2)}, u32[]{:S(2)}) collective-permute-start(f32[3,4,8,128]{3,2,1,0:T(8,128)S(1)} %get-tuple-element.107), channel_id=1, source_target_pairs={{384,448},{320,384},{256,320},{192,256},{128,192},{64,128},{0,64},... | collective-permute-start | bytes 147464 | tf_op jit(solution)/shard_map/ppermute | solution.py:428
  80.3 0.6 window_four.1
  80.9 2.8 %collective-permute-done.9.hi_ref = f32[3,4,8,128]{3,2,1,0:T(8,128)S(1)} collective-permute-done((f32[3,4,8,128]{3,2,1,0:T(8,128)S(1)}, f32[3,4,8,128]{3,2,1,0:T(8,128)S(1)}, u32[]{:S(2)}, u32[]{:S(2)}) %collective-permute-start.9) | collective-permute-done | bytes 49184 | tf_op jit(solution)/shard_map/ppermute | solution.py:428
  83.7 21.2 %all_to_all.11.refs_1_ = f32[32,4,128]{2,1,0:T(4,128)S(1)} all-to-all(f32[32,4,128]{2,1,0:T(4,128)S(1)} %finish.1), channel_id=1, replica_groups=mesh['gx'=8,'gy'=4,'gz'=16] {'gx','gy'}, dimensions={0} | all-to-all | bytes 131072 | tf_op jit(solution)/shard_map/all_to_all | solution.py:495
  104.9 0.7 from_slabs.1
  (11 shorter events, 1.1 us)
Async XLA Ops:
  33.8 9.9 %collective-permute-start = (f32[12,4,8,128]{3,2,1,0:T(8,128)S(1)}, f32[12,4,8,128]{3,2,1,0:T(8,128)S(1)}, u32[]{:S(2)}, u32[]{:S(2)}) collective-permute-start(f32[12,4,8,128]{3,2,1,0:T(8,128)S(1)} %get-tuple-element.58), channel_id=1, source_target_pairs={{448,384},{384,320},{320,256},{256,192},{192,128},{128,64},{64,0},... | collective-permute-start | bytes 589832 | tf_op jit(solution)/shard_map/ppermute | solution.py:428
  38.5 8.5 %collective-permute-start.1 = (f32[12,4,8,128]{3,2,1,0:T(8,128)S(1)}, f32[12,4,8,128]{3,2,1,0:T(8,128)S(1)}, u32[]{:S(2)}, u32[]{:S(2)}) collective-permute-start(f32[12,4,8,128]{3,2,1,0:T(8,128)S(1)} %get-tuple-element.59), channel_id=1, source_target_pairs={{384,448},{320,384},{256,320},{192,256},{128,192},{64,128},{0,64},... | collective-permute-start | bytes 589832 | tf_op jit(solution)/shard_map/ppermute | solution.py:428
  47.6 7.5 %collective-permute-start.2 = (f32[3,4,8,128]{3,2,1,0:T(8,128)S(1)}, f32[3,4,8,128]{3,2,1,0:T(8,128)S(1)}, u32[]{:S(2)}, u32[]{:S(2)}) collective-permute-start(f32[3,4,8,128]{3,2,1,0:T(8,128)S(1)} %get-tuple-element.72), channel_id=1, source_target_pairs={{448,384},{384,320},{320,256},{256,192},{192,128},{128,64},{64,0},... | collective-permute-start | bytes 147464 | tf_op jit(solution)/shard_map/ppermute | solution.py:428
  49.5 6.9 %collective-permute-start.3 = (f32[3,4,8,128]{3,2,1,0:T(8,128)S(1)}, f32[3,4,8,128]{3,2,1,0:T(8,128)S(1)}, u32[]{:S(2)}, u32[]{:S(2)}) collective-permute-start(f32[3,4,8,128]{3,2,1,0:T(8,128)S(1)} %get-tuple-element.73), channel_id=1, source_target_pairs={{384,448},{320,384},{256,320},{192,256},{128,192},{64,128},{0,64},... | collective-permute-start | bytes 147464 | tf_op jit(solution)/shard_map/ppermute | solution.py:428
  56.5 7.5 %collective-permute-start.4 = (f32[3,4,8,128]{3,2,1,0:T(8,128)S(1)}, f32[3,4,8,128]{3,2,1,0:T(8,128)S(1)}, u32[]{:S(2)}, u32[]{:S(2)}) collective-permute-start(f32[3,4,8,128]{3,2,1,0:T(8,128)S(1)} %get-tuple-element.83), channel_id=1, source_target_pairs={{448,384},{384,320},{320,256},{256,192},{192,128},{128,64},{64,0},... | collective-permute-start | bytes 147464 | tf_op jit(solution)/shard_map/ppermute | solution.py:428
  58.5 6.9 %collective-permute-start.5 = (f32[3,4,8,128]{3,2,1,0:T(8,128)S(1)}, f32[3,4,8,128]{3,2,1,0:T(8,128)S(1)}, u32[]{:S(2)}, u32[]{:S(2)}) collective-permute-start(f32[3,4,8,128]{3,2,1,0:T(8,128)S(1)} %get-tuple-element.84), channel_id=1, source_target_pairs={{384,448},{320,384},{256,320},{192,256},{128,192},{64,128},{0,64},... | collective-permute-start | bytes 147464 | tf_op jit(solution)/shard_map/ppermute | solution.py:428
  65.5 7.0 %collective-permute-start.6 = (f32[3,4,8,128]{3,2,1,0:T(8,128)S(1)}, f32[3,4,8,128]{3,2,1,0:T(8,128)S(1)}, u32[]{:S(2)}, u32[]{:S(2)}) collective-permute-start(f32[3,4,8,128]{3,2,1,0:T(8,128)S(1)} %get-tuple-element.95), channel_id=1, source_target_pairs={{448,384},{384,320},{320,256},{256,192},{192,128},{128,64},{64,0},... | collective-permute-start | bytes 147464 | tf_op jit(solution)/shard_map/ppermute | solution.py:428
  67.4 6.9 %collective-permute-start.7 = (f32[3,4,8,128]{3,2,1,0:T(8,128)S(1)}, f32[3,4,8,128]{3,2,1,0:T(8,128)S(1)}, u32[]{:S(2)}, u32[]{:S(2)}) collective-permute-start(f32[3,4,8,128]{3,2,1,0:T(8,128)S(1)} %get-tuple-element.96), channel_id=1, source_target_pairs={{384,448},{320,384},{256,320},{192,256},{128,192},{64,128},{0,64},... | collective-permute-start | bytes 147464 | tf_op jit(solution)/shard_map/ppermute | solution.py:428
  74.4 6.5 %collective-permute-start.8 = (f32[3,4,8,128]{3,2,1,0:T(8,128)S(1)}, f32[3,4,8,128]{3,2,1,0:T(8,128)S(1)}, u32[]{:S(2)}, u32[]{:S(2)}) collective-permute-start(f32[3,4,8,128]{3,2,1,0:T(8,128)S(1)} %get-tuple-element.106), channel_id=1, source_target_pairs={{448,384},{384,320},{320,256},{256,192},{192,128},{128,64},{64,0},... | collective-permute-start | bytes 147464 | tf_op jit(solution)/shard_map/ppermute | solution.py:428
  76.7 6.9 %collective-permute-start.9 = (f32[3,4,8,128]{3,2,1,0:T(8,128)S(1)}, f32[3,4,8,128]{3,2,1,0:T(8,128)S(1)}, u32[]{:S(2)}, u32[]{:S(2)}) collective-permute-start(f32[3,4,8,128]{3,2,1,0:T(8,128)S(1)} %get-tuple-element.107), channel_id=1, source_target_pairs={{384,448},{320,384},{256,320},{192,256},{128,192},{64,128},{0,64},... | collective-permute-start | bytes 147464 | tf_op jit(solution)/shard_map/ppermute | solution.py:428

commit v8 on v7

--- a/solution.py
+++ b/solution.py
@@ -200,7 +200,7 @@
     lax.fori_loop(0, count, plane, 0, unroll=UNROLL_COEF)
 
 
-def coef_depth(section, f_ref, lo_ref, hi_ref, phi_ref, sum_ref, co_ref, scale_ref, pc_ref):
+def coef_depth(section, f_ref, lo_ref, hi_ref, phi_ref, sum_ref, co_ref, scale_ref, pc_ref, unroll=2):
     def column(g, carry):
         f = (
             [lo_ref[3 * section + i, g] for i in range(3)]
@@ -223,7 +223,7 @@
                 co_ref[n, z, g] = part
         return carry
 
-    lax.fori_loop(0, 4, column, 0, unroll=UNROLL_COEF)
+    lax.fori_loop(0, 4, column, 0, unroll=unroll)
 
 
 def apply_depth(c_ref, co_ref, scale_ref, out_ref, up_ref, dn_ref):
@@ -293,7 +293,7 @@
 
 
 def first_stage(f_ref, lo_ref, hi_ref, phi_ref, sum_ref, cot_ref, c_ref, part_ref, up_ref, dn_ref, scale_ref, pc_ref, co_ref):
-    coef_depth(0, f_ref, lo_ref, hi_ref, phi_ref, sum_ref, co_ref, scale_ref, pc_ref)
+    coef_depth(0, f_ref, lo_ref, hi_ref, phi_ref, sum_ref, co_ref, scale_ref, pc_ref, unroll=4)
     c_ref[...] = 0.5 * cot_ref[...]
     apply_depth(c_ref, co_ref, scale_ref, part_ref, up_ref, dn_ref)
 
@@ -348,10 +348,15 @@
 
 
 def to_slabs(count, depth, even_at, odd_at, *refs):
-    odd_ref, ins, out_ref, scratch = refs[0], refs[1:-2], refs[-2], refs[-1]
+    odd_ref, ins, out_ref = refs[0], refs[1:-4], refs[-4]
+    scratch, bricks, sems = refs[-3:]
+    copies = [pltpu.make_async_copy(ref, bricks.at[n], sems.at[n]) for n, ref in enumerate(ins)]
+    for copy in copies:
+        copy.start()
     odd = odd_ref[0] == 1
-    for n, ref in enumerate(ins):
-        block = ref[...].reshape(BX * BY, LANES)
+    for n, copy in enumerate(copies):
+        copy.wait()
+        block = bricks[n].reshape(BX * BY, LANES)
         scratch[...] = block.T
         for j in range(count):
             even_rows = scratch[pl.ds(depth * even_at[j], depth), :]
@@ -416,7 +421,7 @@
         return pl.pallas_call(
             kernel,
             out_shape=out_shape,
-            in_specs=[first] + [vmem] * (len(args) - 1),
+            in_specs=[first] + [pl.BlockSpec(memory_space=pltpu.HBM) if far else vmem] * (len(args) - 1),
             out_specs=[vmem] * len(out_shape) if many else vmem,
             scratch_shapes=list(scratch),
             compiler_params=pltpu.CompilerParams(vmem_limit_bytes=8 << 20),
@@ -435,7 +440,8 @@
             lambda *refs: to_slabs(count, depth, even_at, odd_at, *refs),
             near(count, 5 * depth, LANES),
             odd, section_second, section_middle, section_first, phi_start, cot_final,
-            first=smem, far=True, scratch=[turn], name="to_slabs",
+            first=smem, far=True, name="to_slabs",
+            scratch=[turn, pltpu.VMEM((5, BX, BY, LANES), F32), pltpu.SemaphoreType.DMA((5,))],
         )
         packed = lax.all_to_all(packed, ("gx", "gy"), 0, 0)
         *fields, rim_up, rim_dn = call(

time: 106 us -> 106 us (level)
  no operation moved by 1% of the time
where the time goes in v8:
time: 106 us
  blocking collectives  53.7 us (51%)
  starting transfers between devices  30 us (28%)
  Pallas kernels  11.6 us (11%)
  waiting for transfers between devices  10.4 us (10%)
    all_to_all x1, blocking collectives, shards(): packed = lax.all_to_all(packed, ('gx', 'gy'), 0, 0)  32.5 us
    all_to_all x1, blocking collectives, shards(): slabs = lax.all_to_all(slabs, ('gx', 'gy'), 0, 0)  21.2 us
    ppermute x5, starting transfers between devices, exchange(): lax.ppermute(dn, everywhere, downward)  17.1 us
    ppermute x5, starting transfers between devices, exchange(): lax.ppermute(up, everywhere, upward)  12.8 us
    pallas_call x13, Pallas kernels, call(): pl.pallas_call(kernel, out_shape=out_shape, in_specs=[first] + [pl.BlockS...  11.6 us
    ppermute x5, waiting for transfers between devices, exchange(): lax.ppermute(dn, everywhere, downward)  10.4 us
  transfers between devices with their start and end apart: 10, of which 5 were waited for; matrix products, arithmetic and copies ran while one was open for 0% of the time, Pallas kernels for 8%

profile of v8, /device:TPU:6, one launch (start us, length us, event | category | flops | bytes accessed | tf_op | source)
XLA Modules:
  0.0 105.9 jit_solution(2536652499876501114)
XLA Ops:
  0.0 1.5 %to_slabs.1 = f32[32,20,128]{2,1,0:T(8,128)S(1)} custom-call(s32[1]{0:T(128)} %bitcast.refs_0_, f32[8,16,128]{2,1,0:T(8,128)} %refs_1_.1, f32[8,16,128]{2,1,0:T(8,128)} %refs_2_.1, f32[8,16,128]{2,1,0:T(8,128)} %refs_3_.1, f32[8,16,128]{2,1,0:T(8,128)} %refs_4_.1, f32[8,16,128]{2,1,0:T(8,128)} %refs_5_.1), custom_call_target="tpu_custom_call" | custom-call | tf_op jit(solution)/shard_map/to_slabs/pallas_call | solution.py:421
  1.5 32.5 %all_to_all.10.refs_0_ = f32[32,20,128]{2,1,0:T(8,128)S(1)} all-to-all(f32[32,20,128]{2,1,0:T(8,128)S(1)} %to_slabs.1), channel_id=1, replica_groups=mesh['gx'=8,'gy'=4,'gz'=16] {'gx','gy'}, dimensions={0} | all-to-all | bytes 655360 | tf_op jit(solution)/shard_map/all_to_all | solution.py:446
  34.1 4.7 %collective-permute-start = (f32[12,4,8,128]{3,2,1,0:T(8,128)S(1)}, f32[12,4,8,128]{3,2,1,0:T(8,128)S(1)}, u32[]{:S(2)}, u32[]{:S(2)}) collective-permute-start(f32[12,4,8,128]{3,2,1,0:T(8,128)S(1)} %get-tuple-element.58), channel_id=1, source_target_pairs={{448,384},{384,320},{320,256},{256,192},{192,128},{128,64},{64,0},... | collective-permute-start | bytes 589832 | tf_op jit(solution)/shard_map/ppermute | solution.py:433
  38.8 1.9 %collective-permute-start.1 = (f32[12,4,8,128]{3,2,1,0:T(8,128)S(1)}, f32[12,4,8,128]{3,2,1,0:T(8,128)S(1)}, u32[]{:S(2)}, u32[]{:S(2)}) collective-permute-start(f32[12,4,8,128]{3,2,1,0:T(8,128)S(1)} %get-tuple-element.59), channel_id=1, source_target_pairs={{384,448},{320,384},{256,320},{192,256},{128,192},{64,128},{0,64},... | collective-permute-start | bytes 589832 | tf_op jit(solution)/shard_map/ppermute | solution.py:433
  40.7 3.3 %coef_planes.1 = (f32[20,4,4,8,128]{4,3,2,1,0:T(8,128)S(1)}, f32[4,4,8,128]{3,2,1,0:T(8,128)S(1)}, f32[20,4,4,8,128]{4,3,2,1,0:T(8,128)S(1)}, f32[4,4,8,128]{3,2...) custom-call(f32[4,4,8,128]{3,2,1,0:T(8,128)S(1)} %get-tuple-element.57.refs_0_.f_ref, ...), custom_call_target="tpu_custom_call" | custom-call | tf_op jit(solution)/shard_map/coef_planes/pallas_call | solution.py:421
  44.1 3.2 %collective-permute-done.1.hi_ref = f32[12,4,8,128]{3,2,1,0:T(8,128)S(1)} collective-permute-done((f32[12,4,8,128]{3,2,1,0:T(8,128)S(1)}, f32[12,4,8,128]{3,2,1,0:T(8,128)S(1)}, u32[]{:S(2)}, u32[]{:S(2)}) %collective-permute-start.1) | collective-permute-done | bytes 196640 | tf_op jit(solution)/shard_map/ppermute | solution.py:433
  47.9 2.0 %collective-permute-start.2 = (f32[3,4,8,128]{3,2,1,0:T(8,128)S(1)}, f32[3,4,8,128]{3,2,1,0:T(8,128)S(1)}, u32[]{:S(2)}, u32[]{:S(2)}) collective-permute-start(f32[3,4,8,128]{3,2,1,0:T(8,128)S(1)} %get-tuple-element.72), channel_id=1, source_target_pairs={{448,384},{384,320},{320,256},{256,192},{192,128},{128,64},{64,0},... | collective-permute-start | bytes 147464 | tf_op jit(solution)/shard_map/ppermute | solution.py:433
  49.8 3.9 %collective-permute-start.3 = (f32[3,4,8,128]{3,2,1,0:T(8,128)S(1)}, f32[3,4,8,128]{3,2,1,0:T(8,128)S(1)}, u32[]{:S(2)}, u32[]{:S(2)}) collective-permute-start(f32[3,4,8,128]{3,2,1,0:T(8,128)S(1)} %get-tuple-element.73), channel_id=1, source_target_pairs={{384,448},{320,384},{256,320},{192,256},{128,192},{64,128},{0,64},... | collective-permute-start | bytes 147464 | tf_op jit(solution)/shard_map/ppermute | solution.py:433
  53.7 1.6 %window_one.1 = (f32[4,4,8,128]{3,2,1,0:T(8,128)S(1)}, f32[4,4,8,128]{3,2,1,0:T(8,128)S(1)}, f32[10,4,4,8,128]{4,3,2,1,0:T(8,128)S(1)}, f32[4,4,8,128]{3,2,1,0:T...) custom-call(f32[4,4,8,128]{3,2,1,0:T(8,128)S(1)} %get-tuple-element.65.c_, ...), custom_call_target="tpu_custom_call" | custom-call | tf_op jit(solution)/shard_map/window_one/pallas_call | solution.py:421
  55.4 1.3 %collective-permute-done.3.refs_3_ = f32[3,4,8,128]{3,2,1,0:T(8,128)S(1)} collective-permute-done((f32[3,4,8,128]{3,2,1,0:T(8,128)S(1)}, f32[3,4,8,128]{3,2,1,0:T(8,128)S(1)}, u32[]{:S(2)}, u32[]{:S(2)}) %collective-permute-start.3) | collective-permute-done | bytes 49184 | tf_op jit(solution)/shard_map/ppermute | solution.py:433
  56.8 1.9 %collective-permute-start.4 = (f32[3,4,8,128]{3,2,1,0:T(8,128)S(1)}, f32[3,4,8,128]{3,2,1,0:T(8,128)S(1)}, u32[]{:S(2)}, u32[]{:S(2)}) collective-permute-start(f32[3,4,8,128]{3,2,1,0:T(8,128)S(1)} %get-tuple-element.83), channel_id=1, source_target_pairs={{448,384},{384,320},{320,256},{256,192},{192,128},{128,64},{64,0},... | collective-permute-start | bytes 147464 | tf_op jit(solution)/shard_map/ppermute | solution.py:433
  58.7 3.9 %collective-permute-start.5 = (f32[3,4,8,128]{3,2,1,0:T(8,128)S(1)}, f32[3,4,8,128]{3,2,1,0:T(8,128)S(1)}, u32[]{:S(2)}, u32[]{:S(2)}) collective-permute-start(f32[3,4,8,128]{3,2,1,0:T(8,128)S(1)} %get-tuple-element.84), channel_id=1, source_target_pairs={{384,448},{320,384},{256,320},{192,256},{128,192},{64,128},{0,64},... | collective-permute-start | bytes 147464 | tf_op jit(solution)/shard_map/ppermute | solution.py:433
  62.7 1.6 %window_two.1 = (f32[4,4,8,128]{3,2,1,0:T(8,128)S(1)}, f32[4,4,8,128]{3,2,1,0:T(8,128)S(1)}, f32[10,4,4,8,128]{4,3,2,1,0:T(8,128)S(1)}, f32[4,4,8,128]{3,2,1,0:T...) custom-call(f32[4,4,8,128]{3,2,1,0:T(8,128)S(1)} %get-tuple-element.76.c_, ...), custom_call_target="tpu_custom_call" | custom-call | tf_op jit(solution)/shard_map/window_two/pallas_call | solution.py:421
  64.3 1.3 %collective-permute-done.5.refs_4_ = f32[3,4,8,128]{3,2,1,0:T(8,128)S(1)} collective-permute-done((f32[3,4,8,128]{3,2,1,0:T(8,128)S(1)}, f32[3,4,8,128]{3,2,1,0:T(8,128)S(1)}, u32[]{:S(2)}, u32[]{:S(2)}) %collective-permute-start.5) | collective-permute-done | bytes 49184 | tf_op jit(solution)/shard_map/ppermute | solution.py:433
  65.7 1.9 %collective-permute-start.6 = (f32[3,4,8,128]{3,2,1,0:T(8,128)S(1)}, f32[3,4,8,128]{3,2,1,0:T(8,128)S(1)}, u32[]{:S(2)}, u32[]{:S(2)}) collective-permute-start(f32[3,4,8,128]{3,2,1,0:T(8,128)S(1)} %get-tuple-element.95), channel_id=1, source_target_pairs={{448,384},{384,320},{320,256},{256,192},{192,128},{128,64},{64,0},... | collective-permute-start | bytes 147464 | tf_op jit(solution)/shard_map/ppermute | solution.py:433
  67.7 3.9 %collective-permute-start.7 = (f32[3,4,8,128]{3,2,1,0:T(8,128)S(1)}, f32[3,4,8,128]{3,2,1,0:T(8,128)S(1)}, u32[]{:S(2)}, u32[]{:S(2)}) collective-permute-start(f32[3,4,8,128]{3,2,1,0:T(8,128)S(1)} %get-tuple-element.96), channel_id=1, source_target_pairs={{384,448},{320,384},{256,320},{192,256},{128,192},{64,128},{0,64},... | collective-permute-start | bytes 147464 | tf_op jit(solution)/shard_map/ppermute | solution.py:433
  71.6 1.1 %window_three.1 = (f32[4,4,8,128]{3,2,1,0:T(8,128)S(1)}, f32[4,4,8,128]{3,2,1,0:T(8,128)S(1)}, f32[10,4,4,8,128]{4,3,2,1,0:T(8,128)S(1)}, f32[4,4,8,128]{3,2,1,0:T(8,128)S(1)}, f32[4,4,8,128]{3,2,1,0:T(8,128)S(1)}) custom-call(f32[4,4,8,128]{3,2,1,0:T(8,128)S(1)} %get-tuple-element.87.c_ref.refs_0_.middle_ref, ...), custom_call_target="tpu_custom_call" | custom-call | tf_op jit(solution)/shard_map/window_three/pallas_call | solution.py:421
  72.7 1.8 %collective-permute-done.7.refs_3_ = f32[3,4,8,128]{3,2,1,0:T(8,128)S(1)} collective-permute-done((f32[3,4,8,128]{3,2,1,0:T(8,128)S(1)}, f32[3,4,8,128]{3,2,1,0:T(8,128)S(1)}, u32[]{:S(2)}, u32[]{:S(2)}) %collective-permute-start.7) | collective-permute-done | bytes 49184 | tf_op jit(solution)/shard_map/ppermute | solution.py:433
  74.7 2.3 %collective-permute-start.8 = (f32[3,4,8,128]{3,2,1,0:T(8,128)S(1)}, f32[3,4,8,128]{3,2,1,0:T(8,128)S(1)}, u32[]{:S(2)}, u32[]{:S(2)}) collective-permute-start(f32[3,4,8,128]{3,2,1,0:T(8,128)S(1)} %get-tuple-element.106), channel_id=1, source_target_pairs={{448,384},{384,320},{320,256},{256,192},{192,128},{128,64},{64,0},... | collective-permute-start | bytes 147464 | tf_op jit(solution)/shard_map/ppermute | solution.py:433
  77.0 3.5 %collective-permute-start.9 = (f32[3,4,8,128]{3,2,1,0:T(8,128)S(1)}, f32[3,4,8,128]{3,2,1,0:T(8,128)S(1)}, u32[]{:S(2)}, u32[]{:S(2)}) collective-permute-start(f32[3,4,8,128]{3,2,1,0:T(8,128)S(1)} %get-tuple-element.107), channel_id=1, source_target_pairs={{384,448},{320,384},{256,320},{192,256},{128,192},{64,128},{0,64},... | collective-permute-start | bytes 147464 | tf_op jit(solution)/shard_map/ppermute | solution.py:433
  80.5 0.6 window_four.1
  81.1 2.8 %collective-permute-done.9.hi_ref = f32[3,4,8,128]{3,2,1,0:T(8,128)S(1)} collective-permute-done((f32[3,4,8,128]{3,2,1,0:T(8,128)S(1)}, f32[3,4,8,128]{3,2,1,0:T(8,128)S(1)}, u32[]{:S(2)}, u32[]{:S(2)}) %collective-permute-start.9) | collective-permute-done | bytes 49184 | tf_op jit(solution)/shard_map/ppermute | solution.py:433
  83.9 21.2 %all_to_all.11.refs_1_ = f32[32,4,128]{2,1,0:T(4,128)S(1)} all-to-all(f32[32,4,128]{2,1,0:T(4,128)S(1)} %finish.1), channel_id=1, replica_groups=mesh['gx'=8,'gy'=4,'gz'=16] {'gx','gy'}, dimensions={0} | all-to-all | bytes 131072 | tf_op jit(solution)/shard_map/all_to_all | solution.py:501
  105.2 0.7 from_slabs.1
  (11 shorter events, 1.1 us)
Async XLA Ops:
  34.1 9.9 %collective-permute-start = (f32[12,4,8,128]{3,2,1,0:T(8,128)S(1)}, f32[12,4,8,128]{3,2,1,0:T(8,128)S(1)}, u32[]{:S(2)}, u32[]{:S(2)}) collective-permute-start(f32[12,4,8,128]{3,2,1,0:T(8,128)S(1)} %get-tuple-element.58), channel_id=1, source_target_pairs={{448,384},{384,320},{320,256},{256,192},{192,128},{128,64},{64,0},... | collective-permute-start | bytes 589832 | tf_op jit(solution)/shard_map/ppermute | solution.py:433
  38.8 8.5 %collective-permute-start.1 = (f32[12,4,8,128]{3,2,1,0:T(8,128)S(1)}, f32[12,4,8,128]{3,2,1,0:T(8,128)S(1)}, u32[]{:S(2)}, u32[]{:S(2)}) collective-permute-start(f32[12,4,8,128]{3,2,1,0:T(8,128)S(1)} %get-tuple-element.59), channel_id=1, source_target_pairs={{384,448},{320,384},{256,320},{192,256},{128,192},{64,128},{0,64},... | collective-permute-start | bytes 589832 | tf_op jit(solution)/shard_map/ppermute | solution.py:433
  47.9 7.5 %collective-permute-start.2 = (f32[3,4,8,128]{3,2,1,0:T(8,128)S(1)}, f32[3,4,8,128]{3,2,1,0:T(8,128)S(1)}, u32[]{:S(2)}, u32[]{:S(2)}) collective-permute-start(f32[3,4,8,128]{3,2,1,0:T(8,128)S(1)} %get-tuple-element.72), channel_id=1, source_target_pairs={{448,384},{384,320},{320,256},{256,192},{192,128},{128,64},{64,0},... | collective-permute-start | bytes 147464 | tf_op jit(solution)/shard_map/ppermute | solution.py:433
  49.8 6.9 %collective-permute-start.3 = (f32[3,4,8,128]{3,2,1,0:T(8,128)S(1)}, f32[3,4,8,128]{3,2,1,0:T(8,128)S(1)}, u32[]{:S(2)}, u32[]{:S(2)}) collective-permute-start(f32[3,4,8,128]{3,2,1,0:T(8,128)S(1)} %get-tuple-element.73), channel_id=1, source_target_pairs={{384,448},{320,384},{256,320},{192,256},{128,192},{64,128},{0,64},... | collective-permute-start | bytes 147464 | tf_op jit(solution)/shard_map/ppermute | solution.py:433
  56.8 7.5 %collective-permute-start.4 = (f32[3,4,8,128]{3,2,1,0:T(8,128)S(1)}, f32[3,4,8,128]{3,2,1,0:T(8,128)S(1)}, u32[]{:S(2)}, u32[]{:S(2)}) collective-permute-start(f32[3,4,8,128]{3,2,1,0:T(8,128)S(1)} %get-tuple-element.83), channel_id=1, source_target_pairs={{448,384},{384,320},{320,256},{256,192},{192,128},{128,64},{64,0},... | collective-permute-start | bytes 147464 | tf_op jit(solution)/shard_map/ppermute | solution.py:433
  58.7 6.9 %collective-permute-start.5 = (f32[3,4,8,128]{3,2,1,0:T(8,128)S(1)}, f32[3,4,8,128]{3,2,1,0:T(8,128)S(1)}, u32[]{:S(2)}, u32[]{:S(2)}) collective-permute-start(f32[3,4,8,128]{3,2,1,0:T(8,128)S(1)} %get-tuple-element.84), channel_id=1, source_target_pairs={{384,448},{320,384},{256,320},{192,256},{128,192},{64,128},{0,64},... | collective-permute-start | bytes 147464 | tf_op jit(solution)/shard_map/ppermute | solution.py:433
  65.7 7.0 %collective-permute-start.6 = (f32[3,4,8,128]{3,2,1,0:T(8,128)S(1)}, f32[3,4,8,128]{3,2,1,0:T(8,128)S(1)}, u32[]{:S(2)}, u32[]{:S(2)}) collective-permute-start(f32[3,4,8,128]{3,2,1,0:T(8,128)S(1)} %get-tuple-element.95), channel_id=1, source_target_pairs={{448,384},{384,320},{320,256},{256,192},{192,128},{128,64},{64,0},... | collective-permute-start | bytes 147464 | tf_op jit(solution)/shard_map/ppermute | solution.py:433
  67.7 6.9 %collective-permute-start.7 = (f32[3,4,8,128]{3,2,1,0:T(8,128)S(1)}, f32[3,4,8,128]{3,2,1,0:T(8,128)S(1)}, u32[]{:S(2)}, u32[]{:S(2)}) collective-permute-start(f32[3,4,8,128]{3,2,1,0:T(8,128)S(1)} %get-tuple-element.96), channel_id=1, source_target_pairs={{384,448},{320,384},{256,320},{192,256},{128,192},{64,128},{0,64},... | collective-permute-start | bytes 147464 | tf_op jit(solution)/shard_map/ppermute | solution.py:433
  74.7 6.5 %collective-permute-start.8 = (f32[3,4,8,128]{3,2,1,0:T(8,128)S(1)}, f32[3,4,8,128]{3,2,1,0:T(8,128)S(1)}, u32[]{:S(2)}, u32[]{:S(2)}) collective-permute-start(f32[3,4,8,128]{3,2,1,0:T(8,128)S(1)} %get-tuple-element.106), channel_id=1, source_target_pairs={{448,384},{384,320},{320,256},{256,192},{192,128},{128,64},{64,0},... | collective-permute-start | bytes 147464 | tf_op jit(solution)/shard_map/ppermute | solution.py:433
  77.0 6.9 %collective-permute-start.9 = (f32[3,4,8,128]{3,2,1,0:T(8,128)S(1)}, f32[3,4,8,128]{3,2,1,0:T(8,128)S(1)}, u32[]{:S(2)}, u32[]{:S(2)}) collective-permute-start(f32[3,4,8,128]{3,2,1,0:T(8,128)S(1)} %get-tuple-element.107), channel_id=1, source_target_pairs={{384,448},{320,384},{256,320},{192,256},{128,192},{64,128},{0,64},... | collective-permute-start | bytes 147464 | tf_op jit(solution)/shard_map/ppermute | solution.py:433

commit v9 on v7

--- a/solution.py
+++ b/solution.py
@@ -200,7 +200,7 @@
     lax.fori_loop(0, count, plane, 0, unroll=UNROLL_COEF)
 
 
-def coef_depth(section, f_ref, lo_ref, hi_ref, phi_ref, sum_ref, co_ref, scale_ref, pc_ref):
+def coef_depth(section, f_ref, lo_ref, hi_ref, phi_ref, sum_ref, co_ref, scale_ref, pc_ref, unroll=2):
     def column(g, carry):
         f = (
             [lo_ref[3 * section + i, g] for i in range(3)]
@@ -223,7 +223,7 @@
                 co_ref[n, z, g] = part
         return carry
 
-    lax.fori_loop(0, 4, column, 0, unroll=UNROLL_COEF)
+    lax.fori_loop(0, 4, column, 0, unroll=unroll)
 
 
 def apply_depth(c_ref, co_ref, scale_ref, out_ref, up_ref, dn_ref):
@@ -293,7 +293,7 @@
 
 
 def first_stage(f_ref, lo_ref, hi_ref, phi_ref, sum_ref, cot_ref, c_ref, part_ref, up_ref, dn_ref, scale_ref, pc_ref, co_ref):
-    coef_depth(0, f_ref, lo_ref, hi_ref, phi_ref, sum_ref, co_ref, scale_ref, pc_ref)
+    coef_depth(0, f_ref, lo_ref, hi_ref, phi_ref, sum_ref, co_ref, scale_ref, pc_ref, unroll=4)
     c_ref[...] = 0.5 * cot_ref[...]
     apply_depth(c_ref, co_ref, scale_ref, part_ref, up_ref, dn_ref)
 
@@ -326,13 +326,14 @@
     coef_depth(3, phi_ref, lo_ref, hi_ref, phi_ref, Halves(sum_low, sum_high, 0), *coef_refs)
 
 
-def window_four(c_ref, co_low, co_high, scale_ref, pc_ref, part_ref, acc_in, own_ref, acc_ref):
+def window_four(middle_ref, c_ref, co_low, co_high, scale_ref, pc_ref, part_ref, acc_in, own_ref, acc_ref):
     apply_planes(c_ref, Halves(co_low, co_high, 1), scale_ref, pc_ref, part_ref, acc_in, own_ref, acc_ref)
-
-
-def finish(first_ref, middle_ref, own_in, lo_ref, hi_ref, acc_in, out_ref):
-    for z, back in enumerate(joined(own_in, lo_ref, hi_ref)):
-        whole = (acc_in[z] + back) + (first_ref[z] + middle_ref[z])
+    for z in range(4):
+        own_ref[z] = own_ref[z] + (acc_ref[z] + (c_ref[z] + middle_ref[z]))
+
+
+def finish(own_in, lo_ref, hi_ref, out_ref):
+    for z, whole in enumerate(joined(own_in, lo_ref, hi_ref)):
         for gy in range(whole.shape[0]):
             for gx in range(whole.shape[1]):
                 out_ref[gx * whole.shape[0] + gy, z] = whole[gy, gx]
@@ -488,10 +489,11 @@
             c3, own, lo, hi, deep, scale, name="stage_four",
         )
         lo, hi = exchange(up, dn)
-        own, acc = call(
-            window_four, window_out, c4, flat3a, flat3b, scale, pc, part, acc, name="window_four",
-        )
-        slabs = call(finish, near(count, depth, LANES), c4, c3, own, lo, hi, acc, name="finish")
+        own = call(
+            window_four, near(*slab), c3, c4, flat3a, flat3b, scale, pc, part, acc,
+            scratch=[pltpu.VMEM(slab, F32)], name="window_four",
+        )
+        slabs = call(finish, near(count, depth, LANES), own, lo, hi, name="finish")
         slabs = lax.all_to_all(slabs, ("gx", "gy"), 0, 0)
         return call(
             lambda *refs: from_slabs(count, depth, even_at, odd_at, *refs),

time: 106 us -> 106 us (level)
  no operation moved by 1% of the time
where the time goes in v9:
time: 106 us
  blocking collectives  53.7 us (51%)
  starting transfers between devices  30 us (28%)
  Pallas kernels  11.3 us (11%)
  waiting for transfers between devices  10.4 us (10%)
    all_to_all x1, blocking collectives, shards(): packed = lax.all_to_all(packed, ('gx', 'gy'), 0, 0)  32.5 us
    all_to_all x1, blocking collectives, shards(): slabs = lax.all_to_all(slabs, ('gx', 'gy'), 0, 0)  21.2 us
    ppermute x5, starting transfers between devices, exchange(): lax.ppermute(dn, everywhere, downward)  17.1 us
    ppermute x5, starting transfers between devices, exchange(): lax.ppermute(up, everywhere, upward)  12.8 us
    pallas_call x13, Pallas kernels, call(): pl.pallas_call(kernel, out_shape=out_shape, in_specs=[first] + [vmem] * (...  11.3 us
    ppermute x5, waiting for transfers between devices, exchange(): lax.ppermute(dn, everywhere, downward)  10.4 us
  transfers between devices with their start and end apart: 10, of which 5 were waited for; matrix products, arithmetic and copies ran while one was open for 0% of the time, Pallas kernels for 8%

profile of v9, /device:TPU:6, one launch (start us, length us, event | category | flops | bytes accessed | tf_op | source)
XLA Modules:
  0.0 105.6 jit_solution(16272645482216132500)
XLA Ops:
  0.0 1.2 %to_slabs.1 = f32[32,20,128]{2,1,0:T(8,128)S(1)} custom-call(s32[1]{0:T(128)} %bitcast.refs_0_, f32[8,16,128]{2,1,0:T(8,128)} %refs_1_.1, f32[8,16,128]{2,1,0:T(8,128)} %refs_2_.1, f32[8,16,128]{2,1,0:T(8,128)} %refs_3_.1, f32[8,16,128]{2,1,0:T(8,128)} %refs_4_.1, f32[8,16,128]{2,1,0:T(8,128)} %refs_5_.1), custom_call_target="tpu_custom_call" | custom-call | tf_op jit(solution)/shard_map/to_slabs/pallas_call | solution.py:417
  1.2 32.5 %all_to_all.10.refs_0_ = f32[32,20,128]{2,1,0:T(8,128)S(1)} all-to-all(f32[32,20,128]{2,1,0:T(8,128)S(1)} %to_slabs.1), channel_id=1, replica_groups=mesh['gx'=8,'gy'=4,'gz'=16] {'gx','gy'}, dimensions={0} | all-to-all | bytes 655360 | tf_op jit(solution)/shard_map/all_to_all | solution.py:441
  33.8 4.7 %collective-permute-start = (f32[12,4,8,128]{3,2,1,0:T(8,128)S(1)}, f32[12,4,8,128]{3,2,1,0:T(8,128)S(1)}, u32[]{:S(2)}, u32[]{:S(2)}) collective-permute-start(f32[12,4,8,128]{3,2,1,0:T(8,128)S(1)} %get-tuple-element.56), channel_id=1, source_target_pairs={{448,384},{384,320},{320,256},{256,192},{192,128},{128,64},{64,0},... | collective-permute-start | bytes 589832 | tf_op jit(solution)/shard_map/ppermute | solution.py:429
  38.5 1.9 %collective-permute-start.1 = (f32[12,4,8,128]{3,2,1,0:T(8,128)S(1)}, f32[12,4,8,128]{3,2,1,0:T(8,128)S(1)}, u32[]{:S(2)}, u32[]{:S(2)}) collective-permute-start(f32[12,4,8,128]{3,2,1,0:T(8,128)S(1)} %get-tuple-element.57), channel_id=1, source_target_pairs={{384,448},{320,384},{256,320},{192,256},{128,192},{64,128},{0,64},... | collective-permute-start | bytes 589832 | tf_op jit(solution)/shard_map/ppermute | solution.py:429
  40.4 3.3 %coef_planes.1 = (f32[20,4,4,8,128]{4,3,2,1,0:T(8,128)S(1)}, f32[4,4,8,128]{3,2,1,0:T(8,128)S(1)}, f32[20,4,4,8,128]{4,3,2,1,0:T(8,128)S(1)}, f32[4,4,8,128]{3,2...) custom-call(f32[4,4,8,128]{3,2,1,0:T(8,128)S(1)} %get-tuple-element.55.refs_0_.f_ref, ...), custom_call_target="tpu_custom_call" | custom-call | tf_op jit(solution)/shard_map/coef_planes/pallas_call | solution.py:417
  43.8 3.2 %collective-permute-done.1.hi_ref = f32[12,4,8,128]{3,2,1,0:T(8,128)S(1)} collective-permute-done((f32[12,4,8,128]{3,2,1,0:T(8,128)S(1)}, f32[12,4,8,128]{3,2,1,0:T(8,128)S(1)}, u32[]{:S(2)}, u32[]{:S(2)}) %collective-permute-start.1) | collective-permute-done | bytes 196640 | tf_op jit(solution)/shard_map/ppermute | solution.py:429
  47.5 2.0 %collective-permute-start.2 = (f32[3,4,8,128]{3,2,1,0:T(8,128)S(1)}, f32[3,4,8,128]{3,2,1,0:T(8,128)S(1)}, u32[]{:S(2)}, u32[]{:S(2)}) collective-permute-start(f32[3,4,8,128]{3,2,1,0:T(8,128)S(1)} %get-tuple-element.70), channel_id=1, source_target_pairs={{448,384},{384,320},{320,256},{256,192},{192,128},{128,64},{64,0},... | collective-permute-start | bytes 147464 | tf_op jit(solution)/shard_map/ppermute | solution.py:429
  49.5 3.9 %collective-permute-start.3 = (f32[3,4,8,128]{3,2,1,0:T(8,128)S(1)}, f32[3,4,8,128]{3,2,1,0:T(8,128)S(1)}, u32[]{:S(2)}, u32[]{:S(2)}) collective-permute-start(f32[3,4,8,128]{3,2,1,0:T(8,128)S(1)} %get-tuple-element.71), channel_id=1, source_target_pairs={{384,448},{320,384},{256,320},{192,256},{128,192},{64,128},{0,64},... | collective-permute-start | bytes 147464 | tf_op jit(solution)/shard_map/ppermute | solution.py:429
  53.4 1.6 %window_one.1 = (f32[4,4,8,128]{3,2,1,0:T(8,128)S(1)}, f32[4,4,8,128]{3,2,1,0:T(8,128)S(1)}, f32[10,4,4,8,128]{4,3,2,1,0:T(8,128)S(1)}, f32[4,4,8,128]{3,2,1,0:T...) custom-call(f32[4,4,8,128]{3,2,1,0:T(8,128)S(1)} %get-tuple-element.63.c_, ...), custom_call_target="tpu_custom_call" | custom-call | tf_op jit(solution)/shard_map/window_one/pallas_call | solution.py:417
  55.1 1.3 %collective-permute-done.3.refs_3_ = f32[3,4,8,128]{3,2,1,0:T(8,128)S(1)} collective-permute-done((f32[3,4,8,128]{3,2,1,0:T(8,128)S(1)}, f32[3,4,8,128]{3,2,1,0:T(8,128)S(1)}, u32[]{:S(2)}, u32[]{:S(2)}) %collective-permute-start.3) | collective-permute-done | bytes 49184 | tf_op jit(solution)/shard_map/ppermute | solution.py:429
  56.5 1.9 %collective-permute-start.4 = (f32[3,4,8,128]{3,2,1,0:T(8,128)S(1)}, f32[3,4,8,128]{3,2,1,0:T(8,128)S(1)}, u32[]{:S(2)}, u32[]{:S(2)}) collective-permute-start(f32[3,4,8,128]{3,2,1,0:T(8,128)S(1)} %get-tuple-element.81), channel_id=1, source_target_pairs={{448,384},{384,320},{320,256},{256,192},{192,128},{128,64},{64,0},... | collective-permute-start | bytes 147464 | tf_op jit(solution)/shard_map/ppermute | solution.py:429
  58.4 3.9 %collective-permute-start.5 = (f32[3,4,8,128]{3,2,1,0:T(8,128)S(1)}, f32[3,4,8,128]{3,2,1,0:T(8,128)S(1)}, u32[]{:S(2)}, u32[]{:S(2)}) collective-permute-start(f32[3,4,8,128]{3,2,1,0:T(8,128)S(1)} %get-tuple-element.82), channel_id=1, source_target_pairs={{384,448},{320,384},{256,320},{192,256},{128,192},{64,128},{0,64},... | collective-permute-start | bytes 147464 | tf_op jit(solution)/shard_map/ppermute | solution.py:429
  62.4 1.6 %window_two.1 = (f32[4,4,8,128]{3,2,1,0:T(8,128)S(1)}, f32[4,4,8,128]{3,2,1,0:T(8,128)S(1)}, f32[10,4,4,8,128]{4,3,2,1,0:T(8,128)S(1)}, f32[4,4,8,128]{3,2,1,0:T...) custom-call(f32[4,4,8,128]{3,2,1,0:T(8,128)S(1)} %get-tuple-element.74.c_, ...), custom_call_target="tpu_custom_call" | custom-call | tf_op jit(solution)/shard_map/window_two/pallas_call | solution.py:417
  64.0 1.3 %collective-permute-done.5.refs_4_ = f32[3,4,8,128]{3,2,1,0:T(8,128)S(1)} collective-permute-done((f32[3,4,8,128]{3,2,1,0:T(8,128)S(1)}, f32[3,4,8,128]{3,2,1,0:T(8,128)S(1)}, u32[]{:S(2)}, u32[]{:S(2)}) %collective-permute-start.5) | collective-permute-done | bytes 49184 | tf_op jit(solution)/shard_map/ppermute | solution.py:429
  65.4 1.9 %collective-permute-start.6 = (f32[3,4,8,128]{3,2,1,0:T(8,128)S(1)}, f32[3,4,8,128]{3,2,1,0:T(8,128)S(1)}, u32[]{:S(2)}, u32[]{:S(2)}) collective-permute-start(f32[3,4,8,128]{3,2,1,0:T(8,128)S(1)} %get-tuple-element.93), channel_id=1, source_target_pairs={{448,384},{384,320},{320,256},{256,192},{192,128},{128,64},{64,0},... | collective-permute-start | bytes 147464 | tf_op jit(solution)/shard_map/ppermute | solution.py:429
  67.4 3.9 %collective-permute-start.7 = (f32[3,4,8,128]{3,2,1,0:T(8,128)S(1)}, f32[3,4,8,128]{3,2,1,0:T(8,128)S(1)}, u32[]{:S(2)}, u32[]{:S(2)}) collective-permute-start(f32[3,4,8,128]{3,2,1,0:T(8,128)S(1)} %get-tuple-element.94), channel_id=1, source_target_pairs={{384,448},{320,384},{256,320},{192,256},{128,192},{64,128},{0,64},... | collective-permute-start | bytes 147464 | tf_op jit(solution)/shard_map/ppermute | solution.py:429
  71.3 1.1 %window_three.1 = (f32[4,4,8,128]{3,2,1,0:T(8,128)S(1)}, f32[4,4,8,128]{3,2,1,0:T(8,128)S(1)}, f32[10,4,4,8,128]{4,3,2,1,0:T(8,128)S(1)}, f32[4,4,8,128]{3,2,1,0:T(8,128)S(1)}, f32[4,4,8,128]{3,2,1,0:T(8,128)S(1)}) custom-call(f32[4,4,8,128]{3,2,1,0:T(8,128)S(1)} %get-tuple-element.85.c_ref.refs_0_.middle_ref, ...), custom_call_target="tpu_custom_call" | custom-call | tf_op jit(solution)/shard_map/window_three/pallas_call | solution.py:417
  72.4 1.8 %collective-permute-done.7.refs_3_ = f32[3,4,8,128]{3,2,1,0:T(8,128)S(1)} collective-permute-done((f32[3,4,8,128]{3,2,1,0:T(8,128)S(1)}, f32[3,4,8,128]{3,2,1,0:T(8,128)S(1)}, u32[]{:S(2)}, u32[]{:S(2)}) %collective-permute-start.7) | collective-permute-done | bytes 49184 | tf_op jit(solution)/shard_map/ppermute | solution.py:429
  74.4 2.3 %collective-permute-start.8 = (f32[3,4,8,128]{3,2,1,0:T(8,128)S(1)}, f32[3,4,8,128]{3,2,1,0:T(8,128)S(1)}, u32[]{:S(2)}, u32[]{:S(2)}) collective-permute-start(f32[3,4,8,128]{3,2,1,0:T(8,128)S(1)} %get-tuple-element.103), channel_id=1, source_target_pairs={{448,384},{384,320},{320,256},{256,192},{192,128},{128,64},{64,0},... | collective-permute-start | bytes 147464 | tf_op jit(solution)/shard_map/ppermute | solution.py:429
  76.7 3.5 %collective-permute-start.9 = (f32[3,4,8,128]{3,2,1,0:T(8,128)S(1)}, f32[3,4,8,128]{3,2,1,0:T(8,128)S(1)}, u32[]{:S(2)}, u32[]{:S(2)}) collective-permute-start(f32[3,4,8,128]{3,2,1,0:T(8,128)S(1)} %get-tuple-element.104), channel_id=1, source_target_pairs={{384,448},{320,384},{256,320},{192,256},{128,192},{64,128},{0,64},... | collective-permute-start | bytes 147464 | tf_op jit(solution)/shard_map/ppermute | solution.py:429
  80.2 0.6 window_four.1.own_in
  80.8 2.8 %collective-permute-done.9.hi_ref = f32[3,4,8,128]{3,2,1,0:T(8,128)S(1)} collective-permute-done((f32[3,4,8,128]{3,2,1,0:T(8,128)S(1)}, f32[3,4,8,128]{3,2,1,0:T(8,128)S(1)}, u32[]{:S(2)}, u32[]{:S(2)}) %collective-permute-start.9) | collective-permute-done | bytes 49184 | tf_op jit(solution)/shard_map/ppermute | solution.py:429
  83.6 21.2 %all_to_all.11.refs_1_ = f32[32,4,128]{2,1,0:T(4,128)S(1)} all-to-all(f32[32,4,128]{2,1,0:T(4,128)S(1)} %finish.1), channel_id=1, replica_groups=mesh['gx'=8,'gy'=4,'gz'=16] {'gx','gy'}, dimensions={0} | all-to-all | bytes 131072 | tf_op jit(solution)/shard_map/all_to_all | solution.py:497
  104.9 0.7 from_slabs.1
  (11 shorter events, 1.1 us)
Async XLA Ops:
  33.8 9.9 %collective-permute-start = (f32[12,4,8,128]{3,2,1,0:T(8,128)S(1)}, f32[12,4,8,128]{3,2,1,0:T(8,128)S(1)}, u32[]{:S(2)}, u32[]{:S(2)}) collective-permute-start(f32[12,4,8,128]{3,2,1,0:T(8,128)S(1)} %get-tuple-element.56), channel_id=1, source_target_pairs={{448,384},{384,320},{320,256},{256,192},{192,128},{128,64},{64,0},... | collective-permute-start | bytes 589832 | tf_op jit(solution)/shard_map/ppermute | solution.py:429
  38.5 8.5 %collective-permute-start.1 = (f32[12,4,8,128]{3,2,1,0:T(8,128)S(1)}, f32[12,4,8,128]{3,2,1,0:T(8,128)S(1)}, u32[]{:S(2)}, u32[]{:S(2)}) collective-permute-start(f32[12,4,8,128]{3,2,1,0:T(8,128)S(1)} %get-tuple-element.57), channel_id=1, source_target_pairs={{384,448},{320,384},{256,320},{192,256},{128,192},{64,128},{0,64},... | collective-permute-start | bytes 589832 | tf_op jit(solution)/shard_map/ppermute | solution.py:429
  47.5 7.5 %collective-permute-start.2 = (f32[3,4,8,128]{3,2,1,0:T(8,128)S(1)}, f32[3,4,8,128]{3,2,1,0:T(8,128)S(1)}, u32[]{:S(2)}, u32[]{:S(2)}) collective-permute-start(f32[3,4,8,128]{3,2,1,0:T(8,128)S(1)} %get-tuple-element.70), channel_id=1, source_target_pairs={{448,384},{384,320},{320,256},{256,192},{192,128},{128,64},{64,0},... | collective-permute-start | bytes 147464 | tf_op jit(solution)/shard_map/ppermute | solution.py:429
  49.5 6.9 %collective-permute-start.3 = (f32[3,4,8,128]{3,2,1,0:T(8,128)S(1)}, f32[3,4,8,128]{3,2,1,0:T(8,128)S(1)}, u32[]{:S(2)}, u32[]{:S(2)}) collective-permute-start(f32[3,4,8,128]{3,2,1,0:T(8,128)S(1)} %get-tuple-element.71), channel_id=1, source_target_pairs={{384,448},{320,384},{256,320},{192,256},{128,192},{64,128},{0,64},... | collective-permute-start | bytes 147464 | tf_op jit(solution)/shard_map/ppermute | solution.py:429
  56.5 7.5 %collective-permute-start.4 = (f32[3,4,8,128]{3,2,1,0:T(8,128)S(1)}, f32[3,4,8,128]{3,2,1,0:T(8,128)S(1)}, u32[]{:S(2)}, u32[]{:S(2)}) collective-permute-start(f32[3,4,8,128]{3,2,1,0:T(8,128)S(1)} %get-tuple-element.81), channel_id=1, source_target_pairs={{448,384},{384,320},{320,256},{256,192},{192,128},{128,64},{64,0},... | collective-permute-start | bytes 147464 | tf_op jit(solution)/shard_map/ppermute | solution.py:429
  58.4 6.9 %collective-permute-start.5 = (f32[3,4,8,128]{3,2,1,0:T(8,128)S(1)}, f32[3,4,8,128]{3,2,1,0:T(8,128)S(1)}, u32[]{:S(2)}, u32[]{:S(2)}) collective-permute-start(f32[3,4,8,128]{3,2,1,0:T(8,128)S(1)} %get-tuple-element.82), channel_id=1, source_target_pairs={{384,448},{320,384},{256,320},{192,256},{128,192},{64,128},{0,64},... | collective-permute-start | bytes 147464 | tf_op jit(solution)/shard_map/ppermute | solution.py:429
  65.4 7.0 %collective-permute-start.6 = (f32[3,4,8,128]{3,2,1,0:T(8,128)S(1)}, f32[3,4,8,128]{3,2,1,0:T(8,128)S(1)}, u32[]{:S(2)}, u32[]{:S(2)}) collective-permute-start(f32[3,4,8,128]{3,2,1,0:T(8,128)S(1)} %get-tuple-element.93), channel_id=1, source_target_pairs={{448,384},{384,320},{320,256},{256,192},{192,128},{128,64},{64,0},... | collective-permute-start | bytes 147464 | tf_op jit(solution)/shard_map/ppermute | solution.py:429
  67.4 6.9 %collective-permute-start.7 = (f32[3,4,8,128]{3,2,1,0:T(8,128)S(1)}, f32[3,4,8,128]{3,2,1,0:T(8,128)S(1)}, u32[]{:S(2)}, u32[]{:S(2)}) collective-permute-start(f32[3,4,8,128]{3,2,1,0:T(8,128)S(1)} %get-tuple-element.94), channel_id=1, source_target_pairs={{384,448},{320,384},{256,320},{192,256},{128,192},{64,128},{0,64},... | collective-permute-start | bytes 147464 | tf_op jit(solution)/shard_map/ppermute | solution.py:429
  74.4 6.5 %collective-permute-start.8 = (f32[3,4,8,128]{3,2,1,0:T(8,128)S(1)}, f32[3,4,8,128]{3,2,1,0:T(8,128)S(1)}, u32[]{:S(2)}, u32[]{:S(2)}) collective-permute-start(f32[3,4,8,128]{3,2,1,0:T(8,128)S(1)} %get-tuple-element.103), channel_id=1, source_target_pairs={{448,384},{384,320},{320,256},{256,192},{192,128},{128,64},{64,0},... | collective-permute-start | bytes 147464 | tf_op jit(solution)/shard_map/ppermute | solution.py:429
  76.7 6.9 %collective-permute-start.9 = (f32[3,4,8,128]{3,2,1,0:T(8,128)S(1)}, f32[3,4,8,128]{3,2,1,0:T(8,128)S(1)}, u32[]{:S(2)}, u32[]{:S(2)}) collective-permute-start(f32[3,4,8,128]{3,2,1,0:T(8,128)S(1)} %get-tuple-element.104), channel_id=1, source_target_pairs={{384,448},{320,384},{256,320},{192,256},{128,192},{64,128},{0,64},... | collective-permute-start | bytes 147464 | tf_op jit(solution)/shard_map/ppermute | solution.py:429

commit v10 on v9

--- a/solution.py
+++ b/solution.py
@@ -10,7 +10,7 @@
 SMOOTH_EPS = 0.01
 UNROLL_COEF = 2
 EVEN_TURNS, ODD_TURNS, FIRST_GX = (-1, 1, -1, 1), (1, 1, -1, -1), 7
-UNROLL_DEPTH = 2
+UNROLL_DEPTH = 4
 LANES = 128
 BX, BY = 8, 16
 F32 = jnp.float32

time: 106 us -> 106 us (level)
  no operation moved by 1% of the time
where the time goes in v10:
time: 106 us
  blocking collectives  53.7 us (51%)
  starting transfers between devices  30 us (28%)
  Pallas kernels  11.2 us (11%)
  waiting for transfers between devices  10.4 us (10%)
    all_to_all x1, blocking collectives, shards(): packed = lax.all_to_all(packed, ('gx', 'gy'), 0, 0)  32.5 us
    all_to_all x1, blocking collectives, shards(): slabs = lax.all_to_all(slabs, ('gx', 'gy'), 0, 0)  21.3 us
    ppermute x5, starting transfers between devices, exchange(): lax.ppermute(dn, everywhere, downward)  17.1 us
    ppermute x5, starting transfers between devices, exchange(): lax.ppermute(up, everywhere, upward)  12.8 us
    pallas_call x13, Pallas kernels, call(): pl.pallas_call(kernel, out_shape=out_shape, in_specs=[first] + [vmem] * (...  11.2 us
    ppermute x5, waiting for transfers between devices, exchange(): lax.ppermute(dn, everywhere, downward)  10.4 us
  transfers between devices with their start and end apart: 10, of which 5 were waited for; matrix products, arithmetic and copies ran while one was open for 0% of the time, Pallas kernels for 8%

profile of v10, /device:TPU:6, one launch (start us, length us, event | category | flops | bytes accessed | tf_op | source)
XLA Modules:
  0.0 105.5 jit_solution(13241061359224254965)
XLA Ops:
  0.0 1.2 %to_slabs.1 = f32[32,20,128]{2,1,0:T(8,128)S(1)} custom-call(s32[1]{0:T(128)} %bitcast.refs_0_, f32[8,16,128]{2,1,0:T(8,128)} %refs_1_.1, f32[8,16,128]{2,1,0:T(8,128)} %refs_2_.1, f32[8,16,128]{2,1,0:T(8,128)} %refs_3_.1, f32[8,16,128]{2,1,0:T(8,128)} %refs_4_.1, f32[8,16,128]{2,1,0:T(8,128)} %refs_5_.1), custom_call_target="tpu_custom_call" | custom-call | tf_op jit(solution)/shard_map/to_slabs/pallas_call | solution.py:417
  1.2 32.5 %all_to_all.10.refs_0_ = f32[32,20,128]{2,1,0:T(8,128)S(1)} all-to-all(f32[32,20,128]{2,1,0:T(8,128)S(1)} %to_slabs.1), channel_id=1, replica_groups=mesh['gx'=8,'gy'=4,'gz'=16] {'gx','gy'}, dimensions={0} | all-to-all | bytes 655360 | tf_op jit(solution)/shard_map/all_to_all | solution.py:441
  33.8 4.7 %collective-permute-start = (f32[12,4,8,128]{3,2,1,0:T(8,128)S(1)}, f32[12,4,8,128]{3,2,1,0:T(8,128)S(1)}, u32[]{:S(2)}, u32[]{:S(2)}) collective-permute-start(f32[12,4,8,128]{3,2,1,0:T(8,128)S(1)} %get-tuple-element.56), channel_id=1, source_target_pairs={{448,384},{384,320},{320,256},{256,192},{192,128},{128,64},{64,0},... | collective-permute-start | bytes 589832 | tf_op jit(solution)/shard_map/ppermute | solution.py:429
  38.5 1.9 %collective-permute-start.1 = (f32[12,4,8,128]{3,2,1,0:T(8,128)S(1)}, f32[12,4,8,128]{3,2,1,0:T(8,128)S(1)}, u32[]{:S(2)}, u32[]{:S(2)}) collective-permute-start(f32[12,4,8,128]{3,2,1,0:T(8,128)S(1)} %get-tuple-element.57), channel_id=1, source_target_pairs={{384,448},{320,384},{256,320},{192,256},{128,192},{64,128},{0,64},... | collective-permute-start | bytes 589832 | tf_op jit(solution)/shard_map/ppermute | solution.py:429
  40.4 3.3 %coef_planes.1 = (f32[20,4,4,8,128]{4,3,2,1,0:T(8,128)S(1)}, f32[4,4,8,128]{3,2,1,0:T(8,128)S(1)}, f32[20,4,4,8,128]{4,3,2,1,0:T(8,128)S(1)}, f32[4,4,8,128]{3,2...) custom-call(f32[4,4,8,128]{3,2,1,0:T(8,128)S(1)} %get-tuple-element.55.refs_0_.f_ref, ...), custom_call_target="tpu_custom_call" | custom-call | tf_op jit(solution)/shard_map/coef_planes/pallas_call | solution.py:417
  43.8 3.2 %collective-permute-done.1.hi_ref = f32[12,4,8,128]{3,2,1,0:T(8,128)S(1)} collective-permute-done((f32[12,4,8,128]{3,2,1,0:T(8,128)S(1)}, f32[12,4,8,128]{3,2,1,0:T(8,128)S(1)}, u32[]{:S(2)}, u32[]{:S(2)}) %collective-permute-start.1) | collective-permute-done | bytes 196640 | tf_op jit(solution)/shard_map/ppermute | solution.py:429
  47.5 2.0 %collective-permute-start.2 = (f32[3,4,8,128]{3,2,1,0:T(8,128)S(1)}, f32[3,4,8,128]{3,2,1,0:T(8,128)S(1)}, u32[]{:S(2)}, u32[]{:S(2)}) collective-permute-start(f32[3,4,8,128]{3,2,1,0:T(8,128)S(1)} %get-tuple-element.70), channel_id=1, source_target_pairs={{448,384},{384,320},{320,256},{256,192},{192,128},{128,64},{64,0},... | collective-permute-start | bytes 147464 | tf_op jit(solution)/shard_map/ppermute | solution.py:429
  49.5 3.9 %collective-permute-start.3 = (f32[3,4,8,128]{3,2,1,0:T(8,128)S(1)}, f32[3,4,8,128]{3,2,1,0:T(8,128)S(1)}, u32[]{:S(2)}, u32[]{:S(2)}) collective-permute-start(f32[3,4,8,128]{3,2,1,0:T(8,128)S(1)} %get-tuple-element.71), channel_id=1, source_target_pairs={{384,448},{320,384},{256,320},{192,256},{128,192},{64,128},{0,64},... | collective-permute-start | bytes 147464 | tf_op jit(solution)/shard_map/ppermute | solution.py:429
  53.4 1.6 %window_one.1 = (f32[4,4,8,128]{3,2,1,0:T(8,128)S(1)}, f32[4,4,8,128]{3,2,1,0:T(8,128)S(1)}, f32[10,4,4,8,128]{4,3,2,1,0:T(8,128)S(1)}, f32[4,4,8,128]{3,2,1,0:T...) custom-call(f32[4,4,8,128]{3,2,1,0:T(8,128)S(1)} %get-tuple-element.63.c_, ...), custom_call_target="tpu_custom_call" | custom-call | tf_op jit(solution)/shard_map/window_one/pallas_call | solution.py:417
  55.0 1.3 %collective-permute-done.3.refs_3_ = f32[3,4,8,128]{3,2,1,0:T(8,128)S(1)} collective-permute-done((f32[3,4,8,128]{3,2,1,0:T(8,128)S(1)}, f32[3,4,8,128]{3,2,1,0:T(8,128)S(1)}, u32[]{:S(2)}, u32[]{:S(2)}) %collective-permute-start.3) | collective-permute-done | bytes 49184 | tf_op jit(solution)/shard_map/ppermute | solution.py:429
  56.4 1.9 %collective-permute-start.4 = (f32[3,4,8,128]{3,2,1,0:T(8,128)S(1)}, f32[3,4,8,128]{3,2,1,0:T(8,128)S(1)}, u32[]{:S(2)}, u32[]{:S(2)}) collective-permute-start(f32[3,4,8,128]{3,2,1,0:T(8,128)S(1)} %get-tuple-element.81), channel_id=1, source_target_pairs={{448,384},{384,320},{320,256},{256,192},{192,128},{128,64},{64,0},... | collective-permute-start | bytes 147464 | tf_op jit(solution)/shard_map/ppermute | solution.py:429
  58.4 3.9 %collective-permute-start.5 = (f32[3,4,8,128]{3,2,1,0:T(8,128)S(1)}, f32[3,4,8,128]{3,2,1,0:T(8,128)S(1)}, u32[]{:S(2)}, u32[]{:S(2)}) collective-permute-start(f32[3,4,8,128]{3,2,1,0:T(8,128)S(1)} %get-tuple-element.82), channel_id=1, source_target_pairs={{384,448},{320,384},{256,320},{192,256},{128,192},{64,128},{0,64},... | collective-permute-start | bytes 147464 | tf_op jit(solution)/shard_map/ppermute | solution.py:429
  62.3 1.6 %window_two.1 = (f32[4,4,8,128]{3,2,1,0:T(8,128)S(1)}, f32[4,4,8,128]{3,2,1,0:T(8,128)S(1)}, f32[10,4,4,8,128]{4,3,2,1,0:T(8,128)S(1)}, f32[4,4,8,128]{3,2,1,0:T...) custom-call(f32[4,4,8,128]{3,2,1,0:T(8,128)S(1)} %get-tuple-element.74.c_, ...), custom_call_target="tpu_custom_call" | custom-call | tf_op jit(solution)/shard_map/window_two/pallas_call | solution.py:417
  64.0 1.3 %collective-permute-done.5.refs_4_ = f32[3,4,8,128]{3,2,1,0:T(8,128)S(1)} collective-permute-done((f32[3,4,8,128]{3,2,1,0:T(8,128)S(1)}, f32[3,4,8,128]{3,2,1,0:T(8,128)S(1)}, u32[]{:S(2)}, u32[]{:S(2)}) %collective-permute-start.5) | collective-permute-done | bytes 49184 | tf_op jit(solution)/shard_map/ppermute | solution.py:429
  65.3 1.9 %collective-permute-start.6 = (f32[3,4,8,128]{3,2,1,0:T(8,128)S(1)}, f32[3,4,8,128]{3,2,1,0:T(8,128)S(1)}, u32[]{:S(2)}, u32[]{:S(2)}) collective-permute-start(f32[3,4,8,128]{3,2,1,0:T(8,128)S(1)} %get-tuple-element.93), channel_id=1, source_target_pairs={{448,384},{384,320},{320,256},{256,192},{192,128},{128,64},{64,0},... | collective-permute-start | bytes 147464 | tf_op jit(solution)/shard_map/ppermute | solution.py:429
  67.3 3.9 %collective-permute-start.7 = (f32[3,4,8,128]{3,2,1,0:T(8,128)S(1)}, f32[3,4,8,128]{3,2,1,0:T(8,128)S(1)}, u32[]{:S(2)}, u32[]{:S(2)}) collective-permute-start(f32[3,4,8,128]{3,2,1,0:T(8,128)S(1)} %get-tuple-element.94), channel_id=1, source_target_pairs={{384,448},{320,384},{256,320},{192,256},{128,192},{64,128},{0,64},... | collective-permute-start | bytes 147464 | tf_op jit(solution)/shard_map/ppermute | solution.py:429
  71.2 1.1 %window_three.1 = (f32[4,4,8,128]{3,2,1,0:T(8,128)S(1)}, f32[4,4,8,128]{3,2,1,0:T(8,128)S(1)}, f32[10,4,4,8,128]{4,3,2,1,0:T(8,128)S(1)}, f32[4,4,8,128]{3,2,1,0:T(8,128)S(1)}, f32[4,4,8,128]{3,2,1,0:T(8,128)S(1)}) custom-call(f32[4,4,8,128]{3,2,1,0:T(8,128)S(1)} %get-tuple-element.85.c_ref.refs_0_.middle_ref, ...), custom_call_target="tpu_custom_call" | custom-call | tf_op jit(solution)/shard_map/window_three/pallas_call | solution.py:417
  72.3 1.8 %collective-permute-done.7.refs_3_ = f32[3,4,8,128]{3,2,1,0:T(8,128)S(1)} collective-permute-done((f32[3,4,8,128]{3,2,1,0:T(8,128)S(1)}, f32[3,4,8,128]{3,2,1,0:T(8,128)S(1)}, u32[]{:S(2)}, u32[]{:S(2)}) %collective-permute-start.7) | collective-permute-done | bytes 49184 | tf_op jit(solution)/shard_map/ppermute | solution.py:429
  74.2 2.3 %collective-permute-start.8 = (f32[3,4,8,128]{3,2,1,0:T(8,128)S(1)}, f32[3,4,8,128]{3,2,1,0:T(8,128)S(1)}, u32[]{:S(2)}, u32[]{:S(2)}) collective-permute-start(f32[3,4,8,128]{3,2,1,0:T(8,128)S(1)} %get-tuple-element.103), channel_id=1, source_target_pairs={{448,384},{384,320},{320,256},{256,192},{192,128},{128,64},{64,0},... | collective-permute-start | bytes 147464 | tf_op jit(solution)/shard_map/ppermute | solution.py:429
  76.6 3.5 %collective-permute-start.9 = (f32[3,4,8,128]{3,2,1,0:T(8,128)S(1)}, f32[3,4,8,128]{3,2,1,0:T(8,128)S(1)}, u32[]{:S(2)}, u32[]{:S(2)}) collective-permute-start(f32[3,4,8,128]{3,2,1,0:T(8,128)S(1)} %get-tuple-element.104), channel_id=1, source_target_pairs={{384,448},{320,384},{256,320},{192,256},{128,192},{64,128},{0,64},... | collective-permute-start | bytes 147464 | tf_op jit(solution)/shard_map/ppermute | solution.py:429
  80.1 0.6 window_four.1.own_in
  80.7 2.8 %collective-permute-done.9.hi_ref = f32[3,4,8,128]{3,2,1,0:T(8,128)S(1)} collective-permute-done((f32[3,4,8,128]{3,2,1,0:T(8,128)S(1)}, f32[3,4,8,128]{3,2,1,0:T(8,128)S(1)}, u32[]{:S(2)}, u32[]{:S(2)}) %collective-permute-start.9) | collective-permute-done | bytes 49184 | tf_op jit(solution)/shard_map/ppermute | solution.py:429
  83.5 21.3 %all_to_all.11.refs_1_ = f32[32,4,128]{2,1,0:T(4,128)S(1)} all-to-all(f32[32,4,128]{2,1,0:T(4,128)S(1)} %finish.1), channel_id=1, replica_groups=mesh['gx'=8,'gy'=4,'gz'=16] {'gx','gy'}, dimensions={0} | all-to-all | bytes 131072 | tf_op jit(solution)/shard_map/all_to_all | solution.py:497
  104.8 0.7 from_slabs.1
  (11 shorter events, 1.0 us)
Async XLA Ops:
  33.8 9.9 %collective-permute-start = (f32[12,4,8,128]{3,2,1,0:T(8,128)S(1)}, f32[12,4,8,128]{3,2,1,0:T(8,128)S(1)}, u32[]{:S(2)}, u32[]{:S(2)}) collective-permute-start(f32[12,4,8,128]{3,2,1,0:T(8,128)S(1)} %get-tuple-element.56), channel_id=1, source_target_pairs={{448,384},{384,320},{320,256},{256,192},{192,128},{128,64},{64,0},... | collective-permute-start | bytes 589832 | tf_op jit(solution)/shard_map/ppermute | solution.py:429
  38.5 8.5 %collective-permute-start.1 = (f32[12,4,8,128]{3,2,1,0:T(8,128)S(1)}, f32[12,4,8,128]{3,2,1,0:T(8,128)S(1)}, u32[]{:S(2)}, u32[]{:S(2)}) collective-permute-start(f32[12,4,8,128]{3,2,1,0:T(8,128)S(1)} %get-tuple-element.57), channel_id=1, source_target_pairs={{384,448},{320,384},{256,320},{192,256},{128,192},{64,128},{0,64},... | collective-permute-start | bytes 589832 | tf_op jit(solution)/shard_map/ppermute | solution.py:429
  47.5 7.5 %collective-permute-start.2 = (f32[3,4,8,128]{3,2,1,0:T(8,128)S(1)}, f32[3,4,8,128]{3,2,1,0:T(8,128)S(1)}, u32[]{:S(2)}, u32[]{:S(2)}) collective-permute-start(f32[3,4,8,128]{3,2,1,0:T(8,128)S(1)} %get-tuple-element.70), channel_id=1, source_target_pairs={{448,384},{384,320},{320,256},{256,192},{192,128},{128,64},{64,0},... | collective-permute-start | bytes 147464 | tf_op jit(solution)/shard_map/ppermute | solution.py:429
  49.5 6.9 %collective-permute-start.3 = (f32[3,4,8,128]{3,2,1,0:T(8,128)S(1)}, f32[3,4,8,128]{3,2,1,0:T(8,128)S(1)}, u32[]{:S(2)}, u32[]{:S(2)}) collective-permute-start(f32[3,4,8,128]{3,2,1,0:T(8,128)S(1)} %get-tuple-element.71), channel_id=1, source_target_pairs={{384,448},{320,384},{256,320},{192,256},{128,192},{64,128},{0,64},... | collective-permute-start | bytes 147464 | tf_op jit(solution)/shard_map/ppermute | solution.py:429
  56.4 7.5 %collective-permute-start.4 = (f32[3,4,8,128]{3,2,1,0:T(8,128)S(1)}, f32[3,4,8,128]{3,2,1,0:T(8,128)S(1)}, u32[]{:S(2)}, u32[]{:S(2)}) collective-permute-start(f32[3,4,8,128]{3,2,1,0:T(8,128)S(1)} %get-tuple-element.81), channel_id=1, source_target_pairs={{448,384},{384,320},{320,256},{256,192},{192,128},{128,64},{64,0},... | collective-permute-start | bytes 147464 | tf_op jit(solution)/shard_map/ppermute | solution.py:429
  58.4 6.9 %collective-permute-start.5 = (f32[3,4,8,128]{3,2,1,0:T(8,128)S(1)}, f32[3,4,8,128]{3,2,1,0:T(8,128)S(1)}, u32[]{:S(2)}, u32[]{:S(2)}) collective-permute-start(f32[3,4,8,128]{3,2,1,0:T(8,128)S(1)} %get-tuple-element.82), channel_id=1, source_target_pairs={{384,448},{320,384},{256,320},{192,256},{128,192},{64,128},{0,64},... | collective-permute-start | bytes 147464 | tf_op jit(solution)/shard_map/ppermute | solution.py:429
  65.3 7.0 %collective-permute-start.6 = (f32[3,4,8,128]{3,2,1,0:T(8,128)S(1)}, f32[3,4,8,128]{3,2,1,0:T(8,128)S(1)}, u32[]{:S(2)}, u32[]{:S(2)}) collective-permute-start(f32[3,4,8,128]{3,2,1,0:T(8,128)S(1)} %get-tuple-element.93), channel_id=1, source_target_pairs={{448,384},{384,320},{320,256},{256,192},{192,128},{128,64},{64,0},... | collective-permute-start | bytes 147464 | tf_op jit(solution)/shard_map/ppermute | solution.py:429
  67.3 6.9 %collective-permute-start.7 = (f32[3,4,8,128]{3,2,1,0:T(8,128)S(1)}, f32[3,4,8,128]{3,2,1,0:T(8,128)S(1)}, u32[]{:S(2)}, u32[]{:S(2)}) collective-permute-start(f32[3,4,8,128]{3,2,1,0:T(8,128)S(1)} %get-tuple-element.94), channel_id=1, source_target_pairs={{384,448},{320,384},{256,320},{192,256},{128,192},{64,128},{0,64},... | collective-permute-start | bytes 147464 | tf_op jit(solution)/shard_map/ppermute | solution.py:429
  74.2 6.5 %collective-permute-start.8 = (f32[3,4,8,128]{3,2,1,0:T(8,128)S(1)}, f32[3,4,8,128]{3,2,1,0:T(8,128)S(1)}, u32[]{:S(2)}, u32[]{:S(2)}) collective-permute-start(f32[3,4,8,128]{3,2,1,0:T(8,128)S(1)} %get-tuple-element.103), channel_id=1, source_target_pairs={{448,384},{384,320},{320,256},{256,192},{192,128},{128,64},{64,0},... | collective-permute-start | bytes 147464 | tf_op jit(solution)/shard_map/ppermute | solution.py:429
  76.6 6.9 %collective-permute-start.9 = (f32[3,4,8,128]{3,2,1,0:T(8,128)S(1)}, f32[3,4,8,128]{3,2,1,0:T(8,128)S(1)}, u32[]{:S(2)}, u32[]{:S(2)}) collective-permute-start(f32[3,4,8,128]{3,2,1,0:T(8,128)S(1)} %get-tuple-element.104), channel_id=1, source_target_pairs={{384,448},{320,384},{256,320},{192,256},{128,192},{64,128},{0,64},... | collective-permute-start | bytes 147464 | tf_op jit(solution)/shard_map/ppermute | solution.py:429
